TPU v7x, 32 devices: a whole 2x2x4 slice. The times are simulated.
32 devices in a mesh: src: 4 (over z), delay: 8 (over y, x, core).
Axes of the slice: x: 2, y: 2, z: 4, core: 2. Of those that a mesh axis runs over, the one named last changes fastest.
Arguments:
- history: float32 [32, 16, 16, 128], P('delay', 'src'), may hold values from -6 to 6
- slot_map: int32 [32], P('delay'), may hold values from 0 to 3, as said below
- interaction: float32 [1536, 128, 128], P(('src', 'delay')), may hold values from -0.0546875 to 0.0546875
- pattern: int32 [3, 1536], P(None, ('src', 'delay')), may hold values from 0 to 15, as said below
- live: int32 [32], P(('src', 'delay')), may hold values from 12 to 48
- near_inverse: float32 [16, 128, 128], P('src'), may hold values from -0.5 to 0.5
- incident: float32 [4, 16, 16, 128], P(None, 'src'), may hold values from -6 to 6
Outputs:
- currents: float32 [4, 16, 16, 128], P(None, 'src')
Inputs may be any that keep to these rules, and one draw needn't show every extreme that they name: `slot_map`: each band's 4 entries are a cyclic rotation of 0 .. 3. `pattern`: row 0 lies in 0 .. 3, row 1 in 0 .. 15, row 2 in 0 .. 3.
All inputs are finite; a program needn't handle non-finite values.
Results may differ from a plain program's by a relative error of at most 0.0003.
Values sent between devices are 32-bit elements; how exact they have to be, the bound alone decides.
No kernel may reach another device: no remote copies, remote signals or barrier semaphores. Data moves between devices by JAX's collectives and lax.ppermute only.
A program may use at most 64 MiB of HBM per device.

v0:
```python
import jax
import jax.numpy as jnp
from jax import lax
from jax.sharding import PartitionSpec as P


def shifted(x, axis, by):
    devices = lax.axis_size(axis)
    pairs = [(i, i + by) for i in range(devices) if 0 <= i + by < devices]
    return lax.ppermute(x, axis, pairs)


def slot_holding(slot_map, wanted, moment):
    length = slot_map.shape[0]
    positions = jnp.arange(length, dtype=jnp.int32)
    return jnp.sum(jnp.where((slot_map + moment) % length == wanted, positions, 0))


def body(history, slot_map, interaction, pattern, live, near_inverse, incident):
    slot_count = history.shape[0]
    group_blocks = history.shape[1]
    columns = history.shape[2]
    block_width = history.shape[3]
    moments = incident.shape[0]
    pair_count = interaction.shape[0]
    positions = jnp.arange(slot_count, dtype=jnp.int32)
    at_front = lax.axis_index("delay") == 0
    in_use = (jnp.arange(pair_count, dtype=jnp.int32) < live[0]).astype(jnp.float32)
    row_match = pattern[0][None, :] == jnp.arange(group_blocks, dtype=jnp.int32)[:, None]
    selector = row_match.astype(jnp.float32) * in_use[None, :]
    band_state = lax.all_gather(history, "src", axis=1, tiled=True)
    results = []
    newest = None
    for moment in range(moments):
        if moment > 0:
            vacated = slot_holding(slot_map, slot_count - 1, moment - 1)
            outgoing_slot = lax.dynamic_index_in_dim(band_state, vacated, 0, keepdims=False)
            incoming = shifted(outgoing_slot, "delay", 1)
            entering = jnp.where(at_front, newest, incoming)
            band_state = lax.dynamic_update_index_in_dim(band_state, entering, vacated, 0)
        holder_match = (slot_map[None, :] + moment) % slot_count == pattern[2][:, None]
        holder = jnp.sum(jnp.where(holder_match, positions[None, :], 0), axis=1)
        picked = band_state[holder, pattern[1]]
        products = jnp.einsum("pab,prb->pra", interaction, picked, precision=lax.Precision.HIGHEST)
        partial_field = jnp.dot(
            selector,
            products.reshape(pair_count, columns * block_width),
            precision=lax.Precision.HIGHEST,
        )
        partial_field = partial_field.reshape(group_blocks, columns, block_width)
        field_sum = lax.psum(partial_field, "delay")
        current = jnp.einsum(
            "iab,irb->ira",
            near_inverse,
            incident[moment] - field_sum,
            precision=lax.Precision.HIGHEST,
        )
        results.append(current)
        if moment + 1 < moments:
            newest = lax.all_gather(current, "src", axis=0, tiled=True)
    return jnp.stack(results)


def solution(mesh):
    return jax.shard_map(
        body,
        mesh=mesh,
        in_specs=(
            P("delay", "src", None, None),
            P("delay"),
            P(("src", "delay"), None, None),
            P(None, ("src", "delay")),
            P(("src", "delay")),
            P("src", None, None),
            P(None, "src", None, None),
        ),
        out_specs=P(None, "src", None, None),
        check_vma=False,
    )
```

profile of v0, /device:TPU:0, one launch (start us, length us, event | category | flops | bytes accessed | tf_op | source)
XLA Modules:
  0.0 215.6 jit_solution(3523601571943106550)
XLA Ops:
  0.0 0.0 copy-start
  0.0 1.5 fusion.45
  1.5 19.5 %all_gather.12 = f32[4,16,16,128]{3,2,1,0:T(8,128)} all-gather(f32[4,4,16,128]{3,2,1,0:T(8,128)} %param.7), channel_id=1, replica_groups=mesh['src'=4,'delay'=8] {'src'}, dimensions={1}, use_global_device_ids=true | all-gather | bytes 655360 | tf_op jit(solution)/shard_map/all_gather | solution.py:31
  23.0 1.6 dynamic-slice_bitcast_fusion.2
  24.5 1.9 collective-permute-start
  26.5 0.8 slice_bitcast_fusion.1
  27.2 0.1 select_reduce_fusion
  27.3 0.7 fusion.64
  28.0 2.6 %gather_fusion = f32[48,16,128]{2,1,0:T(8,128)} fusion(f32[4,16,16,128]{3,2,1,0:T(8,128)} %all_gather.12, s32[48]{0:T(128)S(1)} %get-tuple-element.25), kind=kCustom, calls=%fused_computation | custom fusion | bytes 786816 | tf_op jit(solution)/shard_map/gather | solution.py:43
  31.3 0.0 copy-done
  31.4 0.0 copy-start.2
  31.4 6.0 %fusion.74 = f32[48,16,128]{2,1,0:T(8,128)S(1)} fusion(f32[48,16,128]{2,1,0:T(8,128)} %gather_fusion, f32[48,128,128]{2,1,0:T(8,128)S(1)} %copy-done), kind=kOutput, calls=%fused_computation.121 | convolution fusion | flops 150994944 | bytes 3932160 | tf_op jit(solution)/shard_map/pab,prb->pra/dot_general | solution.py:44
  37.3 0.0 copy-done.2
  37.3 0.4 fusion.9
  37.8 23.8 %psum.28 = f32[4,16,128]{2,0,1:T(4,128)S(1)} all-reduce(f32[4,16,128]{2,0,1:T(4,128)S(1)} %fusion.9), channel_id=1, replica_groups=mesh['src'=4,'delay'=8] {'delay'}, use_global_device_ids=true, to_apply=%region_1.2 | all-reduce | flops 8192 | bytes 65536 | tf_op jit(solution)/shard_map/psum | solution.py:51
  61.5 1.4 fusion.73
  62.9 0.0 copy-done.1
  63.0 0.5 fusion.21
  67.1 13.4 %all_gather.13 = f32[16,16,128]{2,1,0:T(8,128)S(1)} all-gather(f32[4,16,128]{2,1,0:T(8,128)S(1)} %fusion.21), channel_id=1, replica_groups=mesh['src'=4,'delay'=8] {'src'}, dimensions={0}, use_global_device_ids=true | all-gather | bytes 163840 | tf_op jit(solution)/shard_map/all_gather | solution.py:60
  80.5 0.0 collective-permute-done
  80.5 0.7 bitcast_dynamic-update-slice_fusion.2
  81.1 2.6 %gather_fusion.1 = f32[48,16,128]{2,1,0:T(8,128)} fusion(f32[4,16,16,128]{3,2,1,0:T(8,128)} %bitcast_dynamic-update-slice_fusion.2, s32[48]{0:T(128)S(1)} %get-tuple-element.24), kind=kCustom, calls=%fused_computation.1 | custom fusion | bytes 786816 | tf_op jit(solution)/shard_map/gather | solution.py:43
  83.8 6.0 %fusion.75 = f32[48,16,128]{2,1,0:T(8,128)S(1)} fusion(f32[48,16,128]{2,1,0:T(8,128)} %gather_fusion.1, f32[48,128,128]{2,1,0:T(8,128)S(1)} %copy-done), kind=kOutput, calls=%fused_computation.122 | convolution fusion | flops 150994944 | bytes 3932160 | tf_op jit(solution)/shard_map/pab,prb->pra/dot_general | solution.py:44
  89.7 1.0 fusion.6
  90.8 22.9 %psum.29 = f32[4,16,128]{2,0,1:T(4,128)S(1)} all-reduce(f32[4,16,128]{2,0,1:T(4,128)} %fusion.6), channel_id=1, replica_groups=mesh['src'=4,'delay'=8] {'delay'}, use_global_device_ids=true, to_apply=%region_4.5 | all-reduce | flops 8192 | bytes 65536 | tf_op jit(solution)/shard_map/psum | solution.py:51
  113.7 0.9 dynamic-slice_bitcast_fusion.1
  114.6 1.3 collective-permute-start.1
  115.9 0.5 fusion.19
  116.4 13.7 %all_gather.14 = f32[16,16,128]{2,1,0:T(8,128)S(1)} all-gather(f32[4,16,128]{2,1,0:T(8,128)S(1)} %fusion.19), channel_id=1, replica_groups=mesh['src'=4,'delay'=8] {'src'}, dimensions={0}, use_global_device_ids=true | all-gather | bytes 163840 | tf_op jit(solution)/shard_map/all_gather | solution.py:60
  130.1 0.0 collective-permute-done.1
  130.1 0.7 bitcast_dynamic-update-slice_fusion.1
  130.8 2.6 %gather_fusion.2 = f32[48,16,128]{2,1,0:T(8,128)} fusion(f32[4,16,16,128]{3,2,1,0:T(8,128)} %bitcast_dynamic-update-slice_fusion.1, s32[48]{0:T(128)S(1)} %get-tuple-element.23), kind=kCustom, calls=%fused_computation.2 | custom fusion | bytes 786816 | tf_op jit(solution)/shard_map/gather | solution.py:43
  133.4 6.0 %fusion.76 = f32[48,16,128]{2,1,0:T(8,128)S(1)} fusion(f32[48,16,128]{2,1,0:T(8,128)} %gather_fusion.2, f32[48,128,128]{2,1,0:T(8,128)S(1)} %copy-done), kind=kOutput, calls=%fused_computation.123 | convolution fusion | flops 150994944 | bytes 3932160 | tf_op jit(solution)/shard_map/pab,prb->pra/dot_general | solution.py:44
  139.4 1.0 fusion.3
  140.4 23.0 %psum.30 = f32[4,16,128]{2,0,1:T(4,128)S(1)} all-reduce(f32[4,16,128]{2,0,1:T(4,128)} %fusion.3), channel_id=1, replica_groups=mesh['src'=4,'delay'=8] {'delay'}, use_global_device_ids=true, to_apply=%region_7.8 | all-reduce | flops 8192 | bytes 65536 | tf_op jit(solution)/shard_map/psum | solution.py:51
  163.4 0.9 dynamic-slice_bitcast_fusion
  164.3 1.4 collective-permute-start.2
  165.7 0.5 fusion.17
  166.2 13.5 %all_gather.15 = f32[16,16,128]{2,1,0:T(8,128)S(1)} all-gather(f32[4,16,128]{2,1,0:T(8,128)S(1)} %fusion.17), channel_id=1, replica_groups=mesh['src'=4,'delay'=8] {'src'}, dimensions={0}, use_global_device_ids=true | all-gather | bytes 163840 | tf_op jit(solution)/shard_map/all_gather | solution.py:60
  179.7 0.0 collective-permute-done.2
  179.7 0.7 bitcast_dynamic-update-slice_fusion
  180.4 2.6 %gather_fusion.3 = f32[48,16,128]{2,1,0:T(8,128)} fusion(f32[4,16,16,128]{3,2,1,0:T(8,128)} %bitcast_dynamic-update-slice_fusion, s32[48]{0:T(128)S(1)} %get-tuple-element.9), kind=kCustom, calls=%fused_computation.3 | custom fusion | bytes 786816 | tf_op jit(solution)/shard_map/gather | solution.py:43
  183.0 6.0 %fusion.77 = f32[48,16,128]{2,1,0:T(8,128)S(1)} fusion(f32[48,16,128]{2,1,0:T(8,128)} %gather_fusion.3, f32[48,128,128]{2,1,0:T(8,128)S(1)} %copy-done), kind=kOutput, calls=%fused_computation.124 | convolution fusion | flops 150994944 | bytes 3932160 | tf_op jit(solution)/shard_map/pab,prb->pra/dot_general | solution.py:44
  189.0 1.0 fusion
  190.0 23.6 %psum.31 = f32[4,16,128]{2,0,1:T(4,128)S(1)} all-reduce(f32[4,16,128]{2,0,1:T(4,128)} %fusion), channel_id=1, replica_groups=mesh['src'=4,'delay'=8] {'delay'}, use_global_device_ids=true, to_apply=%region_10.11 | all-reduce | flops 8192 | bytes 65536 | tf_op jit(solution)/shard_map/psum | solution.py:51
  213.6 0.8 fusion.12
  214.4 0.5 convolution_bitcast_fusion
  214.9 0.7 pad_maximum_fusion
  (10 shorter events, 0.1 us)
Async XLA Ops:
  0.0 31.3 %copy-start = (f32[48,128,128]{2,1,0:T(8,128)S(1)}, f32[48,128,128]{2,1,0:T(8,128)}, u32[]{:S(2)}) copy-start(f32[48,128,128]{2,1,0:T(8,128)} %param.9) | copy-start | bytes 9437188
  1.5 61.4 %copy-start.1 = (f32[4,128,128]{2,1,0:T(8,128)S(1)}, f32[4,128,128]{2,1,0:T(8,128)}, u32[]{:S(2)}) copy-start(f32[4,128,128]{2,1,0:T(8,128)} %param.12) | copy-start | bytes 786436
  24.5 55.9 %collective-permute-start = (f32[16,16,128]{2,1,0:T(8,128)}, f32[16,16,128]{2,1,0:T(8,128)}, u32[]{:S(2)}, u32[]{:S(2)}) collective-permute-start(f32[16,16,128]{2,1,0:T(8,128)} %dynamic-slice_bitcast_fusion.2), channel_id=1, source_target_pairs={{0,1},{1,2},{2,3},{3,4},{4,5},{5,6},{6,7},{8,9},{9,10},{10,11},{11... | collective-permute-start | bytes 393224 | tf_op jit(solution)/shard_map/ppermute | solution.py:10
  31.4 6.0 %copy-start.2 = (f32[48]{0:T(128)}, f32[48]{0:T(128)S(1)}, u32[]{:S(2)}) copy-start(f32[48]{0:T(128)S(1)} %compare_convert_fusion) | copy-start | bytes 580
  62.9 26.8 %copy-start.3 = (f32[48]{0:T(128)S(1)}, f32[48]{0:T(128)}, u32[]{:S(2)}) copy-start(f32[48]{0:T(128)} %copy-done.2) | copy-start | bytes 580
  89.7 49.6 %copy-start.4 = (f32[48]{0:T(128)S(1)}, f32[48]{0:T(128)}, u32[]{:S(2)}) copy-start(f32[48]{0:T(128)} %copy-done.2) | copy-start | bytes 580
  114.6 15.5 %collective-permute-start.1 = (f32[16,16,128]{2,1,0:T(8,128)S(1)}, f32[16,16,128]{2,1,0:T(8,128)S(1)}, u32[]{:S(2)}, u32[]{:S(2)}) collective-permute-start(f32[16,16,128]{2,1,0:T(8,128)S(1)} %dynamic-slice_bitcast_fusion.1), channel_id=1, source_target_pairs={{0,1},{1,2},{2,3},{3,4},{4,5},{5,6},{6,7},{8,9},{9,10},{10,11},{11... | collective-permute-start | bytes 393224 | tf_op jit(solution)/shard_map/ppermute | solution.py:10
  164.3 15.4 %collective-permute-start.2 = (f32[16,16,128]{2,1,0:T(8,128)S(1)}, f32[16,16,128]{2,1,0:T(8,128)S(1)}, u32[]{:S(2)}, u32[]{:S(2)}) collective-permute-start(f32[16,16,128]{2,1,0:T(8,128)S(1)} %dynamic-slice_bitcast_fusion), channel_id=1, source_target_pairs={{0,1},{1,2},{2,3},{3,4},{4,5},{5,6},{6,7},{8,9},{9,10},{10,11},{11... | collective-permute-start | bytes 393224 | tf_op jit(solution)/shard_map/ppermute | solution.py:10
where the time goes:
time: 218 us; the launch traced here: 216 us
  blocking collectives  153 us (70%)
  matrix products  29.4 us (13%)
  local copies, waits for them, and re-layouts  16.2 us (7%)
  between operations  6.33 us (3%)
  other arithmetic  5.83 us (3%)
  starting transfers between devices  4.66 us (2%)
    psum x4, blocking collectives, body(): field_sum = lax.psum(partial_field, 'delay')  93.2 us
    all_gather x3, blocking collectives, body(): newest = lax.all_gather(current, 'src', axis=0, tiled=True)  40.5 us
    dot_general x4, matrix products, body(): jnp.einsum('pab,prb->pra', interaction, picked, precision=lax.Precision.H...  23.8 us
    all_gather x1, blocking collectives, body(): band_state = lax.all_gather(history, 'src', axis=1, tiled=True)  19.5 us
    gather x4, local copies, waits for them, and re-layouts, body(): picked = band_state[holder, pattern[1]]  10.6 us
    ppermute x3, starting transfers between devices, shifted(): return lax.ppermute(x, axis, pairs)  4.66 us
  transfers between devices with their start and end apart: 3, of which 0 were waited for; matrix products, arithmetic and copies ran while one was open for 6% of the time, Pallas kernels for 0%

commit v1 on v0

v1 whole, which is shorter than its diff:
```python
import functools

import jax
import jax.numpy as jnp
from jax import lax
from jax.experimental import pallas as pl
from jax.experimental.pallas import tpu as pltpu
from jax.sharding import PartitionSpec as P

F32 = jnp.float32
BF16 = jnp.bfloat16
VMEM = pltpu.VMEM
SMEM = pltpu.SMEM
UNROLL = 8


def whole(space):
    return pl.BlockSpec(memory_space=space)


def swap(x, axis, bits):
    n = lax.axis_size(axis)
    return lax.ppermute(x, axis, [(i, i ^ bits) for i in range(n)])


def halves(x):
    high = x.astype(BF16)
    low = (x - high.astype(F32)).astype(BF16)
    return high, low


def wide(x):
    high, low = halves(x)
    return jnp.concatenate([high, low], axis=-1)


def times(rows, weights):
    both = jnp.concatenate([rows, rows], axis=-1)
    return lax.dot_general(both, weights, (((1,), (1,)), ((), ())), preferred_element_type=F32)


def split_kernel(pattern, live, blocks, wide_blocks, order, counts):
    wide_blocks[...] = wide(blocks[...])
    pairs = order.shape[0]
    kinds = counts.shape[0]

    @pl.when(pl.program_id(0) == 0)
    def _():
        def place(e, at):
            kind = pattern[2, e]
            for d in range(kinds):
                @pl.when(kind == d)
                def _():
                    order[at[d]] = e
            return tuple(at[d] + (kind == d).astype(jnp.int32) for d in range(kinds))

        def count(e, n):
            kind = pattern[2, e]
            return tuple(n[d] + (kind <= d).astype(jnp.int32) for d in range(kinds))

        def clear(e, c):
            order[e] = 0
            return c

        zero = jnp.int32(0)
        lax.fori_loop(0, pairs, clear, zero)
        upto = lax.fori_loop(0, live[0], count, (zero,) * kinds)
        for d in range(kinds):
            counts[d] = upto[d]
        lax.fori_loop(0, live[0], place, (zero,) + upto[:-1])


def split_blocks(pattern, live, blocks, kinds):
    pairs, a, q = blocks.shape
    per = pairs // 6 if pairs % 6 == 0 else pairs
    return pl.pallas_call(
        split_kernel,
        grid=(pairs // per,),
        in_specs=[whole(SMEM), whole(SMEM), pl.BlockSpec((per, a, q), lambda i: (i, 0, 0))],
        out_specs=[pl.BlockSpec((per, a, 2 * q), lambda i: (i, 0, 0)), whole(SMEM), whole(SMEM)],
        out_shape=[
            jax.ShapeDtypeStruct((pairs, a, 2 * q), BF16),
            jax.ShapeDtypeStruct((pairs,), jnp.int32),
            jax.ShapeDtypeStruct((kinds,), jnp.int32),
        ],
        name="split_blocks",
    )(pattern, live, blocks)


def past_kernel(first, span, steps, me, pattern, live, slots, blocks, *refs):
    *parts, out, packed = refs
    pairs = blocks.shape[0]
    groups = len(parts)
    places, group_blocks, columns, width = parts[0].shape
    nothing = groups * places * group_blocks
    for k in range(groups):
        high, low = halves(parts[k][...].reshape(places * group_blocks, columns, width))
        packed[pl.ds(k * places * group_blocks, places * group_blocks)] = jnp.concatenate([high, low], axis=1)
    packed[nothing] = jnp.zeros((2 * columns, width), BF16)
    out[...] = jnp.zeros_like(out)
    holder = [sum(jnp.where(slots[j] == d, j, 0) for j in range(places)) for d in range(places)]

    def place_of(p):
        at = holder[0]
        for d in range(1, places):
            at = jnp.where(p == d, holder[d], at)
        return at

    def batch(i, carry):
        made = []
        for u in range(UNROLL):
            e = i * UNROLL + u
            used = e < live[0]
            e = jnp.minimum(e, pairs - 1)
            column = pattern[1, e]
            group = (column // group_blocks) ^ me[0]
            rows = []
            for t in range(steps):
                p = pattern[2, e] - first - t + span
                good = used & (p >= 0) & (p < places)
                at = (group * places + place_of(p)) * group_blocks + column % group_blocks
                rows.append(packed[jnp.where(good, at, nothing)])
            made.append((pattern[0, e], times(jnp.concatenate(rows, axis=0), blocks[e])))
        for row, y in made:
            y = y.reshape(steps, 2, columns, width)
            out[:, row] += y[:, 0] + y[:, 1]
        return carry

    lax.fori_loop(0, (live[0] + UNROLL - 1) // UNROLL, batch, 0)


def past_field(first, span, steps, me, pattern, live, slots, blocks, parts):
    places, group_blocks, columns, width = parts[0].shape
    kernel = functools.partial(past_kernel, first, span, steps)
    return pl.pallas_call(
        kernel,
        in_specs=[whole(SMEM)] * 4 + [whole(VMEM)] * (1 + len(parts)),
        out_specs=whole(VMEM),
        out_shape=jax.ShapeDtypeStruct((steps, group_blocks, columns, width), F32),
        scratch_shapes=[VMEM((len(parts) * places * group_blocks + 1, 2 * columns, width), BF16)],
        compiler_params=pltpu.CompilerParams(vmem_limit_bytes=40 << 20),
        name="past_field",
    )(me, pattern, live, slots, blocks, *parts)


def step_kernel(moment, fields, me, front, pattern, order, counts, blocks, inverse, incident, *refs):
    given = refs[:fields]
    recent = refs[fields:-3]
    out, total, packed = refs[-3:]
    group_blocks, columns, width = out.shape
    field = given[0][...]
    for f in given[1:]:
        field = field + f[...]
    total[...] = incident[moment] - field.reshape(out.shape)
    if moment:
        groups = len(recent) // moment
        nothing = moment * groups * group_blocks
        for j, ref in enumerate(recent):
            high, low = halves(ref[...])
            packed[pl.ds(j * group_blocks, group_blocks)] = jnp.concatenate([high, low], axis=1)
        packed[nothing] = jnp.zeros((2 * columns, width), BF16)
        amount = jnp.where(front[0] == 0, counts[moment - 1], 0)

        def batch(i, carry):
            made = []
            for u in range(UNROLL):
                n = i * UNROLL + u
                e = order[jnp.minimum(n, order.shape[0] - 1)]
                column = pattern[1, e]
                group = (column // group_blocks) ^ me[0]
                source = moment - 1 - pattern[2, e]
                at = (source * groups + group) * group_blocks + column % group_blocks
                made.append((pattern[0, e], times(packed[jnp.where(n < amount, at, nothing)], blocks[e])))
            for row, y in made:
                y = y.reshape(2, columns, width)
                total[row] -= y[0] + y[1]
            return carry

        lax.fori_loop(0, (amount + UNROLL - 1) // UNROLL, batch, 0)
    for i in range(group_blocks):
        high, low = halves(total[i])
        y = times(jnp.concatenate([high, low], axis=0), wide(inverse[i])).reshape(2, columns, width)
        out[i] = y[0] + y[1]


def new_currents(moment, me, front, pattern, order, counts, blocks, inverse, incident, fields, recent):
    steps, group_blocks, columns, width = incident.shape
    return pl.pallas_call(
        functools.partial(step_kernel, moment, len(fields)),
        in_specs=[whole(SMEM)] * 5 + [whole(VMEM)] * (3 + len(fields) + len(recent)),
        out_specs=whole(VMEM),
        out_shape=jax.ShapeDtypeStruct((group_blocks, columns, width), F32),
        scratch_shapes=[
            VMEM((group_blocks, columns, width), F32),
            VMEM((len(recent) * group_blocks + 1, 2 * columns, width), BF16),
        ],
        compiler_params=pltpu.CompilerParams(vmem_limit_bytes=40 << 20),
        name="new_currents",
    )(me, front, pattern, order, counts, blocks, inverse, incident, *fields, *recent)


def summands(x):
    bands = lax.axis_size("delay")
    x = x + swap(x, "delay", 1)
    if bands <= 8:
        return [x] + [swap(x, "delay", k) for k in range(2, bands, 2)]
    bit = 2
    while bit < bands:
        x = x + swap(x, "delay", bit)
        bit *= 2
    return [x]


def from_front(x):
    bands = lax.axis_size("delay")
    mine = lax.axis_index("delay")
    bit = bands // 2
    while bit:
        other = swap(x, "delay", bit)
        x = jnp.where((mine & bit) != 0, other, x)
        bit //= 2
    return x


def body(history, slot_map, interaction, pattern, live, near_inverse, incident):
    slot_count = history.shape[0]
    moments = incident.shape[0]
    groups = lax.axis_size("src")
    bands = lax.axis_size("delay")
    assert moments - 1 <= slot_count
    assert groups & (groups - 1) == 0 and bands & (bands - 1) == 0
    me = lax.axis_index("src").reshape(1)
    front = lax.axis_index("delay").reshape(1)

    parts = [history] + [swap(history, "src", k) for k in range(1, groups)]
    blocks, order, counts = split_blocks(pattern, live, interaction, slot_count)
    field = past_field(0, 0, moments, me, pattern, live, slot_map, blocks, parts)

    late = moments - 1
    ring = [(i, (i + 1) % bands) for i in range(bands)]
    slots_before = lax.ppermute(slot_map, "delay", ring)
    before = [lax.ppermute(p, "delay", ring) for p in parts]
    live_before = jnp.where(front == 0, 0, live)
    more = past_field(1, slot_count, late, me, pattern, live_before, slots_before, blocks, before)

    first_fields = summands(field[0])
    later_fields = summands(field[1:] + more)
    step = functools.partial(new_currents, me=me, front=front, pattern=pattern, order=order, counts=counts,
                             blocks=blocks, inverse=near_inverse, incident=incident)
    results = [step(0, fields=first_fields, recent=[])]
    recent = []
    for moment in range(1, moments):
        newest = results[-1]
        recent = recent + [newest] + [swap(newest, "src", k) for k in range(1, groups)]
        results.append(step(moment, fields=[f[moment - 1] for f in later_fields], recent=recent))
    return jnp.concatenate([results[0][None], from_front(jnp.stack(results[1:]))])


def solution(mesh):
    return jax.shard_map(
        body,
        mesh=mesh,
        in_specs=(
            P("delay", "src", None, None),
            P("delay"),
            P(("src", "delay"), None, None),
            P(None, ("src", "delay")),
            P(("src", "delay")),
            P("src", None, None),
            P(None, "src", None, None),
        ),
        out_specs=P(None, "src", None, None),
        check_vma=False,
    )
```

time: 218 us -> 80.6 us (0.37); the launches traced: 216 us -> 81 us
  blocking collectives: 153 us -> 0 us
  starting transfers between devices: 4.66 us -> 36.2 us
  matrix products: 29.4 us -> 0 us
  waiting for transfers between devices: 0.01 us -> 28.9 us
  local copies, waits for them, and re-layouts: 16.2 us -> 1.95 us
  Pallas kernels: 0 us -> 12.4 us
  between operations: 6.33 us -> 0.86 us
  other arithmetic: 5.83 us -> 0.77 us
    psum x4 -> x0, blocking collectives: 93.2 us -> none  [body(): field_sum = lax.psum(partial_field, 'delay')]
    all_gather x4 -> x0, blocking collectives: 60 us -> none  [the longest x3 40.5 us: body(): newest = lax.all_gather(current, 'src', axis=0, tiled=True)]
    ppermute x3 -> x28, starting transfers between devices: 4.66 us -> 36.2 us  [the longest x23 32.5 us: swap(): return lax.ppermute(x, axis, [(i, i ^ bits) for i in range(n)])]
    dot_general x12 -> x0, matrix products: 29.4 us -> none  [the longest x4 23.8 us: body(): jnp.einsum('pab,prb->pra', interaction, picked, precision=lax.Precision.H...]
    ppermute x3 -> x28, waiting for transfers between devices: 0.01 us -> 28.9 us  [the longest x23 28.9 us: swap(): return lax.ppermute(x, axis, [(i, i ^ bits) for i in range(n)])]
    pallas_call x0 -> x7, Pallas kernels: none -> 12.4 us  [the longest x1 6.02 us: split_blocks(): pl.pallas_call(split_kernel, grid=(pairs // per,), in_specs=[whole(SMEM),...]
    gather x4 -> x0, local copies, waits for them, and re-layouts: 10.6 us -> none  [body(): picked = band_state[holder, pattern[1]]]
    squeeze x3 -> x5, local copies, waits for them, and re-layouts: 3.4 us -> 0.04 us  [the longest x4 0.03 us: body(): f[moment - 1]]
  transfers between devices with their start and end apart: 3 -> 28, of which waited for: 0 -> 13; matrix products, arithmetic and copies ran while one was open for 6% -> 0% of each run, Pallas kernels for 0% -> 11%
where the time goes in v1:
time: 80.6 us; the launch traced here: 81 us
  starting transfers between devices  36.2 us (45%)
  waiting for transfers between devices  28.9 us (36%)
  Pallas kernels  12.4 us (15%)
  local copies, waits for them, and re-layouts  1.95 us (2%)
  between operations  0.86 us (1%)
    ppermute x23, starting transfers between devices, swap(): return lax.ppermute(x, axis, [(i, i ^ bits) for i in range(n)])  32.5 us
    ppermute x23, waiting for transfers between devices, swap(): return lax.ppermute(x, axis, [(i, i ^ bits) for i in range(n)])  28.9 us
    pallas_call x1, Pallas kernels, split_blocks(): pl.pallas_call(split_kernel, grid=(pairs // per,), in_specs=[whole(SMEM),...  6.02 us
    pallas_call x4, Pallas kernels, new_currents(): pl.pallas_call(functools.partial(step_kernel, moment, len(fields)), in_sp...  4.33 us
    pallas_call x2, Pallas kernels, past_field(): pl.pallas_call(kernel, in_specs=[whole(SMEM)] * 4 + [whole(VMEM)] * (1 +...  2.05 us
    ppermute x4, starting transfers between devices, body(): before = [lax.ppermute(p, 'delay', ring) for p in parts]  2.02 us
    unnamed x16, local copies, waits for them, and re-layouts  1.91 us
  transfers between devices with their start and end apart: 28, of which 13 were waited for; matrix products, arithmetic and copies ran while one was open for 0% of the time, Pallas kernels for 11%

profile of v1, /device:TPU:0, one launch (start us, length us, event | category | flops | bytes accessed | tf_op | source)
XLA Modules:
  0.0 81.0 jit_solution(513068758626891329)
XLA Ops:
  0.0 4.1 %collective-permute-start.1 = (f32[4,4,16,128]{3,2,1,0:T(8,128)}, f32[4,4,16,128]{3,2,1,0:T(8,128)S(1)}, u32[]{:S(2)}, u32[]{:S(2)}) collective-permute-start(f32[4,4,16,128]{3,2,1,0:T(8,128)} %refs_0_.1), channel_id=1, source_target_pairs={{0,16},{8,24},{16,0},{24,8},{1,17},{9,25},{17,1},{25,9},{2,18},{10... | collective-permute-start | bytes 393224 | tf_op jit(solution)/shard_map/ppermute | solution.py:23
  4.1 1.3 %collective-permute-start.2 = (f32[4,4,16,128]{3,2,1,0:T(8,128)}, f32[4,4,16,128]{3,2,1,0:T(8,128)S(1)}, u32[]{:S(2)}, u32[]{:S(2)}) collective-permute-start(f32[4,4,16,128]{3,2,1,0:T(8,128)} %refs_0_.1), channel_id=1, source_target_pairs={{0,24},{8,16},{16,8},{24,0},{1,25},{9,17},{17,9},{25,1},{2,26},{10... | collective-permute-start | bytes 393224 | tf_op jit(solution)/shard_map/ppermute | solution.py:23
  5.5 0.2 collective-permute-start
  5.7 1.6 %collective-permute-start.7 = (s32[4]{0:T(128)}, s32[4]{0:T(128)S(1)}, u32[]{:S(2)}, u32[]{:S(2)}) collective-permute-start(s32[4]{0:T(128)} %slots.1), channel_id=1, source_target_pairs={{0,1},{1,2},{2,3},{3,4},{4,5},{5,6},{6,7},{7,0},{8,9},{9,10},{10,1... | collective-permute-start | bytes 56 | tf_op jit(solution)/shard_map/ppermute | solution.py:241
  8.0 6.0 %split_blocks.1 = (bf16[48,128,256]{2,1,0:T(8,128)(2,1)}, s32[48]{0:T(128)}, s32[4]{0:T(128)}) custom-call(s32[3,48]{1,0:T(4,128)} %pattern.13, s32[1]{0:T(128)S(6)} %copy.8.live, f32[48,128,128]{2,1,0:T(8,128)} %blocks.1), custom_call_target="tpu_custom_call" | custom-call | tf_op jit(solution)/shard_map/split_blocks/pallas_call | solution.py:76
  14.0 0.3 collective-permute-done.1.refs_2_
  14.3 0.5 collective-permute-start.10
  14.8 1.5 %collective-permute-start.11 = (f32[4,4,16,128]{3,2,1,0:T(8,128)S(1)}, f32[4,4,16,128]{3,2,1,0:T(8,128)S(1)}, u32[]{:S(2)}, u32[]{:S(2)}) collective-permute-start(f32[4,4,16,128]{3,2,1,0:T(8,128)S(1)} %collective-permute-done.2.refs_3_), channel_id=1, source_target_pairs={{0,1},{1,2},{2,3},{3,4},{4,5},{5,6},{6,7},{7,0},{8,9},{9,10},{10,1... | collective-permute-start | bytes 393224 | tf_op jit(solution)/shard_map/ppermute | solution.py:242
  16.3 0.1 collective-permute-start.9
  16.3 1.9 %copy-done = bf16[48,128,256]{2,1,0:T(8,128)(2,1)S(1)} copy-done((bf16[48,128,256]{2,1,0:T(8,128)(2,1)S(1)}, bf16[48,128,256]{2,1,0:T(8,128)(2,1)}, u32[]{:S(2)}) %copy-start) | copy-done | bytes 3145752
  18.2 1.4 %past_field.2 = f32[4,4,16,128]{3,2,1,0:T(8,128)S(1)} custom-call(s32[1]{0:T(128)} %bitcast.me, s32[3,48]{1,0:T(4,128)S(1)} %copy-done.4, s32[1]{0:T(128)S(6)} %copy.8.live, s32[4]{0:T(128)S(1)} %copy-done.7, bf16[48,128,256]{2,1,0:T(8,128)(2,1)S(1)} %copy-done, f32[4,4,16,128]{3,2,1,0:T(8,128)S(1)} %copy-done.3, ...), custom_call_target="tpu_custom_call" | custom-call | tf_op jit(solution)/shard_map/past_field/pallas_call | solution.py:135
  19.7 3.2 %collective-permute-start.3 = (f32[4,16,128]{2,1,0:T(8,128)S(1)}, f32[4,16,128]{2,1,0:T(8,128)S(1)}, u32[]{:S(2)}, u32[]{:S(2)}) collective-permute-start(f32[4,16,128]{2,1,0:T(8,128)S(1)} %slice_bitcast_fusion.12), channel_id=1, source_target_pairs={{0,1},{1,0},{2,3},{3,2},{4,5},{5,4},{6,7},{7,6},{8,9},{9,8},{10,11... | collective-permute-start | bytes 98312 | tf_op jit(solution)/shard_map/ppermute | solution.py:23
  22.9 0.6 past_field.3
  23.6 2.2 %collective-permute-start.12 = (f32[3,4,16,128]{3,2,1,0:T(8,128)S(1)}, f32[3,4,16,128]{3,2,1,0:T(8,128)S(1)}, u32[]{:S(2)}, u32[]{:S(2)}) collective-permute-start(f32[3,4,16,128]{3,2,1,0:T(8,128)S(1)} %slice_add_fusion), channel_id=1, source_target_pairs={{0,1},{1,0},{2,3},{3,2},{4,5},{5,4},{6,7},{7,6},{8,9},{9,8},{10,11... | collective-permute-start | bytes 294920 | tf_op jit(solution)/shard_map/ppermute | solution.py:23
  25.8 0.8 %collective-permute-start.4 = (f32[4,16,128]{2,1,0:T(8,128)S(1)}, f32[4,16,128]{2,1,0:T(8,128)S(1)}, u32[]{:S(2)}, u32[]{:S(2)}) collective-permute-start(f32[4,16,128]{2,1,0:T(8,128)S(1)} %fusion.refs_0_), channel_id=1, source_target_pairs={{0,2},{1,3},{2,0},{3,1},{4,6},{5,7},{6,4},{7,5},{8,10},{9,11},{10,... | collective-permute-start | bytes 98312 | tf_op jit(solution)/shard_map/ppermute | solution.py:23
  26.6 1.3 %collective-permute-start.5 = (f32[4,16,128]{2,1,0:T(8,128)S(1)}, f32[4,16,128]{2,1,0:T(8,128)S(1)}, u32[]{:S(2)}, u32[]{:S(2)}) collective-permute-start(f32[4,16,128]{2,1,0:T(8,128)S(1)} %fusion.refs_0_), channel_id=1, source_target_pairs={{0,4},{1,5},{2,6},{3,7},{4,0},{5,1},{6,2},{7,3},{8,12},{9,13},{10,... | collective-permute-start | bytes 98312 | tf_op jit(solution)/shard_map/ppermute | solution.py:23
  27.8 1.5 %collective-permute-start.6 = (f32[4,16,128]{2,1,0:T(8,128)S(1)}, f32[4,16,128]{2,1,0:T(8,128)S(1)}, u32[]{:S(2)}, u32[]{:S(2)}) collective-permute-start(f32[4,16,128]{2,1,0:T(8,128)S(1)} %fusion.refs_0_), channel_id=1, source_target_pairs={{0,6},{1,7},{2,4},{3,5},{4,2},{5,3},{6,0},{7,1},{8,14},{9,15},{10,... | collective-permute-start | bytes 98312 | tf_op jit(solution)/shard_map/ppermute | solution.py:23
  29.3 0.4 collective-permute-done.4.refs_1_
  29.7 0.7 collective-permute-done.5.refs_2_
  30.5 2.1 %collective-permute-done.6.refs_3_ = f32[4,16,128]{2,1,0:T(8,128)S(1)} collective-permute-done((f32[4,16,128]{2,1,0:T(8,128)S(1)}, f32[4,16,128]{2,1,0:T(8,128)S(1)}, u32[]{:S(2)}, u32[]{:S(2)}) %collective-permute-start.6) | collective-permute-done | bytes 32800 | tf_op jit(solution)/shard_map/ppermute | solution.py:23
  32.7 0.8 new_currents.4.refs_4_
  33.4 1.6 %collective-permute-start.16 = (f32[4,16,128]{2,1,0:T(8,128)S(1)}, f32[4,16,128]{2,1,0:T(8,128)S(1)}, u32[]{:S(2)}, u32[]{:S(2)}) collective-permute-start(f32[4,16,128]{2,1,0:T(8,128)S(1)} %new_currents.4.refs_4_), channel_id=1, source_target_pairs={{0,8},{8,0},{16,24},{24,16},{1,9},{9,1},{17,25},{25,17},{2,10},{10... | collective-permute-start | bytes 98312 | tf_op jit(solution)/shard_map/ppermute | solution.py:23
  35.0 2.2 %collective-permute-start.17 = (f32[4,16,128]{2,1,0:T(8,128)S(1)}, f32[4,16,128]{2,1,0:T(8,128)S(1)}, u32[]{:S(2)}, u32[]{:S(2)}) collective-permute-start(f32[4,16,128]{2,1,0:T(8,128)S(1)} %new_currents.4.refs_4_), channel_id=1, source_target_pairs={{0,16},{8,24},{16,0},{24,8},{1,17},{9,25},{17,1},{25,9},{2,18},{10... | collective-permute-start | bytes 98312 | tf_op jit(solution)/shard_map/ppermute | solution.py:23
  37.2 0.8 %collective-permute-start.18 = (f32[4,16,128]{2,1,0:T(8,128)S(1)}, f32[4,16,128]{2,1,0:T(8,128)S(1)}, u32[]{:S(2)}, u32[]{:S(2)}) collective-permute-start(f32[4,16,128]{2,1,0:T(8,128)S(1)} %new_currents.4.refs_4_), channel_id=1, source_target_pairs={{0,24},{8,16},{16,8},{24,0},{1,25},{9,17},{17,9},{25,1},{2,26},{10... | collective-permute-start | bytes 98312 | tf_op jit(solution)/shard_map/ppermute | solution.py:23
  38.1 1.3 %collective-permute-start.15 = (f32[3,4,16,128]{3,2,1,0:T(8,128)S(1)}, f32[3,4,16,128]{3,2,1,0:T(8,128)S(1)}, u32[]{:S(2)}, u32[]{:S(2)}) collective-permute-start(f32[3,4,16,128]{3,2,1,0:T(8,128)S(1)} %add.11), channel_id=1, source_target_pairs={{0,6},{1,7},{2,4},{3,5},{4,2},{5,3},{6,0},{7,1},{8,14},{9,15},{10,... | collective-permute-start | bytes 294920 | tf_op jit(solution)/shard_map/ppermute | solution.py:23
  39.4 1.3 %collective-permute-start.14 = (f32[3,4,16,128]{3,2,1,0:T(8,128)S(1)}, f32[3,4,16,128]{3,2,1,0:T(8,128)S(1)}, u32[]{:S(2)}, u32[]{:S(2)}) collective-permute-start(f32[3,4,16,128]{3,2,1,0:T(8,128)S(1)} %add.11), channel_id=1, source_target_pairs={{0,4},{1,5},{2,6},{3,7},{4,0},{5,1},{6,2},{7,3},{8,12},{9,13},{10,... | collective-permute-start | bytes 294920 | tf_op jit(solution)/shard_map/ppermute | solution.py:23
  40.7 3.3 %collective-permute-done.15 = f32[3,4,16,128]{3,2,1,0:T(8,128)S(1)} collective-permute-done((f32[3,4,16,128]{3,2,1,0:T(8,128)S(1)}, f32[3,4,16,128]{3,2,1,0:T(8,128)S(1)}, u32[]{:S(2)}, u32[]{:S(2)}) %collective-permute-start.15) | collective-permute-done | bytes 98336 | tf_op jit(solution)/shard_map/ppermute | solution.py:23
  44.0 1.6 %collective-permute-start.13 = (f32[3,4,16,128]{3,2,1,0:T(8,128)S(1)}, f32[3,4,16,128]{3,2,1,0:T(8,128)S(1)}, u32[]{:S(2)}, u32[]{:S(2)}) collective-permute-start(f32[3,4,16,128]{3,2,1,0:T(8,128)S(1)} %add.11), channel_id=1, source_target_pairs={{0,2},{1,3},{2,0},{3,1},{4,6},{5,7},{6,4},{7,5},{8,10},{9,11},{10,... | collective-permute-start | bytes 294920 | tf_op jit(solution)/shard_map/ppermute | solution.py:23
  45.7 2.9 %collective-permute-done.13 = f32[3,4,16,128]{3,2,1,0:T(8,128)S(1)} collective-permute-done((f32[3,4,16,128]{3,2,1,0:T(8,128)S(1)}, f32[3,4,16,128]{3,2,1,0:T(8,128)S(1)}, u32[]{:S(2)}, u32[]{:S(2)}) %collective-permute-start.13) | collective-permute-done | bytes 98336 | tf_op jit(solution)/shard_map/ppermute | solution.py:23
  48.7 1.1 %new_currents.5.refs_8_ = f32[4,16,128]{2,1,0:T(8,128)S(1)} custom-call(s32[1]{0:T(128)} %bitcast.me, s32[1]{0:T(128)} %bitcast.1.front, s32[3,48]{1,0:T(4,128)S(1)} %copy-done.4, s32[48]{0:T(128)S(1)} %copy-done.5, s32[4]{0:T(128)S(1)} %copy-done.6, bf16[48,128,256]{2,1,0:T(8,128)(2,1)S(1)} %copy-done, f32[4,128,128]{2,1,0:T(8,128)S(1)} %copy-done.1, ...), custom_call_target="tpu_custom_call" | custom-call | tf_op jit(solution)/shard_map/new_currents/pallas_call | solution.py:188
  49.8 1.0 %collective-permute-start.19 = (f32[4,16,128]{2,1,0:T(8,128)S(1)}, f32[4,16,128]{2,1,0:T(8,128)S(1)}, u32[]{:S(2)}, u32[]{:S(2)}) collective-permute-start(f32[4,16,128]{2,1,0:T(8,128)S(1)} %new_currents.5.refs_8_), channel_id=1, source_target_pairs={{0,8},{8,0},{16,24},{24,16},{1,9},{9,1},{17,25},{25,17},{2,10},{10... | collective-permute-start | bytes 98312 | tf_op jit(solution)/shard_map/ppermute | solution.py:23
  50.8 2.6 %collective-permute-start.20 = (f32[4,16,128]{2,1,0:T(8,128)S(1)}, f32[4,16,128]{2,1,0:T(8,128)S(1)}, u32[]{:S(2)}, u32[]{:S(2)}) collective-permute-start(f32[4,16,128]{2,1,0:T(8,128)S(1)} %new_currents.5.refs_8_), channel_id=1, source_target_pairs={{0,16},{8,24},{16,0},{24,8},{1,17},{9,25},{17,1},{25,9},{2,18},{10... | collective-permute-start | bytes 98312 | tf_op jit(solution)/shard_map/ppermute | solution.py:23
  53.4 0.8 collective-permute-start.21
  54.2 1.4 %collective-permute-done.20.refs_10_ = f32[4,16,128]{2,1,0:T(8,128)S(1)} collective-permute-done((f32[4,16,128]{2,1,0:T(8,128)S(1)}, f32[4,16,128]{2,1,0:T(8,128)S(1)}, u32[]{:S(2)}, u32[]{:S(2)}) %collective-permute-start.20) | collective-permute-done | bytes 32800 | tf_op jit(solution)/shard_map/ppermute | solution.py:23
  55.6 3.9 %collective-permute-done.21.refs_11_ = f32[4,16,128]{2,1,0:T(8,128)S(1)} collective-permute-done((f32[4,16,128]{2,1,0:T(8,128)S(1)}, f32[4,16,128]{2,1,0:T(8,128)S(1)}, u32[]{:S(2)}, u32[]{:S(2)}) %collective-permute-start.21) | collective-permute-done | bytes 32800 | tf_op jit(solution)/shard_map/ppermute | solution.py:23
  59.4 1.1 %new_currents.6.refs_12_ = f32[4,16,128]{2,1,0:T(8,128)S(1)} custom-call(s32[1]{0:T(128)} %bitcast.me, s32[1]{0:T(128)} %bitcast.1.front, s32[3,48]{1,0:T(4,128)S(1)} %copy-done.4, s32[48]{0:T(128)S(1)} %copy-done.5, s32[4]{0:T(128)S(1)} %copy-done.6, bf16[48,128,256]{2,1,0:T(8,128)(2,1)S(1)} %copy-done, f32[4,128,128]{2,1,0:T(8,128)S(1)} %copy-done.1, ...), custom_call_target="tpu_custom_call" | custom-call | tf_op jit(solution)/shard_map/new_currents/pallas_call | solution.py:188
  60.5 1.9 %collective-permute-start.23 = (f32[4,16,128]{2,1,0:T(8,128)S(1)}, f32[4,16,128]{2,1,0:T(8,128)S(1)}, u32[]{:S(2)}, u32[]{:S(2)}) collective-permute-start(f32[4,16,128]{2,1,0:T(8,128)S(1)} %new_currents.6.refs_12_), channel_id=1, source_target_pairs={{0,16},{8,24},{16,0},{24,8},{1,17},{9,25},{17,1},{25,9},{2,18},{10... | collective-permute-start | bytes 98312 | tf_op jit(solution)/shard_map/ppermute | solution.py:23
  62.5 2.5 %collective-permute-start.24 = (f32[4,16,128]{2,1,0:T(8,128)S(1)}, f32[4,16,128]{2,1,0:T(8,128)S(1)}, u32[]{:S(2)}, u32[]{:S(2)}) collective-permute-start(f32[4,16,128]{2,1,0:T(8,128)S(1)} %new_currents.6.refs_12_), channel_id=1, source_target_pairs={{0,24},{8,16},{16,8},{24,0},{1,25},{9,17},{17,9},{25,1},{2,26},{10... | collective-permute-start | bytes 98312 | tf_op jit(solution)/shard_map/ppermute | solution.py:23
  64.9 0.5 collective-permute-done.23.refs_14_
  65.4 2.8 %collective-permute-done.24.refs_15_ = f32[4,16,128]{2,1,0:T(8,128)S(1)} collective-permute-done((f32[4,16,128]{2,1,0:T(8,128)S(1)}, f32[4,16,128]{2,1,0:T(8,128)S(1)}, u32[]{:S(2)}, u32[]{:S(2)}) %collective-permute-start.24) | collective-permute-done | bytes 32800 | tf_op jit(solution)/shard_map/ppermute | solution.py:23
  68.2 1.4 %new_currents.7 = f32[4,16,128]{2,1,0:T(8,128)S(1)} custom-call(s32[1]{0:T(128)} %bitcast.me, s32[1]{0:T(128)} %bitcast.1.front, s32[3,48]{1,0:T(4,128)S(1)} %copy-done.4, s32[48]{0:T(128)S(1)} %copy-done.5, s32[4]{0:T(128)S(1)} %copy-done.6, bf16[48,128,256]{2,1,0:T(8,128)(2,1)S(1)} %copy-done, f32[4,128,128]{2,1,0:T(8,128)S(1)} %copy-done.1, ...), custom_call_target="tpu_custom_call" | custom-call | tf_op jit(solution)/shard_map/new_currents/pallas_call | solution.py:188
  69.6 0.1 collective-permute-start.25
  69.7 4.6 %collective-permute-done.25 = f32[3,4,16,128]{3,2,1,0:T(8,128)S(1)} collective-permute-done((f32[3,4,16,128]{3,2,1,0:T(8,128)S(1)}, f32[3,4,16,128]{3,2,1,0:T(8,128)S(1)}, u32[]{:S(2)}, u32[]{:S(2)}) %collective-permute-start.25) | collective-permute-done | bytes 98336 | tf_op jit(solution)/shard_map/ppermute | solution.py:23
  74.3 0.1 collective-permute-start.26
  74.4 4.6 %collective-permute-done.26 = f32[3,4,16,128]{3,2,1,0:T(8,128)S(1)} collective-permute-done((f32[3,4,16,128]{3,2,1,0:T(8,128)S(1)}, f32[3,4,16,128]{3,2,1,0:T(8,128)S(1)}, u32[]{:S(2)}, u32[]{:S(2)}) %collective-permute-start.26) | collective-permute-done | bytes 98336 | tf_op jit(solution)/shard_map/ppermute | solution.py:23
  79.0 0.1 collective-permute-start.27
  79.1 1.3 %collective-permute-done.27 = f32[3,4,16,128]{3,2,1,0:T(8,128)S(1)} collective-permute-done((f32[3,4,16,128]{3,2,1,0:T(8,128)S(1)}, f32[3,4,16,128]{3,2,1,0:T(8,128)S(1)}, u32[]{:S(2)}, u32[]{:S(2)}) %collective-permute-start.27) | collective-permute-done | bytes 98336 | tf_op jit(solution)/shard_map/ppermute | solution.py:23
  80.4 0.7 pad_maximum_fusion
  (44 shorter events, 0.2 us)
Async XLA Ops:
  0.0 16.3 %copy-start.3 = (f32[4,4,16,128]{3,2,1,0:T(8,128)S(1)}, f32[4,4,16,128]{3,2,1,0:T(8,128)}, u32[]{:S(2)}) copy-start(f32[4,4,16,128]{3,2,1,0:T(8,128)} %refs_0_.1) | copy-start | bytes 393220
  0.0 16.3 %copy-start.7 = (s32[4]{0:T(128)S(1)}, s32[4]{0:T(128)}, u32[]{:S(2)}) copy-start(s32[4]{0:T(128)} %slots.1) | copy-start | bytes 52
  0.0 16.3 %copy-start.4 = (s32[3,48]{1,0:T(4,128)S(1)}, s32[3,48]{1,0:T(4,128)}, u32[]{:S(2)}) copy-start(s32[3,48]{1,0:T(4,128)} %pattern.13) | copy-start | bytes 1732
  0.0 14.3 %collective-permute-start.1 = (f32[4,4,16,128]{3,2,1,0:T(8,128)}, f32[4,4,16,128]{3,2,1,0:T(8,128)S(1)}, u32[]{:S(2)}, u32[]{:S(2)}) collective-permute-start(f32[4,4,16,128]{3,2,1,0:T(8,128)} %refs_0_.1), channel_id=1, source_target_pairs={{0,16},{8,24},{16,0},{24,8},{1,17},{9,25},{17,1},{25,9},{2,18},{10... | collective-permute-start | bytes 393224 | tf_op jit(solution)/shard_map/ppermute | solution.py:23
  4.1 10.7 %collective-permute-start.2 = (f32[4,4,16,128]{3,2,1,0:T(8,128)}, f32[4,4,16,128]{3,2,1,0:T(8,128)S(1)}, u32[]{:S(2)}, u32[]{:S(2)}) collective-permute-start(f32[4,4,16,128]{3,2,1,0:T(8,128)} %refs_0_.1), channel_id=1, source_target_pairs={{0,24},{8,16},{16,8},{24,0},{1,25},{9,17},{17,9},{25,1},{2,26},{10... | collective-permute-start | bytes 393224 | tf_op jit(solution)/shard_map/ppermute | solution.py:23
  5.5 10.8 %collective-permute-start = (f32[4,4,16,128]{3,2,1,0:T(8,128)}, f32[4,4,16,128]{3,2,1,0:T(8,128)S(1)}, u32[]{:S(2)}, u32[]{:S(2)}) collective-permute-start(f32[4,4,16,128]{3,2,1,0:T(8,128)} %refs_0_.1), channel_id=1, source_target_pairs={{0,8},{8,0},{16,24},{24,16},{1,9},{9,1},{17,25},{25,17},{2,10},{10... | collective-permute-start | bytes 393224 | tf_op jit(solution)/shard_map/ppermute | solution.py:23
  5.7 17.2 %collective-permute-start.8 = (f32[4,4,16,128]{3,2,1,0:T(8,128)}, f32[4,4,16,128]{3,2,1,0:T(8,128)S(1)}, u32[]{:S(2)}, u32[]{:S(2)}) collective-permute-start(f32[4,4,16,128]{3,2,1,0:T(8,128)} %refs_0_.1), channel_id=1, source_target_pairs={{0,1},{1,2},{2,3},{3,4},{4,5},{5,6},{6,7},{7,0},{8,9},{9,10},{10,1... | collective-permute-start | bytes 393224 | tf_op jit(solution)/shard_map/ppermute | solution.py:242
  5.7 14.0 %collective-permute-start.7 = (s32[4]{0:T(128)}, s32[4]{0:T(128)S(1)}, u32[]{:S(2)}, u32[]{:S(2)}) collective-permute-start(s32[4]{0:T(128)} %slots.1), channel_id=1, source_target_pairs={{0,1},{1,2},{2,3},{3,4},{4,5},{5,6},{6,7},{7,0},{8,9},{9,10},{10,1... | collective-permute-start | bytes 56 | tf_op jit(solution)/shard_map/ppermute | solution.py:241
  14.3 8.6 %collective-permute-start.10 = (f32[4,4,16,128]{3,2,1,0:T(8,128)S(1)}, f32[4,4,16,128]{3,2,1,0:T(8,128)S(1)}, u32[]{:S(2)}, u32[]{:S(2)}) collective-permute-start(f32[4,4,16,128]{3,2,1,0:T(8,128)S(1)} %collective-permute-done.1.refs_2_), channel_id=1, source_target_pairs={{0,1},{1,2},{2,3},{3,4},{4,5},{5,6},{6,7},{7,0},{8,9},{9,10},{10,1... | collective-permute-start | bytes 393224 | tf_op jit(solution)/shard_map/ppermute | solution.py:242
  14.8 8.1 %collective-permute-start.11 = (f32[4,4,16,128]{3,2,1,0:T(8,128)S(1)}, f32[4,4,16,128]{3,2,1,0:T(8,128)S(1)}, u32[]{:S(2)}, u32[]{:S(2)}) collective-permute-start(f32[4,4,16,128]{3,2,1,0:T(8,128)S(1)} %collective-permute-done.2.refs_3_), channel_id=1, source_target_pairs={{0,1},{1,2},{2,3},{3,4},{4,5},{5,6},{6,7},{7,0},{8,9},{9,10},{10,1... | collective-permute-start | bytes 393224 | tf_op jit(solution)/shard_map/ppermute | solution.py:242
  16.3 6.6 %collective-permute-start.9 = (f32[4,4,16,128]{3,2,1,0:T(8,128)S(1)}, f32[4,4,16,128]{3,2,1,0:T(8,128)S(1)}, u32[]{:S(2)}, u32[]{:S(2)}) collective-permute-start(f32[4,4,16,128]{3,2,1,0:T(8,128)S(1)} %collective-permute-done.refs_1_), channel_id=1, source_target_pairs={{0,1},{1,2},{2,3},{3,4},{4,5},{5,6},{6,7},{7,0},{8,9},{9,10},{10,1... | collective-permute-start | bytes 393224 | tf_op jit(solution)/shard_map/ppermute | solution.py:242
  16.3 1.9 %copy-start = (bf16[48,128,256]{2,1,0:T(8,128)(2,1)S(1)}, bf16[48,128,256]{2,1,0:T(8,128)(2,1)}, u32[]{:S(2)}) copy-start(bf16[48,128,256]{2,1,0:T(8,128)(2,1)} %get-tuple-element.10.blocks) | copy-start | bytes 9437188
  18.2 14.4 %copy-start.1 = (f32[4,128,128]{2,1,0:T(8,128)S(1)}, f32[4,128,128]{2,1,0:T(8,128)}, u32[]{:S(2)}) copy-start(f32[4,128,128]{2,1,0:T(8,128)} %inverse.7) | copy-start | bytes 786436
  18.2 14.4 %copy-start.2 = (f32[4,4,16,128]{3,2,1,0:T(8,128)S(1)}, f32[4,4,16,128]{3,2,1,0:T(8,128)}, u32[]{:S(2)}) copy-start(f32[4,4,16,128]{3,2,1,0:T(8,128)} %incident.7) | copy-start | bytes 393220
  18.2 14.4 %copy-start.5 = (s32[48]{0:T(128)S(1)}, s32[48]{0:T(128)}, u32[]{:S(2)}) copy-start(s32[48]{0:T(128)} %get-tuple-element.8.order) | copy-start | bytes 580
  18.2 14.4 %copy-start.6 = (s32[4]{0:T(128)S(1)}, s32[4]{0:T(128)}, u32[]{:S(2)}) copy-start(s32[4]{0:T(128)} %get-tuple-element.9.counts) | copy-start | bytes 52
  19.7 6.1 %collective-permute-start.3 = (f32[4,16,128]{2,1,0:T(8,128)S(1)}, f32[4,16,128]{2,1,0:T(8,128)S(1)}, u32[]{:S(2)}, u32[]{:S(2)}) collective-permute-start(f32[4,16,128]{2,1,0:T(8,128)S(1)} %slice_bitcast_fusion.12), channel_id=1, source_target_pairs={{0,1},{1,0},{2,3},{3,2},{4,5},{5,4},{6,7},{7,6},{8,9},{9,8},{10,11... | collective-permute-start | bytes 98312 | tf_op jit(solution)/shard_map/ppermute | solution.py:23
  23.6 14.5 %collective-permute-start.12 = (f32[3,4,16,128]{3,2,1,0:T(8,128)S(1)}, f32[3,4,16,128]{3,2,1,0:T(8,128)S(1)}, u32[]{:S(2)}, u32[]{:S(2)}) collective-permute-start(f32[3,4,16,128]{3,2,1,0:T(8,128)S(1)} %slice_add_fusion), channel_id=1, source_target_pairs={{0,1},{1,0},{2,3},{3,2},{4,5},{5,4},{6,7},{7,6},{8,9},{9,8},{10,11... | collective-permute-start | bytes 294920 | tf_op jit(solution)/shard_map/ppermute | solution.py:23
  25.8 4.0 %collective-permute-start.4 = (f32[4,16,128]{2,1,0:T(8,128)S(1)}, f32[4,16,128]{2,1,0:T(8,128)S(1)}, u32[]{:S(2)}, u32[]{:S(2)}) collective-permute-start(f32[4,16,128]{2,1,0:T(8,128)S(1)} %fusion.refs_0_), channel_id=1, source_target_pairs={{0,2},{1,3},{2,0},{3,1},{4,6},{5,7},{6,4},{7,5},{8,10},{9,11},{10,... | collective-permute-start | bytes 98312 | tf_op jit(solution)/shard_map/ppermute | solution.py:23
  26.6 3.9 %collective-permute-start.5 = (f32[4,16,128]{2,1,0:T(8,128)S(1)}, f32[4,16,128]{2,1,0:T(8,128)S(1)}, u32[]{:S(2)}, u32[]{:S(2)}) collective-permute-start(f32[4,16,128]{2,1,0:T(8,128)S(1)} %fusion.refs_0_), channel_id=1, source_target_pairs={{0,4},{1,5},{2,6},{3,7},{4,0},{5,1},{6,2},{7,3},{8,12},{9,13},{10,... | collective-permute-start | bytes 98312 | tf_op jit(solution)/shard_map/ppermute | solution.py:23
  27.8 4.8 %collective-permute-start.6 = (f32[4,16,128]{2,1,0:T(8,128)S(1)}, f32[4,16,128]{2,1,0:T(8,128)S(1)}, u32[]{:S(2)}, u32[]{:S(2)}) collective-permute-start(f32[4,16,128]{2,1,0:T(8,128)S(1)} %fusion.refs_0_), channel_id=1, source_target_pairs={{0,6},{1,7},{2,4},{3,5},{4,2},{5,3},{6,0},{7,1},{8,14},{9,15},{10,... | collective-permute-start | bytes 98312 | tf_op jit(solution)/shard_map/ppermute | solution.py:23
  33.4 15.2 %collective-permute-start.16 = (f32[4,16,128]{2,1,0:T(8,128)S(1)}, f32[4,16,128]{2,1,0:T(8,128)S(1)}, u32[]{:S(2)}, u32[]{:S(2)}) collective-permute-start(f32[4,16,128]{2,1,0:T(8,128)S(1)} %new_currents.4.refs_4_), channel_id=1, source_target_pairs={{0,8},{8,0},{16,24},{24,16},{1,9},{9,1},{17,25},{25,17},{2,10},{10... | collective-permute-start | bytes 98312 | tf_op jit(solution)/shard_map/ppermute | solution.py:23
  35.0 13.6 %collective-permute-start.17 = (f32[4,16,128]{2,1,0:T(8,128)S(1)}, f32[4,16,128]{2,1,0:T(8,128)S(1)}, u32[]{:S(2)}, u32[]{:S(2)}) collective-permute-start(f32[4,16,128]{2,1,0:T(8,128)S(1)} %new_currents.4.refs_4_), channel_id=1, source_target_pairs={{0,16},{8,24},{16,0},{24,8},{1,17},{9,25},{17,1},{25,9},{2,18},{10... | collective-permute-start | bytes 98312 | tf_op jit(solution)/shard_map/ppermute | solution.py:23
  37.2 11.5 %collective-permute-start.18 = (f32[4,16,128]{2,1,0:T(8,128)S(1)}, f32[4,16,128]{2,1,0:T(8,128)S(1)}, u32[]{:S(2)}, u32[]{:S(2)}) collective-permute-start(f32[4,16,128]{2,1,0:T(8,128)S(1)} %new_currents.4.refs_4_), channel_id=1, source_target_pairs={{0,24},{8,16},{16,8},{24,0},{1,25},{9,17},{17,9},{25,1},{2,26},{10... | collective-permute-start | bytes 98312 | tf_op jit(solution)/shard_map/ppermute | solution.py:23
  38.1 5.9 %collective-permute-start.15 = (f32[3,4,16,128]{3,2,1,0:T(8,128)S(1)}, f32[3,4,16,128]{3,2,1,0:T(8,128)S(1)}, u32[]{:S(2)}, u32[]{:S(2)}) collective-permute-start(f32[3,4,16,128]{3,2,1,0:T(8,128)S(1)} %add.11), channel_id=1, source_target_pairs={{0,6},{1,7},{2,4},{3,5},{4,2},{5,3},{6,0},{7,1},{8,14},{9,15},{10,... | collective-permute-start | bytes 294920 | tf_op jit(solution)/shard_map/ppermute | solution.py:23
  39.4 6.2 %collective-permute-start.14 = (f32[3,4,16,128]{3,2,1,0:T(8,128)S(1)}, f32[3,4,16,128]{3,2,1,0:T(8,128)S(1)}, u32[]{:S(2)}, u32[]{:S(2)}) collective-permute-start(f32[3,4,16,128]{3,2,1,0:T(8,128)S(1)} %add.11), channel_id=1, source_target_pairs={{0,4},{1,5},{2,6},{3,7},{4,0},{5,1},{6,2},{7,3},{8,12},{9,13},{10,... | collective-permute-start | bytes 294920 | tf_op jit(solution)/shard_map/ppermute | solution.py:23
  44.0 4.6 %collective-permute-start.13 = (f32[3,4,16,128]{3,2,1,0:T(8,128)S(1)}, f32[3,4,16,128]{3,2,1,0:T(8,128)S(1)}, u32[]{:S(2)}, u32[]{:S(2)}) collective-permute-start(f32[3,4,16,128]{3,2,1,0:T(8,128)S(1)} %add.11), channel_id=1, source_target_pairs={{0,2},{1,3},{2,0},{3,1},{4,6},{5,7},{6,4},{7,5},{8,10},{9,11},{10,... | collective-permute-start | bytes 294920 | tf_op jit(solution)/shard_map/ppermute | solution.py:23
  49.8 4.4 %collective-permute-start.19 = (f32[4,16,128]{2,1,0:T(8,128)S(1)}, f32[4,16,128]{2,1,0:T(8,128)S(1)}, u32[]{:S(2)}, u32[]{:S(2)}) collective-permute-start(f32[4,16,128]{2,1,0:T(8,128)S(1)} %new_currents.5.refs_8_), channel_id=1, source_target_pairs={{0,8},{8,0},{16,24},{24,16},{1,9},{9,1},{17,25},{25,17},{2,10},{10... | collective-permute-start | bytes 98312 | tf_op jit(solution)/shard_map/ppermute | solution.py:23
  50.8 4.8 %collective-permute-start.20 = (f32[4,16,128]{2,1,0:T(8,128)S(1)}, f32[4,16,128]{2,1,0:T(8,128)S(1)}, u32[]{:S(2)}, u32[]{:S(2)}) collective-permute-start(f32[4,16,128]{2,1,0:T(8,128)S(1)} %new_currents.5.refs_8_), channel_id=1, source_target_pairs={{0,16},{8,24},{16,0},{24,8},{1,17},{9,25},{17,1},{25,9},{2,18},{10... | collective-permute-start | bytes 98312 | tf_op jit(solution)/shard_map/ppermute | solution.py:23
  53.4 6.0 %collective-permute-start.21 = (f32[4,16,128]{2,1,0:T(8,128)S(1)}, f32[4,16,128]{2,1,0:T(8,128)S(1)}, u32[]{:S(2)}, u32[]{:S(2)}) collective-permute-start(f32[4,16,128]{2,1,0:T(8,128)S(1)} %new_currents.5.refs_8_), channel_id=1, source_target_pairs={{0,24},{8,16},{16,8},{24,0},{1,25},{9,17},{17,9},{25,1},{2,26},{10... | collective-permute-start | bytes 98312 | tf_op jit(solution)/shard_map/ppermute | solution.py:23
  60.5 4.4 %collective-permute-start.22 = (f32[4,16,128]{2,1,0:T(8,128)S(1)}, f32[4,16,128]{2,1,0:T(8,128)S(1)}, u32[]{:S(2)}, u32[]{:S(2)}) collective-permute-start(f32[4,16,128]{2,1,0:T(8,128)S(1)} %new_currents.6.refs_12_), channel_id=1, source_target_pairs={{0,8},{8,0},{16,24},{24,16},{1,9},{9,1},{17,25},{25,17},{2,10},{10... | collective-permute-start | bytes 98312 | tf_op jit(solution)/shard_map/ppermute | solution.py:23
  60.5 4.9 %collective-permute-start.23 = (f32[4,16,128]{2,1,0:T(8,128)S(1)}, f32[4,16,128]{2,1,0:T(8,128)S(1)}, u32[]{:S(2)}, u32[]{:S(2)}) collective-permute-start(f32[4,16,128]{2,1,0:T(8,128)S(1)} %new_currents.6.refs_12_), channel_id=1, source_target_pairs={{0,16},{8,24},{16,0},{24,8},{1,17},{9,25},{17,1},{25,9},{2,18},{10... | collective-permute-start | bytes 98312 | tf_op jit(solution)/shard_map/ppermute | solution.py:23
  62.5 5.7 %collective-permute-start.24 = (f32[4,16,128]{2,1,0:T(8,128)S(1)}, f32[4,16,128]{2,1,0:T(8,128)S(1)}, u32[]{:S(2)}, u32[]{:S(2)}) collective-permute-start(f32[4,16,128]{2,1,0:T(8,128)S(1)} %new_currents.6.refs_12_), channel_id=1, source_target_pairs={{0,24},{8,16},{16,8},{24,0},{1,25},{9,17},{17,9},{25,1},{2,26},{10... | collective-permute-start | bytes 98312 | tf_op jit(solution)/shard_map/ppermute | solution.py:23
  69.6 4.7 %collective-permute-start.25 = (f32[3,4,16,128]{3,2,1,0:T(8,128)S(1)}, f32[3,4,16,128]{3,2,1,0:T(8,128)S(1)}, u32[]{:S(2)}, u32[]{:S(2)}) collective-permute-start(f32[3,4,16,128]{3,2,1,0:T(8,128)S(1)} %pad_maximum_fusion.1), channel_id=1, source_target_pairs={{0,4},{1,5},{2,6},{3,7},{4,0},{5,1},{6,2},{7,3},{8,12},{9,13},{10,... | collective-permute-start | bytes 294920 | tf_op jit(solution)/shard_map/ppermute | solution.py:23
  74.3 4.7 %collective-permute-start.26 = (f32[3,4,16,128]{3,2,1,0:T(8,128)S(1)}, f32[3,4,16,128]{3,2,1,0:T(8,128)S(1)}, u32[]{:S(2)}, u32[]{:S(2)}) collective-permute-start(f32[3,4,16,128]{3,2,1,0:T(8,128)S(1)} %broadcast_select_fusion), channel_id=1, source_target_pairs={{0,2},{1,3},{2,0},{3,1},{4,6},{5,7},{6,4},{7,5},{8,10},{9,11},{10,... | collective-permute-start | bytes 294920 | tf_op jit(solution)/shard_map/ppermute | solution.py:23
  79.0 1.4 %collective-permute-start.27 = (f32[3,4,16,128]{3,2,1,0:T(8,128)S(1)}, f32[3,4,16,128]{3,2,1,0:T(8,128)S(1)}, u32[]{:S(2)}, u32[]{:S(2)}) collective-permute-start(f32[3,4,16,128]{3,2,1,0:T(8,128)S(1)} %broadcast_select_fusion.1), channel_id=1, source_target_pairs={{0,1},{1,0},{2,3},{3,2},{4,5},{5,4},{6,7},{7,6},{8,9},{9,8},{10,11... | collective-permute-start | bytes 294920 | tf_op jit(solution)/shard_map/ppermute | solution.py:23

commit v2 on v0

v2 whole, which is shorter than its diff:
```python
import functools

import jax
import jax.numpy as jnp
from jax import lax
from jax.experimental import pallas as pl
from jax.experimental.pallas import tpu as pltpu
from jax.sharding import PartitionSpec as P

F32 = jnp.float32
BF16 = jnp.bfloat16
VMEM = pltpu.VMEM
SMEM = pltpu.SMEM
UNROLL = 16


def whole(space):
    return pl.BlockSpec(memory_space=space)


def swap(x, axis, bits):
    n = lax.axis_size(axis)
    return lax.ppermute(x, axis, [(i, i ^ bits) for i in range(n)])


def halves(x):
    high = x.astype(BF16)
    low = (x - high.astype(F32)).astype(BF16)
    return high, low


def wide(x):
    high, low = halves(x)
    return jnp.concatenate([high, low], axis=-1)


def times(rows, weights):
    both = jnp.concatenate([rows, rows], axis=-1)
    return lax.dot_general(both, weights, (((1,), (1,)), ((), ())), preferred_element_type=F32)


def room(pairs):
    return (pairs + UNROLL - 1) // UNROLL * UNROLL + UNROLL


def plan_kernel(groups, group_blocks, steps, me, band, pattern, live, slots, past, newer, held, count):
    places = slots.shape[0]
    size = room(pattern.shape[1])
    cells = places * group_blocks
    for d in range(places):
        held[d] = sum(jnp.where(slots[j] == d, j, 0) for j in range(places))
        count[d] = 0
    wide_entry, late_entry, late_start = 2 + steps, 1 + steps, 3 + 2 * size * (2 + steps)

    def place(e, near):
        row, column, d = pattern[0, e], pattern[1, e], pattern[2, e]
        group = (column // group_blocks) ^ me[0]
        block = column % group_blocks
        is_far = (group >= 2).astype(jnp.int32)
        to = 3 + (is_far * size + jnp.where(is_far == 1, e - near, near)) * wide_entry
        past[to] = e
        past[to + 1] = row
        for t in range(steps):
            at = ((group - 2 * is_far) * places + held[jnp.maximum(d - t, 0)]) * group_blocks + block
            nothing = jnp.where(is_far == 1, (groups - 2) * cells, 2 * cells)
            past[to + 2 + t] = jnp.where(d >= t, at, nothing)
        to = late_start + e * late_entry
        past[to] = e
        past[to + 1] = row
        for t in range(1, steps):
            at = (group * places + d - t + places) * group_blocks + block
            past[to + 1 + t] = jnp.where(d < t, at, groups * cells)
        n = count[d]
        count[d] = n + 1
        to = places + (d * size + n) * 3
        newer[to] = e
        newer[to + 1] = row
        newer[to + 2] = group * group_blocks + block
        return near + 1 - is_far

    near = lax.fori_loop(0, live[0], place, jnp.int32(0))
    far = live[0] - near
    past[0] = near
    past[1] = far
    past[2] = jnp.where(band[0] == 0, 0, live[0])

    def fill(i, c):
        for k, n, nothing in ((0, near, 2 * cells), (1, far, (groups - 2) * cells)):
            to = 3 + (k * size + n + i) * wide_entry
            past[to] = 0
            past[to + 1] = 0
            for t in range(steps):
                past[to + 2 + t] = nothing
        to = late_start + (live[0] + i) * late_entry
        past[to] = 0
        past[to + 1] = 0
        for t in range(1, steps):
            past[to + 1 + t] = groups * cells
        for d in range(places):
            to = places + (d * size + count[d] + i) * 3
            newer[to] = 0
            newer[to + 1] = 0
            newer[to + 2] = groups * group_blocks
        return c

    lax.fori_loop(0, UNROLL, fill, 0)
    for d in range(places):
        newer[d] = jnp.where(band[0] == 0, count[d], 0)


def make_plan(groups, group_blocks, steps, me, band, pattern, live, slots):
    places = slots.shape[0]
    size = room(pattern.shape[1])
    return pl.pallas_call(
        functools.partial(plan_kernel, groups, group_blocks, steps),
        in_specs=[whole(SMEM)] * 5,
        out_specs=[whole(SMEM)] * 2,
        out_shape=[
            jax.ShapeDtypeStruct((3 + size * (2 * (2 + steps) + 1 + steps),), jnp.int32),
            jax.ShapeDtypeStruct((places + places * size * 3,), jnp.int32),
        ],
        scratch_shapes=[SMEM((places,), jnp.int32), SMEM((places,), jnp.int32)],
        name="make_plan",
    )(me, band, pattern, live, slots)


def split_kernel(blocks, inverse, wide_blocks, wide_inverse, held, held_inverse, sems):
    chunks = sems.shape[0] - 1
    per = blocks.shape[0] // chunks
    copies = [
        pltpu.make_async_copy(blocks.at[pl.ds(k * per, per)], held.at[pl.ds(k * per, per)], sems.at[k])
        for k in range(chunks)
    ]
    copies.append(pltpu.make_async_copy(inverse, held_inverse, sems.at[chunks]))
    for c in copies:
        c.start()
    for k in range(chunks):
        copies[k].wait()

        def split(e, c):
            wide_blocks[e] = wide(held[e])
            return c

        lax.fori_loop(k * per, (k + 1) * per, split, 0, unroll=4)
    copies[chunks].wait()
    wide_inverse[...] = wide(held_inverse[...])


def split_blocks(blocks, inverse):
    pairs, a, q = blocks.shape
    chunks = 4 if pairs % 4 == 0 else 1
    return pl.pallas_call(
        split_kernel,
        in_specs=[whole(pltpu.HBM)] * 2,
        out_specs=[whole(VMEM)] * 2,
        out_shape=[
            jax.ShapeDtypeStruct((pairs, a, 2 * q), BF16),
            jax.ShapeDtypeStruct((inverse.shape[0], a, 2 * q), BF16),
        ],
        scratch_shapes=[VMEM(blocks.shape, F32), VMEM(inverse.shape, F32), pltpu.SemaphoreType.DMA((chunks + 1,))],
        compiler_params=pltpu.CompilerParams(vmem_limit_bytes=16 << 20),
        cost_estimate=pl.CostEstimate(flops=8 * pairs * a * q, bytes_accessed=8 * pairs * a * q, transcendentals=0),
        name="split_blocks",
    )(blocks, inverse)


def pack(packed, start, x):
    high, low = halves(x)
    packed[pl.ds(start, x.shape[0])] = jnp.concatenate([high, low], axis=1)


def batches(plan, start, entry, amount, packed, blocks, add):
    def batch(i, carry):
        made = []
        for u in range(UNROLL):
            at = start + (i * UNROLL + u) * entry
            rows = [packed[plan[at + 2 + t]] for t in range(entry - 2)]
            made.append((plan[at + 1], times(jnp.concatenate(rows, axis=0), blocks[plan[at]])))
        for row, y in made:
            y = y.reshape(entry - 2, 2, packed.shape[1] // 2, y.shape[-1])
            add(row, y[:, 0] + y[:, 1])
        return carry

    lax.fori_loop(0, (amount + UNROLL - 1) // UNROLL, batch, 0)


def past_kernel(when, plan, *refs):
    if when == "near":
        blocks, *parts, out, packed = refs
        out[...] = jnp.zeros_like(out)
    elif when == "far":
        blocks, base, *parts, out, now, packed = refs
        out[...] = base[...]
    else:
        slots, blocks, base, *parts, out, packed = refs
        out[...] = base[1:]
    places, group_blocks, columns, width = parts[0].shape
    cells = places * group_blocks
    for k in range(len(parts)):
        if when == "late":
            for j in range(places):
                pack(packed, (k * places + slots[j]) * group_blocks, parts[k][j])
        else:
            pack(packed, k * cells, parts[k][...].reshape(cells, columns, width))
    packed[len(parts) * cells] = jnp.zeros((2 * columns, width), BF16)
    size = room(blocks.shape[0])
    which = ("near", "far", "late").index(when)
    entry = 2 + out.shape[0]
    start = 3 + which * size * (entry + which // 2)

    def add(row, y):
        out[:, row] += y

    batches(plan, start, entry, plan[which], packed, blocks, add)
    if when == "far":
        now[...] = out[0]


def past_field(when, steps, plan, blocks, parts, base=None, slots=None):
    places, group_blocks, columns, width = parts[0].shape
    shape = (group_blocks, columns, width)
    packed = VMEM((len(parts) * places * group_blocks + 1, 2 * columns, width), BF16)
    out = [jax.ShapeDtypeStruct((steps - (when == "late"),) + shape, F32)]
    if when == "far":
        out.append(jax.ShapeDtypeStruct(shape, F32))
    scalars = [plan] + [slots] * (when == "late")
    given = [blocks] + [base] * (when != "near")
    return pl.pallas_call(
        functools.partial(past_kernel, when),
        in_specs=[whole(SMEM)] * len(scalars) + [whole(VMEM)] * (len(given) + len(parts)),
        out_specs=[whole(VMEM)] * len(out),
        out_shape=out,
        scratch_shapes=[packed],
        compiler_params=pltpu.CompilerParams(vmem_limit_bytes=16 << 20),
        name=when + "_field",
    )(*scalars, *given, *parts)


def solve(inverse, right, out):
    for i in range(out.shape[0]):
        high, low = halves(right[i])
        y = times(jnp.concatenate([high, low], axis=0), inverse[i]).reshape((2,) + out.shape[1:])
        out[i] = y[0] + y[1]


def summed(refs, t):
    total = refs[0][t]
    for r in refs[1:]:
        total = total + r[t]
    return total


def first_kernel(inverse, incident, *refs):
    *terms, out, right = refs
    right[...] = incident[0] - summed(terms, ...)
    solve(inverse, right, out)


def first_currents(inverse, incident, terms):
    shape = incident.shape[1:]
    return pl.pallas_call(
        first_kernel,
        in_specs=[whole(VMEM)] * (2 + len(terms)),
        out_specs=whole(VMEM),
        out_shape=jax.ShapeDtypeStruct(shape, F32),
        scratch_shapes=[VMEM(shape, F32)],
        compiler_params=pltpu.CompilerParams(vmem_limit_bytes=16 << 20),
        name="first_currents",
    )(inverse, incident, *terms)


def recent(kind, plan, places, packed, blocks, add):
    start = places + kind * room(blocks.shape[0]) * 3
    batches(plan, start, 3, plan[kind], packed, blocks, lambda row, y: add(row, y[0]))


def right_side(rights, t):
    if len(rights) == 1:
        return rights[0][t]
    return rights[0][t + 1] - summed(rights[1:], t)


def step_kernel(places, count, plan, blocks, inverse, *refs):
    rights, parts, (out, packed, right) = refs[:count], refs[count:-3], refs[-3:]
    group_blocks, columns, width = out.shape
    for k in range(len(parts)):
        pack(packed, k * group_blocks, parts[k][...])
    packed[len(parts) * group_blocks] = jnp.zeros((2 * columns, width), BF16)
    right[...] = right_side(rights, 0)

    def add(row, y):
        right[row] -= y

    recent(0, plan, places, packed, blocks, add)
    solve(inverse, right, out)


def next_currents(places, plan, blocks, inverse, rights, parts):
    shape = parts[0].shape
    packed = (len(parts) * shape[0] + 1, 2 * shape[1], shape[2])
    return pl.pallas_call(
        functools.partial(step_kernel, places, len(rights)),
        in_specs=[whole(SMEM)] + [whole(VMEM)] * (2 + len(rights) + len(parts)),
        out_specs=[whole(VMEM)] * 2,
        out_shape=[jax.ShapeDtypeStruct(shape, F32), jax.ShapeDtypeStruct(packed, BF16)],
        scratch_shapes=[VMEM(shape, F32)],
        compiler_params=pltpu.CompilerParams(vmem_limit_bytes=16 << 20),
        name="next_currents",
    )(plan, blocks, inverse, *rights, *parts)


def older_kernel(places, plan, blocks, packed, newest, *refs):
    *rights, out, passed = refs
    passed[...] = newest[...]
    for t in range(out.shape[0]):
        out[t] = right_side(rights, t + 1)

        def add(row, y):
            out[t, row] -= y

        recent(t + 1, plan, places, packed, blocks, add)


def older_field(places, steps, plan, blocks, packed, newest, rights):
    return pl.pallas_call(
        functools.partial(older_kernel, places),
        in_specs=[whole(SMEM)] + [whole(VMEM)] * (3 + len(rights)),
        out_specs=[whole(VMEM)] * 2,
        out_shape=[jax.ShapeDtypeStruct((steps,) + newest.shape, F32), jax.ShapeDtypeStruct(newest.shape, F32)],
        compiler_params=pltpu.CompilerParams(vmem_limit_bytes=16 << 20),
        name="older_field",
    )(plan, blocks, packed, newest, *rights)


def summands(x):
    bands = lax.axis_size("delay")
    if bands <= 8:
        return [x] + [swap(x, "delay", k) for k in range(2, bands, 2)]
    return [doubled(x)]


def front_summands(x):
    bands = lax.axis_size("delay")
    if bands > 8:
        return [doubled(x)]
    terms = [x]
    for c in range(bands - 2, 0, -2):
        goes = {i: i ^ 1 for i in range(bands)} | {c: 0, 0: 1, 1: c + 1, c + 1: c}
        terms.append(lax.ppermute(x, "delay", list(goes.items())))
    return terms


def doubled(x):
    bit = 2
    while bit < lax.axis_size("delay"):
        x = x + swap(x, "delay", bit)
        bit *= 2
    return x


def from_front(x):
    bands = lax.axis_size("delay")
    mine = lax.axis_index("delay")
    bit = bands // 2
    while bit > 1:
        goes = {i: i ^ 1 for i in range(bands)}
        for i in range(0, bands, 2 * bit):
            goes |= {i: i + bit, i + bit: i + bit + 1, i + bit + 1: i + 1, i + 1: i}
        other = lax.ppermute(x, "delay", list(goes.items()))
        x = jnp.where((mine & (2 * bit - 1)) == bit, other, x)
        bit //= 2
    return x


def from_even(x):
    return jnp.where((lax.axis_index("delay") & 1) != 0, swap(x, "delay", 1), x)


def body(history, slot_map, interaction, pattern, live, near_inverse, incident):
    slot_count = history.shape[0]
    moments = incident.shape[0]
    groups = lax.axis_size("src")
    bands = lax.axis_size("delay")
    assert moments - 1 <= slot_count and moments % 2 == 0
    assert groups & (groups - 1) == 0 and bands & (bands - 1) == 0
    me = lax.axis_index("src").reshape(1)
    band = lax.axis_index("delay").reshape(1)

    def front_over_src(x):
        pairs = [[(i * bands + j, (i ^ k) * bands if j == 0 else i * bands + j % (bands - 1) + 1)
                  for i in range(groups) for j in range(bands)] for k in range(1, groups)]
        return [x] + [lax.ppermute(x, ("src", "delay"), p) for p in pairs]

    parts = [history] + [swap(history, "src", k) for k in range(1, groups)]
    ring = [(i, (i + 1) % bands) for i in range(bands)]
    slots_before = lax.ppermute(slot_map, "delay", ring)
    blocks, inverse = split_blocks(interaction, near_inverse)
    past, newer = make_plan(groups, history.shape[1], moments, me, band, pattern, live, slot_map)
    parts[1], slots_before, past, newer, blocks, inverse = lax.optimization_barrier(
        (parts[1], slots_before, past, newer, blocks, inverse)
    )
    (field,) = past_field("near", moments, past, blocks, parts[:2])
    field, parts[2:] = lax.optimization_barrier((field, parts[2:]))
    before = [lax.ppermute(p, "delay", ring) for p in parts]
    field, now = past_field("far", moments, past, blocks, parts[2:], field)
    now = now + swap(now, "delay", 1)
    now, field = lax.optimization_barrier((now, field))
    (later,) = past_field("late", moments, past, blocks, before, field, slots_before)

    newest = first_currents(inverse, incident, summands(now))
    results = [newest]
    rights = None
    for moment in range(1, moments):
        shared = front_over_src(newest)
        if moment == 1:
            rights = [incident] + front_summands(later + swap(later, "delay", 1))
        else:
            rights, newest = older_field(slot_count, moments - moment, newer, blocks, packed, newest, rights)
            rights = [rights]
            results.append(from_even(from_front(newest)))
        newest, packed = next_currents(slot_count, newer, blocks, inverse, rights, shared)
    results.append(from_even(from_front(newest)))
    return jnp.stack(results)


def solution(mesh):
    return jax.shard_map(
        body,
        mesh=mesh,
        in_specs=(
            P("delay", "src", None, None),
            P("delay"),
            P(("src", "delay"), None, None),
            P(None, ("src", "delay")),
            P(("src", "delay")),
            P("src", None, None),
            P(None, "src", None, None),
        ),
        out_specs=P(None, "src", None, None),
        check_vma=False,
    )
```

time: 218 us -> 71.2 us (0.33)
  blocking collectives: 153 us -> 0 us
  starting transfers between devices: 4.66 us -> 38.2 us
  matrix products: 29.4 us -> 0 us
  Pallas kernels: 0 us -> 14.6 us
  local copies, waits for them, and re-layouts: 16.2 us -> 2.85 us
  waiting for transfers between devices: 0.01 us -> 12.6 us
  between operations: 6.33 us -> 0.87 us
  other arithmetic: 5.83 us -> 1.5 us
    psum x4 -> x0, blocking collectives: 93.2 us -> none  [body(): field_sum = lax.psum(partial_field, 'delay')]
    all_gather x4 -> x0, blocking collectives: 60 us -> none  [the longest x3 40.5 us: body(): newest = lax.all_gather(current, 'src', axis=0, tiled=True)]
    ppermute x3 -> x34, starting transfers between devices: 4.66 us -> 38.2 us  [the longest x9 16.5 us: front_over_src(): return [x] + [lax.ppermute(x, ('src', 'delay'), p) for p in pairs]]
    dot_general x12 -> x0, matrix products: 29.4 us -> none  [the longest x4 23.8 us: body(): jnp.einsum('pab,prb->pra', interaction, picked, precision=lax.Precision.H...]
    pallas_call x0 -> x11, Pallas kernels: none -> 14.6 us  [the longest x3 4.47 us: next_currents(): pl.pallas_call(functools.partial(step_kernel, places, len(rights)), in_sp...]
    ppermute x3 -> x34, waiting for transfers between devices: 0.01 us -> 12.6 us  [the longest x9 5.98 us: front_over_src(): return [x] + [lax.ppermute(x, ('src', 'delay'), p) for p in pairs]]
    gather x4 -> x0, local copies, waits for them, and re-layouts: 10.6 us -> none  [body(): picked = band_state[holder, pattern[1]]]
    squeeze x3 -> x0, local copies, waits for them, and re-layouts: 3.4 us -> none  [body(): lax.dynamic_index_in_dim(band_state, vacated, 0, keepdims=False)]
  transfers between devices with their start and end apart: 3 -> 34, of which waited for: 0 -> 11; matrix products, arithmetic and copies ran while one was open for 6% -> 1% of each run, Pallas kernels for 0% -> 18%
where the time goes in v2:
time: 71.2 us; the launch traced here: 70.6 us
  starting transfers between devices  38.2 us (54%)
  Pallas kernels  14.6 us (21%)
  waiting for transfers between devices  12.6 us (18%)
  local copies, waits for them, and re-layouts  2.85 us (4%)
  other arithmetic  1.5 us (2%)
  between operations  0.87 us (1%)
    ppermute x9, starting transfers between devices, front_over_src(): return [x] + [lax.ppermute(x, ('src', 'delay'), p) for p in pairs]  16.5 us
    ppermute x11, starting transfers between devices, swap(): return lax.ppermute(x, axis, [(i, i ^ bits) for i in range(n)])  12.7 us
    ppermute x9, waiting for transfers between devices, front_over_src(): return [x] + [lax.ppermute(x, ('src', 'delay'), p) for p in pairs]  5.98 us
    pallas_call x3, Pallas kernels, next_currents(): pl.pallas_call(functools.partial(step_kernel, places, len(rights)), in_sp...  4.47 us
    pallas_call x3, Pallas kernels, past_field(): pl.pallas_call(functools.partial(past_kernel, when), in_specs=[whole(SMEM...  3.54 us
    ppermute x11, waiting for transfers between devices, swap(): return lax.ppermute(x, axis, [(i, i ^ bits) for i in range(n)])  3.53 us
    pallas_call x2, Pallas kernels, older_field(): pl.pallas_call(functools.partial(older_kernel, places), in_specs=[whole(S...  3.22 us
    unnamed x12, local copies, waits for them, and re-layouts  2.85 us
  transfers between devices with their start and end apart: 34, of which 11 were waited for; matrix products, arithmetic and copies ran while one was open for 1% of the time, Pallas kernels for 18%

profile of v2, /device:TPU:0, one launch (start us, length us, event | category | flops | bytes accessed | tf_op | source)
XLA Modules:
  0.0 70.6 jit_solution(9396148743459240126)
XLA Ops:
  0.0 3.0 %collective-permute-start = (f32[4,4,16,128]{3,2,1,0:T(8,128)}, f32[4,4,16,128]{3,2,1,0:T(8,128)S(1)}, u32[]{:S(2)}, u32[]{:S(2)}) collective-permute-start(f32[4,4,16,128]{3,2,1,0:T(8,128)} %refs_1_.1), channel_id=1, source_target_pairs={{0,8},{8,0},{16,24},{24,16},{1,9},{9,1},{17,25},{25,17},{2,10},{10... | collective-permute-start | bytes 393224 | tf_op jit(solution)/shard_map/ppermute | solution.py:23
  3.0 2.6 %collective-permute-start.2 = (f32[4,4,16,128]{3,2,1,0:T(8,128)}, f32[4,4,16,128]{3,2,1,0:T(8,128)}, u32[]{:S(2)}, u32[]{:S(2)}) collective-permute-start(f32[4,4,16,128]{3,2,1,0:T(8,128)} %refs_1_.1), channel_id=1, source_target_pairs={{0,16},{8,24},{16,0},{24,8},{1,17},{9,25},{17,1},{25,9},{2,18},{10... | collective-permute-start | bytes 393224 | tf_op jit(solution)/shard_map/ppermute | solution.py:23
  5.6 1.8 %collective-permute-start.1 = (s32[4]{0:T(128)}, s32[4]{0:T(128)S(1)}, u32[]{:S(2)}, u32[]{:S(2)}) collective-permute-start(s32[4]{0:T(128)} %slots.1), channel_id=1, source_target_pairs={{0,1},{1,2},{2,3},{3,4},{4,5},{5,6},{6,7},{7,0},{8,9},{9,10},{10,1... | collective-permute-start | bytes 56 | tf_op jit(solution)/shard_map/ppermute | solution.py:396
  8.1 2.5 %make_plan.1 = (s32[1091]{0:T(1024)}, s32[772]{0:T(1024)}) custom-call(s32[1]{0:T(128)} %bitcast.me, s32[1]{0:T(128)} %bitcast.1.band, s32[3,48]{1,0:T(4,128)} %pattern.1, s32[1]{0:T(128)S(6)} %copy.8.live, s32[4]{0:T(128)} %slots.1), custom_call_target="tpu_custom_call" | custom-call | tf_op jit(solution)/shard_map/make_plan/pallas_call | solution.py:114
  10.6 1.9 %copy-done = f32[48,128,128]{2,1,0:T(8,128)S(1)} copy-done((f32[48,128,128]{2,1,0:T(8,128)S(1)}, f32[48,128,128]{2,1,0:T(8,128)}, u32[]{:S(2)}) %copy-start) | copy-done | bytes 3145752
  12.5 0.9 %copy-done.2 = f32[4,128,128]{2,1,0:T(8,128)S(1)} copy-done((f32[4,128,128]{2,1,0:T(8,128)S(1)}, f32[4,128,128]{2,1,0:T(8,128)}, u32[]{:S(2)}) %copy-start.2) | copy-done | bytes 262168
  13.4 0.7 %split_blocks.1 = (bf16[48,128,256]{2,1,0:T(8,128)(2,1)S(1)}, bf16[4,128,256]{2,1,0:T(8,128)(2,1)S(1)}) custom-call(f32[48,128,128]{2,1,0:T(8,128)S(1)} %copy-done, f32[4,128,128]{2,1,0:T(8,128)S(1)} %copy-done.2), custom_call_target="tpu_custom_call" | custom-call | flops 6291456 | bytes 6291456 | tf_op jit(solution)/shard_map/split_blocks/pallas_call | solution.py:152
  14.2 0.6 collective-permute-start.9
  14.8 1.1 %near_field.1.refs_1_ = f32[4,4,16,128]{3,2,1,0:T(8,128)S(1)} custom-call(s32[1091]{0:T(1024)S(1)} %copy-done.5, bf16[48,128,256]{2,1,0:T(8,128)(2,1)S(1)} %get-tuple-element.37.refs_0_.refs_1_.blocks, f32[4,4,16,128]{3,2,1,0:T(8,128)S(1)} %copy-done.3, f32[4,4,16,128]{3,2,1,0:T(8,128)S(1)} %collective-permute-done.refs_2_), custom_call_target="tpu_custom_call" | custom-call | tf_op jit(solution)/shard_map/near_field/pallas_call | solution.py:228
  16.0 0.3 collective-permute-done.2.refs_2_
  16.3 1.7 %collective-permute-start.10 = (f32[4,4,16,128]{3,2,1,0:T(8,128)}, f32[4,4,16,128]{3,2,1,0:T(8,128)S(1)}, u32[]{:S(2)}, u32[]{:S(2)}) collective-permute-start(f32[4,4,16,128]{3,2,1,0:T(8,128)} %collective-permute-done.2.refs_2_), channel_id=1, source_target_pairs={{0,1},{1,2},{2,3},{3,4},{4,5},{5,6},{6,7},{7,0},{8,9},{9,10},{10,1... | collective-permute-start | bytes 393224 | tf_op jit(solution)/shard_map/ppermute | solution.py:404
  17.9 0.4 collective-permute-start.11
  18.3 1.5 %far_field.1 = (f32[4,4,16,128]{3,2,1,0:T(8,128)S(1)}, f32[4,16,128]{2,1,0:T(8,128)S(1)}) custom-call(s32[1091]{0:T(1024)S(1)} %copy-done.5, bf16[48,128,256]{2,1,0:T(8,128)(2,1)S(1)} %get-tuple-element.37.refs_0_.refs_1_.blocks, f32[4,4,16,128]{3,2,1,0:T(8,128)S(1)} %near_field.1.refs_1_, f32[4,4,16,128]{3,2,1,0:T(8,128)} %collective-permute-done.2.refs_2_, ...), custom_call_target="tpu_custom_call" | custom-call | tf_op jit(solution)/shard_map/far_field/pallas_call | solution.py:228
  19.8 1.1 %collective-permute-start.4 = (f32[4,16,128]{2,1,0:T(8,128)S(1)}, f32[4,16,128]{2,1,0:T(8,128)S(1)}, u32[]{:S(2)}, u32[]{:S(2)}) collective-permute-start(f32[4,16,128]{2,1,0:T(8,128)S(1)} %get-tuple-element.42), channel_id=1, source_target_pairs={{0,1},{1,0},{2,3},{3,2},{4,5},{5,4},{6,7},{7,6},{8,9},{9,8},{10,11... | collective-permute-start | bytes 98312 | tf_op jit(solution)/shard_map/ppermute | solution.py:23
  20.9 0.9 %collective-permute-done.4 = f32[4,16,128]{2,1,0:T(8,128)S(1)} collective-permute-done((f32[4,16,128]{2,1,0:T(8,128)S(1)}, f32[4,16,128]{2,1,0:T(8,128)S(1)}, u32[]{:S(2)}, u32[]{:S(2)}) %collective-permute-start.4) | collective-permute-done | bytes 32800 | tf_op jit(solution)/shard_map/ppermute | solution.py:23
  21.8 1.6 %collective-permute-done.11.refs_6_ = f32[4,4,16,128]{3,2,1,0:T(8,128)S(1)} collective-permute-done((f32[4,4,16,128]{3,2,1,0:T(8,128)}, f32[4,4,16,128]{3,2,1,0:T(8,128)S(1)}, u32[]{:S(2)}, u32[]{:S(2)}) %collective-permute-start.11) | collective-permute-done | bytes 131104 | tf_op jit(solution)/shard_map/ppermute | solution.py:404
  23.5 1.0 %late_field.1 = f32[3,4,16,128]{3,2,1,0:T(8,128)S(1)} custom-call(s32[1091]{0:T(1024)S(1)} %copy-done.5, s32[4]{0:T(128)S(1)} %collective-permute-done.1.refs_0_, bf16[48,128,256]{2,1,0:T(8,128)(2,1)S(1)} %get-tuple-element.37.refs_0_.refs_1_.blocks, f32[4,4,16,128]{3,2,1,0:T(8,128)S(1)} %get-tuple-element.47.refs_2_, ...), custom_call_target="tpu_custom_call" | custom-call | tf_op jit(solution)/shard_map/late_field/pallas_call | solution.py:228
  24.5 2.3 %collective-permute-start.5 = (f32[4,16,128]{2,1,0:T(8,128)S(1)}, f32[4,16,128]{2,1,0:T(8,128)S(1)}, u32[]{:S(2)}, u32[]{:S(2)}) collective-permute-start(f32[4,16,128]{2,1,0:T(8,128)S(1)} %add.6.refs_0_), channel_id=1, source_target_pairs={{0,2},{1,3},{2,0},{3,1},{4,6},{5,7},{6,4},{7,5},{8,10},{9,11},{10,... | collective-permute-start | bytes 98312 | tf_op jit(solution)/shard_map/ppermute | solution.py:23
  26.8 1.1 %collective-permute-start.6 = (f32[4,16,128]{2,1,0:T(8,128)S(1)}, f32[4,16,128]{2,1,0:T(8,128)S(1)}, u32[]{:S(2)}, u32[]{:S(2)}) collective-permute-start(f32[4,16,128]{2,1,0:T(8,128)S(1)} %add.6.refs_0_), channel_id=1, source_target_pairs={{0,4},{1,5},{2,6},{3,7},{4,0},{5,1},{6,2},{7,3},{8,12},{9,13},{10,... | collective-permute-start | bytes 98312 | tf_op jit(solution)/shard_map/ppermute | solution.py:23
  27.9 1.0 %collective-permute-start.7 = (f32[4,16,128]{2,1,0:T(8,128)S(1)}, f32[4,16,128]{2,1,0:T(8,128)S(1)}, u32[]{:S(2)}, u32[]{:S(2)}) collective-permute-start(f32[4,16,128]{2,1,0:T(8,128)S(1)} %add.6.refs_0_), channel_id=1, source_target_pairs={{0,6},{1,7},{2,4},{3,5},{4,2},{5,3},{6,0},{7,1},{8,14},{9,15},{10,... | collective-permute-start | bytes 98312 | tf_op jit(solution)/shard_map/ppermute | solution.py:23
  28.9 1.2 %collective-permute-start.14 = (f32[3,4,16,128]{3,2,1,0:T(8,128)S(1)}, f32[3,4,16,128]{3,2,1,0:T(8,128)S(1)}, u32[]{:S(2)}, u32[]{:S(2)}) collective-permute-start(f32[3,4,16,128]{3,2,1,0:T(8,128)S(1)} %add.7.refs_1_), channel_id=1, source_target_pairs={{0,1},{1,5},{2,3},{3,2},{4,0},{5,4},{6,7},{7,6},{8,9},{9,13},{10,1... | collective-permute-start | bytes 294920 | tf_op jit(solution)/shard_map/ppermute | solution.py:349
  30.2 1.0 %collective-permute-start.15 = (f32[3,4,16,128]{3,2,1,0:T(8,128)S(1)}, f32[3,4,16,128]{3,2,1,0:T(8,128)S(1)}, u32[]{:S(2)}, u32[]{:S(2)}) collective-permute-start(f32[3,4,16,128]{3,2,1,0:T(8,128)S(1)} %add.7.refs_1_), channel_id=1, source_target_pairs={{0,1},{1,3},{2,0},{3,2},{4,5},{5,4},{6,7},{7,6},{8,9},{9,11},{10,8... | collective-permute-start | bytes 294920 | tf_op jit(solution)/shard_map/ppermute | solution.py:349
  31.2 1.5 %collective-permute-done.7.refs_3_ = f32[4,16,128]{2,1,0:T(8,128)S(1)} collective-permute-done((f32[4,16,128]{2,1,0:T(8,128)S(1)}, f32[4,16,128]{2,1,0:T(8,128)S(1)}, u32[]{:S(2)}, u32[]{:S(2)}) %collective-permute-start.7) | collective-permute-done | bytes 32800 | tf_op jit(solution)/shard_map/ppermute | solution.py:23
  32.9 1.5 %collective-permute-start.16 = (f32[4,16,128]{2,1,0:T(8,128)S(1)}, f32[4,16,128]{2,1,0:T(8,128)S(1)}, u32[]{:S(2)}, u32[]{:S(2)}) collective-permute-start(f32[4,16,128]{2,1,0:T(8,128)S(1)} %first_currents.1.refs_5_), channel_id=1, source_target_pairs={{0,8},{1,2},{2,3},{3,4},{4,5},{5,6},{6,7},{7,1},{8,0},{9,10},{10,1... | collective-permute-start | bytes 98312 | tf_op jit(solution)/shard_map/ppermute | solution.py:392
  34.4 2.8 %collective-permute-start.17 = (f32[4,16,128]{2,1,0:T(8,128)S(1)}, f32[4,16,128]{2,1,0:T(8,128)S(1)}, u32[]{:S(2)}, u32[]{:S(2)}) collective-permute-start(f32[4,16,128]{2,1,0:T(8,128)S(1)} %first_currents.1.refs_5_), channel_id=1, source_target_pairs={{0,16},{1,2},{2,3},{3,4},{4,5},{5,6},{6,7},{7,1},{8,24},{9,10},{10... | collective-permute-start | bytes 98312 | tf_op jit(solution)/shard_map/ppermute | solution.py:392
  37.2 3.3 %collective-permute-start.18 = (f32[4,16,128]{2,1,0:T(8,128)S(1)}, f32[4,16,128]{2,1,0:T(8,128)S(1)}, u32[]{:S(2)}, u32[]{:S(2)}) collective-permute-start(f32[4,16,128]{2,1,0:T(8,128)S(1)} %first_currents.1.refs_5_), channel_id=1, source_target_pairs={{0,24},{1,2},{2,3},{3,4},{4,5},{5,6},{6,7},{7,1},{8,16},{9,10},{10... | collective-permute-start | bytes 98312 | tf_op jit(solution)/shard_map/ppermute | solution.py:392
  40.5 2.4 %collective-permute-done.18.refs_8_ = f32[4,16,128]{2,1,0:T(8,128)S(1)} collective-permute-done((f32[4,16,128]{2,1,0:T(8,128)S(1)}, f32[4,16,128]{2,1,0:T(8,128)S(1)}, u32[]{:S(2)}, u32[]{:S(2)}) %collective-permute-start.18) | collective-permute-done | bytes 32800 | tf_op jit(solution)/shard_map/ppermute | solution.py:392
  42.9 1.3 %next_currents.3 = (f32[4,16,128]{2,1,0:T(8,128)S(1)}, bf16[17,32,128]{2,1,0:T(8,128)(2,1)S(1)}) custom-call(s32[772]{0:T(1024)S(1)} %copy-done.4, bf16[48,128,256]{2,1,0:T(8,128)(2,1)S(1)} %get-tuple-element.37.refs_0_.refs_1_.blocks, bf16[4,128,256]{2,1,0:T(8,128)(2,1)S(1)} %get-tuple-element.35.inverse, f32[4,4,16,128]{3,2,1,0:T(8,128)S(1)} %copy-done.1, ...), custom_call_target="tpu_custom_call" | custom-call | tf_op jit(solution)/shard_map/next_currents/pallas_call | solution.py:301
  44.2 3.9 %collective-permute-start.23 = (f32[4,16,128]{2,1,0:T(8,128)S(1)}, f32[4,16,128]{2,1,0:T(8,128)}, u32[]{:S(2)}, u32[]{:S(2)}) collective-permute-start(f32[4,16,128]{2,1,0:T(8,128)S(1)} %get-tuple-element.49.newest.refs_1_), channel_id=1, source_target_pairs={{0,16},{1,2},{2,3},{3,4},{4,5},{5,6},{6,7},{7,1},{8,24},{9,10},{10... | collective-permute-start | bytes 98312 | tf_op jit(solution)/shard_map/ppermute | solution.py:392
  48.1 0.5 collective-permute-start.24
  48.6 2.2 %older_field.2 = (f32[2,4,16,128]{3,2,1,0:T(8,128)S(1)}, f32[4,16,128]{2,1,0:T(8,128)}) custom-call(s32[772]{0:T(1024)S(1)} %copy-done.4, bf16[48,128,256]{2,1,0:T(8,128)(2,1)S(1)} %get-tuple-element.37.refs_0_.refs_1_.blocks, bf16[17,32,128]{2,1,0:T(8,128)(2,1)S(1)} %get-tuple-element.48.packed, f32[4,16,128]{2,1,0:T(8,128)S(1)} %get-tuple-element.49.newest.refs_1_, ...), custom_call_target="tpu_custom_call" | custom-call | tf_op jit(solution)/shard_map/older_field/pallas_call | solution.py:325
  50.8 3.2 %collective-permute-done.24.refs_4_ = f32[4,16,128]{2,1,0:T(8,128)} collective-permute-done((f32[4,16,128]{2,1,0:T(8,128)S(1)}, f32[4,16,128]{2,1,0:T(8,128)}, u32[]{:S(2)}, u32[]{:S(2)}) %collective-permute-start.24) | collective-permute-done | bytes 32800 | tf_op jit(solution)/shard_map/ppermute | solution.py:392
  53.9 1.5 %next_currents.4 = (f32[4,16,128]{2,1,0:T(8,128)S(1)}, bf16[17,32,128]{2,1,0:T(8,128)(2,1)S(1)}) custom-call(s32[772]{0:T(1024)S(1)} %copy-done.4, bf16[48,128,256]{2,1,0:T(8,128)(2,1)S(1)} %get-tuple-element.37.refs_0_.refs_1_.blocks, bf16[4,128,256]{2,1,0:T(8,128)(2,1)S(1)} %get-tuple-element.35.inverse, f32[2,4,16,128]{3,2,1,0:T(8,128)S(1)} %get-tuple-element.51.refs_0_, ...), custom_call_target="tpu_custom_call" | custom-call | tf_op jit(solution)/shard_map/next_currents/pallas_call | solution.py:301
  55.4 1.1 %collective-permute-start.29 = (f32[4,16,128]{2,1,0:T(8,128)S(1)}, f32[4,16,128]{2,1,0:T(8,128)S(1)}, u32[]{:S(2)}, u32[]{:S(2)}) collective-permute-start(f32[4,16,128]{2,1,0:T(8,128)S(1)} %get-tuple-element.53.newest.refs_1_), channel_id=1, source_target_pairs={{0,16},{1,2},{2,3},{3,4},{4,5},{5,6},{6,7},{7,1},{8,24},{9,10},{10... | collective-permute-start | bytes 98312 | tf_op jit(solution)/shard_map/ppermute | solution.py:392
  56.5 3.3 %collective-permute-start.30 = (f32[4,16,128]{2,1,0:T(8,128)S(1)}, f32[4,16,128]{2,1,0:T(8,128)S(1)}, u32[]{:S(2)}, u32[]{:S(2)}) collective-permute-start(f32[4,16,128]{2,1,0:T(8,128)S(1)} %get-tuple-element.53.newest.refs_1_), channel_id=1, source_target_pairs={{0,24},{1,2},{2,3},{3,4},{4,5},{5,6},{6,7},{7,1},{8,16},{9,10},{10... | collective-permute-start | bytes 98312 | tf_op jit(solution)/shard_map/ppermute | solution.py:392
  59.8 1.1 %older_field.3 = (f32[1,4,16,128]{3,2,1,0:T(8,128)S(1)}, f32[4,16,128]{2,1,0:T(8,128)S(1)}) custom-call(s32[772]{0:T(1024)S(1)} %copy-done.4, bf16[48,128,256]{2,1,0:T(8,128)(2,1)S(1)} %get-tuple-element.37.refs_0_.refs_1_.blocks, bf16[17,32,128]{2,1,0:T(8,128)(2,1)S(1)} %get-tuple-element.52.packed, f32[4,16,128]{2,1,0:T(8,128)S(1)} %get-tuple-element.53.newest.refs_1_, ...), custom_call_target="tpu_custom_call" | custom-call | tf_op jit(solution)/shard_map/older_field/pallas_call | solution.py:325
  60.9 0.8 %broadcast_select_fusion.2 = f32[4,16,128]{2,1,0:T(8,128)S(1)} fusion(f32[4,16,128]{2,1,0:T(8,128)} %collective-permute-done.19, f32[4,16,128]{2,1,0:T(8,128)} %get-tuple-element.50, pred[]{:T(512)S(6)} %eq.5), kind=kLoop, calls=%fused_computation.6 | loop fusion | flops 8192 | bytes 98305 | tf_op jit(solution)/shard_map/jit(_where)/select_n | solution.py:370
  61.7 0.4 collective-permute-done.30.refs_4_
  62.2 1.8 %next_currents.5 = (f32[4,16,128]{2,1,0:T(8,128)S(1)}, bf16[17,32,128]{2,1,0:T(8,128)(2,1)}) custom-call(s32[772]{0:T(1024)S(1)} %copy-done.4, bf16[48,128,256]{2,1,0:T(8,128)(2,1)S(1)} %get-tuple-element.37.refs_0_.refs_1_.blocks, bf16[4,128,256]{2,1,0:T(8,128)(2,1)S(1)} %get-tuple-element.35.inverse, f32[1,4,16,128]{3,2,1,0:T(8,128)S(1)} %get-tuple-element.55.refs_0_, ...), custom_call_target="tpu_custom_call" | custom-call | tf_op jit(solution)/shard_map/next_currents/pallas_call | solution.py:301
  64.0 1.3 %collective-permute-start.26 = (f32[4,16,128]{2,1,0:T(8,128)S(1)}, f32[4,16,128]{2,1,0:T(8,128)S(1)}, u32[]{:S(2)}, u32[]{:S(2)}) collective-permute-start(f32[4,16,128]{2,1,0:T(8,128)S(1)} %broadcast_select_fusion.1), channel_id=1, source_target_pairs={{0,2},{1,0},{2,3},{3,1},{4,6},{5,4},{6,7},{7,5},{8,10},{9,8},{10,1... | collective-permute-start | bytes 98312 | tf_op jit(solution)/shard_map/ppermute | solution.py:369
  65.4 0.2 collective-permute-done.31
  65.6 0.8 %collective-permute-start.32 = (f32[4,16,128]{2,1,0:T(8,128)S(1)}, f32[4,16,128]{2,1,0:T(8,128)S(1)}, u32[]{:S(2)}, u32[]{:S(2)}) collective-permute-start(f32[4,16,128]{2,1,0:T(8,128)S(1)} %broadcast_select_fusion), channel_id=1, source_target_pairs={{0,2},{1,0},{2,3},{3,1},{4,6},{5,4},{6,7},{7,5},{8,10},{9,8},{10,1... | collective-permute-start | bytes 98312 | tf_op jit(solution)/shard_map/ppermute | solution.py:369
  66.3 0.5 collective-permute-done.26
  66.9 0.4 collective-permute-start.27
  67.3 0.7 collective-permute-done.32
  67.9 1.1 %collective-permute-start.33 = (f32[4,16,128]{2,1,0:T(8,128)S(1)}, f32[4,16,128]{2,1,0:T(8,128)S(1)}, u32[]{:S(2)}, u32[]{:S(2)}) collective-permute-start(f32[4,16,128]{2,1,0:T(8,128)S(1)} %broadcast_select_fusion.3), channel_id=1, source_target_pairs={{0,1},{1,0},{2,3},{3,2},{4,5},{5,4},{6,7},{7,6},{8,9},{9,8},{10,11... | collective-permute-start | bytes 98312 | tf_op jit(solution)/shard_map/ppermute | solution.py:23
  69.1 0.8 %collective-permute-done.33 = f32[4,16,128]{2,1,0:T(8,128)S(1)} collective-permute-done((f32[4,16,128]{2,1,0:T(8,128)S(1)}, f32[4,16,128]{2,1,0:T(8,128)S(1)}, u32[]{:S(2)}, u32[]{:S(2)}) %collective-permute-start.33) | collective-permute-done | bytes 32800 | tf_op jit(solution)/shard_map/ppermute | solution.py:23
  69.9 0.7 pad_maximum_fusion
  (55 shorter events, 0.6 us)
Async XLA Ops:
  0.0 14.2 %collective-permute-start = (f32[4,4,16,128]{3,2,1,0:T(8,128)}, f32[4,4,16,128]{3,2,1,0:T(8,128)S(1)}, u32[]{:S(2)}, u32[]{:S(2)}) collective-permute-start(f32[4,4,16,128]{3,2,1,0:T(8,128)} %refs_1_.1), channel_id=1, source_target_pairs={{0,8},{8,0},{16,24},{24,16},{1,9},{9,1},{17,25},{25,17},{2,10},{10... | collective-permute-start | bytes 393224 | tf_op jit(solution)/shard_map/ppermute | solution.py:23
  3.0 13.3 %collective-permute-start.2 = (f32[4,4,16,128]{3,2,1,0:T(8,128)}, f32[4,4,16,128]{3,2,1,0:T(8,128)}, u32[]{:S(2)}, u32[]{:S(2)}) collective-permute-start(f32[4,4,16,128]{3,2,1,0:T(8,128)} %refs_1_.1), channel_id=1, source_target_pairs={{0,16},{8,24},{16,0},{24,8},{1,17},{9,25},{17,1},{25,9},{2,18},{10... | collective-permute-start | bytes 393224 | tf_op jit(solution)/shard_map/ppermute | solution.py:23
  5.6 10.7 %collective-permute-start.3 = (f32[4,4,16,128]{3,2,1,0:T(8,128)}, f32[4,4,16,128]{3,2,1,0:T(8,128)}, u32[]{:S(2)}, u32[]{:S(2)}) collective-permute-start(f32[4,4,16,128]{3,2,1,0:T(8,128)} %refs_1_.1), channel_id=1, source_target_pairs={{0,24},{8,16},{16,8},{24,0},{1,25},{9,17},{17,9},{25,1},{2,26},{10... | collective-permute-start | bytes 393224 | tf_op jit(solution)/shard_map/ppermute | solution.py:23
  5.6 16.2 %collective-permute-start.8 = (f32[4,4,16,128]{3,2,1,0:T(8,128)}, f32[4,4,16,128]{3,2,1,0:T(8,128)}, u32[]{:S(2)}, u32[]{:S(2)}) collective-permute-start(f32[4,4,16,128]{3,2,1,0:T(8,128)} %refs_1_.1), channel_id=1, source_target_pairs={{0,1},{1,2},{2,3},{3,4},{4,5},{5,6},{6,7},{7,0},{8,9},{9,10},{10,1... | collective-permute-start | bytes 393224 | tf_op jit(solution)/shard_map/ppermute | solution.py:404
  5.6 8.6 %collective-permute-start.1 = (s32[4]{0:T(128)}, s32[4]{0:T(128)S(1)}, u32[]{:S(2)}, u32[]{:S(2)}) collective-permute-start(s32[4]{0:T(128)} %slots.1), channel_id=1, source_target_pairs={{0,1},{1,2},{2,3},{3,4},{4,5},{5,6},{6,7},{7,0},{8,9},{9,10},{10,1... | collective-permute-start | bytes 56 | tf_op jit(solution)/shard_map/ppermute | solution.py:396
  10.6 1.9 %copy-start = (f32[48,128,128]{2,1,0:T(8,128)S(1)}, f32[48,128,128]{2,1,0:T(8,128)}, u32[]{:S(2)}) copy-start(f32[48,128,128]{2,1,0:T(8,128)} %blocks.1) | copy-start | bytes 9437188
  12.5 0.9 %copy-start.2 = (f32[4,128,128]{2,1,0:T(8,128)S(1)}, f32[4,128,128]{2,1,0:T(8,128)}, u32[]{:S(2)}) copy-start(f32[4,128,128]{2,1,0:T(8,128)} %inverse.1) | copy-start | bytes 786436
  13.4 1.4 %copy-start.3 = (f32[4,4,16,128]{3,2,1,0:T(8,128)S(1)}, f32[4,4,16,128]{3,2,1,0:T(8,128)}, u32[]{:S(2)}) copy-start(f32[4,4,16,128]{3,2,1,0:T(8,128)} %refs_1_.1) | copy-start | bytes 393220
  13.4 1.4 %copy-start.5 = (s32[1091]{0:T(1024)S(1)}, s32[1091]{0:T(1024)}, u32[]{:S(2)}) copy-start(s32[1091]{0:T(1024)} %get-tuple-element.36.plan) | copy-start | bytes 13096
  14.2 7.6 %collective-permute-start.9 = (f32[4,4,16,128]{3,2,1,0:T(8,128)S(1)}, f32[4,4,16,128]{3,2,1,0:T(8,128)S(1)}, u32[]{:S(2)}, u32[]{:S(2)}) collective-permute-start(f32[4,4,16,128]{3,2,1,0:T(8,128)S(1)} %collective-permute-done.refs_2_), channel_id=1, source_target_pairs={{0,1},{1,2},{2,3},{3,4},{4,5},{5,6},{6,7},{7,0},{8,9},{9,10},{10,1... | collective-permute-start | bytes 393224 | tf_op jit(solution)/shard_map/ppermute | solution.py:404
  15.9 16.7 %copy-start.1 = (f32[4,4,16,128]{3,2,1,0:T(8,128)S(1)}, f32[4,4,16,128]{3,2,1,0:T(8,128)}, u32[]{:S(2)}) copy-start(f32[4,4,16,128]{3,2,1,0:T(8,128)} %refs_0_.3) | copy-start | bytes 393220
  16.3 5.5 %collective-permute-start.10 = (f32[4,4,16,128]{3,2,1,0:T(8,128)}, f32[4,4,16,128]{3,2,1,0:T(8,128)S(1)}, u32[]{:S(2)}, u32[]{:S(2)}) collective-permute-start(f32[4,4,16,128]{3,2,1,0:T(8,128)} %collective-permute-done.2.refs_2_), channel_id=1, source_target_pairs={{0,1},{1,2},{2,3},{3,4},{4,5},{5,6},{6,7},{7,0},{8,9},{9,10},{10,1... | collective-permute-start | bytes 393224 | tf_op jit(solution)/shard_map/ppermute | solution.py:404
  17.9 5.5 %collective-permute-start.11 = (f32[4,4,16,128]{3,2,1,0:T(8,128)}, f32[4,4,16,128]{3,2,1,0:T(8,128)S(1)}, u32[]{:S(2)}, u32[]{:S(2)}) collective-permute-start(f32[4,4,16,128]{3,2,1,0:T(8,128)} %collective-permute-done.3.refs_3_), channel_id=1, source_target_pairs={{0,1},{1,2},{2,3},{3,4},{4,5},{5,6},{6,7},{7,0},{8,9},{9,10},{10,1... | collective-permute-start | bytes 393224 | tf_op jit(solution)/shard_map/ppermute | solution.py:404
  19.8 23.1 %copy-start.4 = (s32[772]{0:T(1024)S(1)}, s32[772]{0:T(1024)}, u32[]{:S(2)}) copy-start(s32[772]{0:T(1024)} %get-tuple-element.45.plan) | copy-start | bytes 9268
  19.8 2.0 %collective-permute-start.4 = (f32[4,16,128]{2,1,0:T(8,128)S(1)}, f32[4,16,128]{2,1,0:T(8,128)S(1)}, u32[]{:S(2)}, u32[]{:S(2)}) collective-permute-start(f32[4,16,128]{2,1,0:T(8,128)S(1)} %get-tuple-element.42), channel_id=1, source_target_pairs={{0,1},{1,0},{2,3},{3,2},{4,5},{5,4},{6,7},{7,6},{8,9},{9,8},{10,11... | collective-permute-start | bytes 98312 | tf_op jit(solution)/shard_map/ppermute | solution.py:23
  24.4 4.4 %collective-permute-start.12 = (f32[3,4,16,128]{3,2,1,0:T(8,128)S(1)}, f32[3,4,16,128]{3,2,1,0:T(8,128)S(1)}, u32[]{:S(2)}, u32[]{:S(2)}) collective-permute-start(f32[3,4,16,128]{3,2,1,0:T(8,128)S(1)} %late_field.1), channel_id=1, source_target_pairs={{0,1},{1,0},{2,3},{3,2},{4,5},{5,4},{6,7},{7,6},{8,9},{9,8},{10,11... | collective-permute-start | bytes 294920 | tf_op jit(solution)/shard_map/ppermute | solution.py:23
  24.5 5.7 %collective-permute-start.5 = (f32[4,16,128]{2,1,0:T(8,128)S(1)}, f32[4,16,128]{2,1,0:T(8,128)S(1)}, u32[]{:S(2)}, u32[]{:S(2)}) collective-permute-start(f32[4,16,128]{2,1,0:T(8,128)S(1)} %add.6.refs_0_), channel_id=1, source_target_pairs={{0,2},{1,3},{2,0},{3,1},{4,6},{5,7},{6,4},{7,5},{8,10},{9,11},{10,... | collective-permute-start | bytes 98312 | tf_op jit(solution)/shard_map/ppermute | solution.py:23
  26.8 4.4 %collective-permute-start.6 = (f32[4,16,128]{2,1,0:T(8,128)S(1)}, f32[4,16,128]{2,1,0:T(8,128)S(1)}, u32[]{:S(2)}, u32[]{:S(2)}) collective-permute-start(f32[4,16,128]{2,1,0:T(8,128)S(1)} %add.6.refs_0_), channel_id=1, source_target_pairs={{0,4},{1,5},{2,6},{3,7},{4,0},{5,1},{6,2},{7,3},{8,12},{9,13},{10,... | collective-permute-start | bytes 98312 | tf_op jit(solution)/shard_map/ppermute | solution.py:23
  27.9 4.8 %collective-permute-start.7 = (f32[4,16,128]{2,1,0:T(8,128)S(1)}, f32[4,16,128]{2,1,0:T(8,128)S(1)}, u32[]{:S(2)}, u32[]{:S(2)}) collective-permute-start(f32[4,16,128]{2,1,0:T(8,128)S(1)} %add.6.refs_0_), channel_id=1, source_target_pairs={{0,6},{1,7},{2,4},{3,5},{4,2},{5,3},{6,0},{7,1},{8,14},{9,15},{10,... | collective-permute-start | bytes 98312 | tf_op jit(solution)/shard_map/ppermute | solution.py:23
  28.9 14.0 %collective-permute-start.13 = (f32[3,4,16,128]{3,2,1,0:T(8,128)S(1)}, f32[3,4,16,128]{3,2,1,0:T(8,128)S(1)}, u32[]{:S(2)}, u32[]{:S(2)}) collective-permute-start(f32[3,4,16,128]{3,2,1,0:T(8,128)S(1)} %add.7.refs_1_), channel_id=1, source_target_pairs={{0,1},{1,7},{2,3},{3,2},{4,5},{5,4},{6,0},{7,6},{8,9},{9,15},{10,1... | collective-permute-start | bytes 294920 | tf_op jit(solution)/shard_map/ppermute | solution.py:349
  28.9 14.0 %collective-permute-start.14 = (f32[3,4,16,128]{3,2,1,0:T(8,128)S(1)}, f32[3,4,16,128]{3,2,1,0:T(8,128)S(1)}, u32[]{:S(2)}, u32[]{:S(2)}) collective-permute-start(f32[3,4,16,128]{3,2,1,0:T(8,128)S(1)} %add.7.refs_1_), channel_id=1, source_target_pairs={{0,1},{1,5},{2,3},{3,2},{4,0},{5,4},{6,7},{7,6},{8,9},{9,13},{10,1... | collective-permute-start | bytes 294920 | tf_op jit(solution)/shard_map/ppermute | solution.py:349
  30.2 12.7 %collective-permute-start.15 = (f32[3,4,16,128]{3,2,1,0:T(8,128)S(1)}, f32[3,4,16,128]{3,2,1,0:T(8,128)S(1)}, u32[]{:S(2)}, u32[]{:S(2)}) collective-permute-start(f32[3,4,16,128]{3,2,1,0:T(8,128)S(1)} %add.7.refs_1_), channel_id=1, source_target_pairs={{0,1},{1,3},{2,0},{3,2},{4,5},{5,4},{6,7},{7,6},{8,9},{9,11},{10,8... | collective-permute-start | bytes 294920 | tf_op jit(solution)/shard_map/ppermute | solution.py:349
  32.9 4.3 %collective-permute-start.16 = (f32[4,16,128]{2,1,0:T(8,128)S(1)}, f32[4,16,128]{2,1,0:T(8,128)S(1)}, u32[]{:S(2)}, u32[]{:S(2)}) collective-permute-start(f32[4,16,128]{2,1,0:T(8,128)S(1)} %first_currents.1.refs_5_), channel_id=1, source_target_pairs={{0,8},{1,2},{2,3},{3,4},{4,5},{5,6},{6,7},{7,1},{8,0},{9,10},{10,1... | collective-permute-start | bytes 98312 | tf_op jit(solution)/shard_map/ppermute | solution.py:392
  34.4 6.2 %collective-permute-start.17 = (f32[4,16,128]{2,1,0:T(8,128)S(1)}, f32[4,16,128]{2,1,0:T(8,128)S(1)}, u32[]{:S(2)}, u32[]{:S(2)}) collective-permute-start(f32[4,16,128]{2,1,0:T(8,128)S(1)} %first_currents.1.refs_5_), channel_id=1, source_target_pairs={{0,16},{1,2},{2,3},{3,4},{4,5},{5,6},{6,7},{7,1},{8,24},{9,10},{10... | collective-permute-start | bytes 98312 | tf_op jit(solution)/shard_map/ppermute | solution.py:392
  37.2 5.7 %collective-permute-start.18 = (f32[4,16,128]{2,1,0:T(8,128)S(1)}, f32[4,16,128]{2,1,0:T(8,128)S(1)}, u32[]{:S(2)}, u32[]{:S(2)}) collective-permute-start(f32[4,16,128]{2,1,0:T(8,128)S(1)} %first_currents.1.refs_5_), channel_id=1, source_target_pairs={{0,24},{1,2},{2,3},{3,4},{4,5},{5,6},{6,7},{7,1},{8,16},{9,10},{10... | collective-permute-start | bytes 98312 | tf_op jit(solution)/shard_map/ppermute | solution.py:392
  44.2 6.6 %collective-permute-start.22 = (f32[4,16,128]{2,1,0:T(8,128)S(1)}, f32[4,16,128]{2,1,0:T(8,128)}, u32[]{:S(2)}, u32[]{:S(2)}) collective-permute-start(f32[4,16,128]{2,1,0:T(8,128)S(1)} %get-tuple-element.49.newest.refs_1_), channel_id=1, source_target_pairs={{0,8},{1,2},{2,3},{3,4},{4,5},{5,6},{6,7},{7,1},{8,0},{9,10},{10,1... | collective-permute-start | bytes 98312 | tf_op jit(solution)/shard_map/ppermute | solution.py:392
  44.2 6.6 %collective-permute-start.23 = (f32[4,16,128]{2,1,0:T(8,128)S(1)}, f32[4,16,128]{2,1,0:T(8,128)}, u32[]{:S(2)}, u32[]{:S(2)}) collective-permute-start(f32[4,16,128]{2,1,0:T(8,128)S(1)} %get-tuple-element.49.newest.refs_1_), channel_id=1, source_target_pairs={{0,16},{1,2},{2,3},{3,4},{4,5},{5,6},{6,7},{7,1},{8,24},{9,10},{10... | collective-permute-start | bytes 98312 | tf_op jit(solution)/shard_map/ppermute | solution.py:392
  48.1 5.8 %collective-permute-start.24 = (f32[4,16,128]{2,1,0:T(8,128)S(1)}, f32[4,16,128]{2,1,0:T(8,128)}, u32[]{:S(2)}, u32[]{:S(2)}) collective-permute-start(f32[4,16,128]{2,1,0:T(8,128)S(1)} %get-tuple-element.49.newest.refs_1_), channel_id=1, source_target_pairs={{0,24},{1,2},{2,3},{3,4},{4,5},{5,6},{6,7},{7,1},{8,16},{9,10},{10... | collective-permute-start | bytes 98312 | tf_op jit(solution)/shard_map/ppermute | solution.py:392
  50.8 10.2 %collective-permute-start.19 = (f32[4,16,128]{2,1,0:T(8,128)}, f32[4,16,128]{2,1,0:T(8,128)}, u32[]{:S(2)}, u32[]{:S(2)}) collective-permute-start(f32[4,16,128]{2,1,0:T(8,128)} %get-tuple-element.50), channel_id=1, source_target_pairs={{0,4},{1,0},{2,3},{3,2},{4,5},{5,1},{6,7},{7,6},{8,12},{9,8},{10,1... | collective-permute-start | bytes 98312 | tf_op jit(solution)/shard_map/ppermute | solution.py:369
  55.4 6.3 %collective-permute-start.28 = (f32[4,16,128]{2,1,0:T(8,128)S(1)}, f32[4,16,128]{2,1,0:T(8,128)S(1)}, u32[]{:S(2)}, u32[]{:S(2)}) collective-permute-start(f32[4,16,128]{2,1,0:T(8,128)S(1)} %get-tuple-element.53.newest.refs_1_), channel_id=1, source_target_pairs={{0,8},{1,2},{2,3},{3,4},{4,5},{5,6},{6,7},{7,1},{8,0},{9,10},{10,1... | collective-permute-start | bytes 98312 | tf_op jit(solution)/shard_map/ppermute | solution.py:392
  55.4 6.3 %collective-permute-start.29 = (f32[4,16,128]{2,1,0:T(8,128)S(1)}, f32[4,16,128]{2,1,0:T(8,128)S(1)}, u32[]{:S(2)}, u32[]{:S(2)}) collective-permute-start(f32[4,16,128]{2,1,0:T(8,128)S(1)} %get-tuple-element.53.newest.refs_1_), channel_id=1, source_target_pairs={{0,16},{1,2},{2,3},{3,4},{4,5},{5,6},{6,7},{7,1},{8,24},{9,10},{10... | collective-permute-start | bytes 98312 | tf_op jit(solution)/shard_map/ppermute | solution.py:392
  56.5 5.7 %collective-permute-start.30 = (f32[4,16,128]{2,1,0:T(8,128)S(1)}, f32[4,16,128]{2,1,0:T(8,128)S(1)}, u32[]{:S(2)}, u32[]{:S(2)}) collective-permute-start(f32[4,16,128]{2,1,0:T(8,128)S(1)} %get-tuple-element.53.newest.refs_1_), channel_id=1, source_target_pairs={{0,24},{1,2},{2,3},{3,4},{4,5},{5,6},{6,7},{7,1},{8,16},{9,10},{10... | collective-permute-start | bytes 98312 | tf_op jit(solution)/shard_map/ppermute | solution.py:392
  60.9 3.1 %collective-permute-start.25 = (f32[4,16,128]{2,1,0:T(8,128)S(1)}, f32[4,16,128]{2,1,0:T(8,128)S(1)}, u32[]{:S(2)}, u32[]{:S(2)}) collective-permute-start(f32[4,16,128]{2,1,0:T(8,128)S(1)} %get-tuple-element.54), channel_id=1, source_target_pairs={{0,4},{1,0},{2,3},{3,2},{4,5},{5,1},{6,7},{7,6},{8,12},{9,8},{10,1... | collective-permute-start | bytes 98312 | tf_op jit(solution)/shard_map/ppermute | solution.py:369
  61.7 3.5 %collective-permute-start.20 = (f32[4,16,128]{2,1,0:T(8,128)S(1)}, f32[4,16,128]{2,1,0:T(8,128)S(1)}, u32[]{:S(2)}, u32[]{:S(2)}) collective-permute-start(f32[4,16,128]{2,1,0:T(8,128)S(1)} %broadcast_select_fusion.2), channel_id=1, source_target_pairs={{0,2},{1,0},{2,3},{3,1},{4,6},{5,4},{6,7},{7,5},{8,10},{9,8},{10,1... | collective-permute-start | bytes 98312 | tf_op jit(solution)/shard_map/ppermute | solution.py:369
  63.9 1.6 %collective-permute-start.31 = (f32[4,16,128]{2,1,0:T(8,128)S(1)}, f32[4,16,128]{2,1,0:T(8,128)S(1)}, u32[]{:S(2)}, u32[]{:S(2)}) collective-permute-start(f32[4,16,128]{2,1,0:T(8,128)S(1)} %get-tuple-element.56), channel_id=1, source_target_pairs={{0,4},{1,0},{2,3},{3,2},{4,5},{5,1},{6,7},{7,6},{8,12},{9,8},{10,1... | collective-permute-start | bytes 98312 | tf_op jit(solution)/shard_map/ppermute | solution.py:369
  64.0 2.9 %collective-permute-start.26 = (f32[4,16,128]{2,1,0:T(8,128)S(1)}, f32[4,16,128]{2,1,0:T(8,128)S(1)}, u32[]{:S(2)}, u32[]{:S(2)}) collective-permute-start(f32[4,16,128]{2,1,0:T(8,128)S(1)} %broadcast_select_fusion.1), channel_id=1, source_target_pairs={{0,2},{1,0},{2,3},{3,1},{4,6},{5,4},{6,7},{7,5},{8,10},{9,8},{10,1... | collective-permute-start | bytes 98312 | tf_op jit(solution)/shard_map/ppermute | solution.py:369
  65.3 2.0 %collective-permute-start.21 = (f32[4,16,128]{2,1,0:T(8,128)S(1)}, f32[4,16,128]{2,1,0:T(8,128)S(1)}, u32[]{:S(2)}, u32[]{:S(2)}) collective-permute-start(f32[4,16,128]{2,1,0:T(8,128)S(1)} %broadcast_select_fusion.5), channel_id=1, source_target_pairs={{0,1},{1,0},{2,3},{3,2},{4,5},{5,4},{6,7},{7,6},{8,9},{9,8},{10,11... | collective-permute-start | bytes 98312 | tf_op jit(solution)/shard_map/ppermute | solution.py:23
  65.6 2.4 %collective-permute-start.32 = (f32[4,16,128]{2,1,0:T(8,128)S(1)}, f32[4,16,128]{2,1,0:T(8,128)S(1)}, u32[]{:S(2)}, u32[]{:S(2)}) collective-permute-start(f32[4,16,128]{2,1,0:T(8,128)S(1)} %broadcast_select_fusion), channel_id=1, source_target_pairs={{0,2},{1,0},{2,3},{3,1},{4,6},{5,4},{6,7},{7,5},{8,10},{9,8},{10,1... | collective-permute-start | bytes 98312 | tf_op jit(solution)/shard_map/ppermute | solution.py:369
  66.9 2.2 %collective-permute-start.27 = (f32[4,16,128]{2,1,0:T(8,128)S(1)}, f32[4,16,128]{2,1,0:T(8,128)S(1)}, u32[]{:S(2)}, u32[]{:S(2)}) collective-permute-start(f32[4,16,128]{2,1,0:T(8,128)S(1)} %broadcast_select_fusion.4), channel_id=1, source_target_pairs={{0,1},{1,0},{2,3},{3,2},{4,5},{5,4},{6,7},{7,6},{8,9},{9,8},{10,11... | collective-permute-start | bytes 98312 | tf_op jit(solution)/shard_map/ppermute | solution.py:23
  67.9 2.0 %collective-permute-start.33 = (f32[4,16,128]{2,1,0:T(8,128)S(1)}, f32[4,16,128]{2,1,0:T(8,128)S(1)}, u32[]{:S(2)}, u32[]{:S(2)}) collective-permute-start(f32[4,16,128]{2,1,0:T(8,128)S(1)} %broadcast_select_fusion.3), channel_id=1, source_target_pairs={{0,1},{1,0},{2,3},{3,2},{4,5},{5,4},{6,7},{7,6},{8,9},{9,8},{10,11... | collective-permute-start | bytes 98312 | tf_op jit(solution)/shard_map/ppermute | solution.py:23

commit v3 on v2

--- a/solution.py
+++ b/solution.py
@@ -12,6 +12,7 @@
 VMEM = pltpu.VMEM
 SMEM = pltpu.SMEM
 UNROLL = 16
+BRIEF = pl.CostEstimate(flops=1, bytes_accessed=1, transcendentals=0)
 
 
 def whole(space):
@@ -52,7 +53,8 @@
         count[d] = 0
     wide_entry, late_entry, late_start = 2 + steps, 1 + steps, 3 + 2 * size * (2 + steps)
 
-    def place(e, near):
+    def place(e, taken):
+        near, few = taken
         row, column, d = pattern[0, e], pattern[1, e], pattern[2, e]
         group = (column // group_blocks) ^ me[0]
         block = column % group_blocks
@@ -64,7 +66,7 @@
             at = ((group - 2 * is_far) * places + held[jnp.maximum(d - t, 0)]) * group_blocks + block
             nothing = jnp.where(is_far == 1, (groups - 2) * cells, 2 * cells)
             past[to + 2 + t] = jnp.where(d >= t, at, nothing)
-        to = late_start + e * late_entry
+        to = late_start + few * late_entry
         past[to] = e
         past[to + 1] = row
         for t in range(1, steps):
@@ -76,13 +78,13 @@
         newer[to] = e
         newer[to + 1] = row
         newer[to + 2] = group * group_blocks + block
-        return near + 1 - is_far
-
-    near = lax.fori_loop(0, live[0], place, jnp.int32(0))
+        return near + 1 - is_far, few + (d < steps - 1).astype(jnp.int32)
+
+    near, few = lax.fori_loop(0, live[0], place, (jnp.int32(0), jnp.int32(0)))
     far = live[0] - near
     past[0] = near
     past[1] = far
-    past[2] = jnp.where(band[0] == 0, 0, live[0])
+    past[2] = jnp.where(band[0] == 0, 0, few)
 
     def fill(i, c):
         for k, n, nothing in ((0, near, 2 * cells), (1, far, (groups - 2) * cells)):
@@ -91,7 +93,7 @@
             past[to + 1] = 0
             for t in range(steps):
                 past[to + 2 + t] = nothing
-        to = late_start + (live[0] + i) * late_entry
+        to = late_start + (few + i) * late_entry
         past[to] = 0
         past[to + 1] = 0
         for t in range(1, steps):
@@ -232,6 +234,7 @@
         out_shape=out,
         scratch_shapes=[packed],
         compiler_params=pltpu.CompilerParams(vmem_limit_bytes=16 << 20),
+        cost_estimate=BRIEF,
         name=when + "_field",
     )(*scalars, *given, *parts)
 
@@ -265,6 +268,7 @@
         out_shape=jax.ShapeDtypeStruct(shape, F32),
         scratch_shapes=[VMEM(shape, F32)],
         compiler_params=pltpu.CompilerParams(vmem_limit_bytes=16 << 20),
+        cost_estimate=BRIEF,
         name="first_currents",
     )(inverse, incident, *terms)
 
@@ -280,9 +284,10 @@
     return rights[0][t + 1] - summed(rights[1:], t)
 
 
-def step_kernel(places, count, plan, blocks, inverse, *refs):
-    rights, parts, (out, packed, right) = refs[:count], refs[count:-3], refs[-3:]
-    group_blocks, columns, width = out.shape
+def step_kernel(places, count, done, plan, blocks, inverse, *refs):
+    rights, refs = refs[:count], refs[count:]
+    earlier, parts, (out, packed, right) = refs[:done], refs[done:-3], refs[-3:]
+    group_blocks, columns, width = right.shape
     for k in range(len(parts)):
         pack(packed, k * group_blocks, parts[k][...])
     packed[len(parts) * group_blocks] = jnp.zeros((2 * columns, width), BF16)
@@ -292,26 +297,39 @@
         right[row] -= y
 
     recent(0, plan, places, packed, blocks, add)
+    if done:
+        last = out.shape[0] - 1
+        out[:last] = earlier[0][...]
+        out = out.at[last]
     solve(inverse, right, out)
 
 
-def next_currents(places, plan, blocks, inverse, rights, parts):
+def next_currents(places, plan, blocks, inverse, rights, parts, earlier=None):
     shape = parts[0].shape
     packed = (len(parts) * shape[0] + 1, 2 * shape[1], shape[2])
-    return pl.pallas_call(
-        functools.partial(step_kernel, places, len(rights)),
-        in_specs=[whole(SMEM)] + [whole(VMEM)] * (2 + len(rights) + len(parts)),
-        out_specs=[whole(VMEM)] * 2,
-        out_shape=[jax.ShapeDtypeStruct(shape, F32), jax.ShapeDtypeStruct(packed, BF16)],
-        scratch_shapes=[VMEM(shape, F32)],
+    scratch = [VMEM(shape, F32)]
+    if earlier is None:
+        given, out = [], [jax.ShapeDtypeStruct(shape, F32), jax.ShapeDtypeStruct(packed, BF16)]
+    else:
+        given, out = [earlier], [jax.ShapeDtypeStruct((earlier.shape[0] + 1,) + shape, F32)]
+        scratch.insert(0, VMEM(packed, BF16))
+    return pl.pallas_call(
+        functools.partial(step_kernel, places, len(rights), len(given)),
+        in_specs=[whole(SMEM)] + [whole(VMEM)] * (2 + len(rights) + len(given) + len(parts)),
+        out_specs=[whole(VMEM)] * len(out),
+        out_shape=out,
+        scratch_shapes=scratch,
         compiler_params=pltpu.CompilerParams(vmem_limit_bytes=16 << 20),
+        cost_estimate=BRIEF,
         name="next_currents",
-    )(plan, blocks, inverse, *rights, *parts)
-
-
-def older_kernel(places, plan, blocks, packed, newest, *refs):
-    *rights, out, passed = refs
-    passed[...] = newest[...]
+    )(plan, blocks, inverse, *rights, *given, *parts)
+
+
+def older_kernel(places, count, plan, blocks, packed, newest, *refs):
+    rights, earlier, (out, stacked) = refs[:count], refs[count:-2], refs[-2:]
+    if earlier:
+        stacked[: stacked.shape[0] - 1] = earlier[0][...]
+    stacked[stacked.shape[0] - 1] = newest[...]
     for t in range(out.shape[0]):
         out[t] = right_side(rights, t + 1)
 
@@ -321,15 +339,18 @@
         recent(t + 1, plan, places, packed, blocks, add)
 
 
-def older_field(places, steps, plan, blocks, packed, newest, rights):
-    return pl.pallas_call(
-        functools.partial(older_kernel, places),
-        in_specs=[whole(SMEM)] + [whole(VMEM)] * (3 + len(rights)),
+def older_field(places, steps, plan, blocks, packed, newest, rights, earlier):
+    given = [] if earlier is None else [earlier]
+    stacked = (sum(x.shape[0] for x in given) + 1,) + newest.shape
+    return pl.pallas_call(
+        functools.partial(older_kernel, places, len(rights)),
+        in_specs=[whole(SMEM)] + [whole(VMEM)] * (3 + len(rights) + len(given)),
         out_specs=[whole(VMEM)] * 2,
-        out_shape=[jax.ShapeDtypeStruct((steps,) + newest.shape, F32), jax.ShapeDtypeStruct(newest.shape, F32)],
+        out_shape=[jax.ShapeDtypeStruct((steps,) + newest.shape, F32), jax.ShapeDtypeStruct(stacked, F32)],
         compiler_params=pltpu.CompilerParams(vmem_limit_bytes=16 << 20),
+        cost_estimate=BRIEF,
         name="older_field",
-    )(plan, blocks, packed, newest, *rights)
+    )(plan, blocks, packed, newest, *rights, *given)
 
 
 def summands(x):
@@ -372,6 +393,20 @@
     return x
 
 
+AT_ONCE = {2: ((0, 2, 3), (1, 5), (4, 6, 7)), 4: ((0, 4, 5), (1, 7), (2, 3, 6)), 6: ((0, 6, 7, 1), (2, 3), (4, 5))}
+
+
+def from_front_at_once(x):
+    if lax.axis_size("delay") != 8:
+        return from_front(x)
+    pair = lax.axis_index("delay") // 2 * 2
+    y = x
+    for c, cycles in reversed(AT_ONCE.items()):
+        goes = [(a, b) for cycle in cycles for a, b in zip(cycle, cycle[1:] + cycle[:1])]
+        y = jnp.where(pair == c, lax.ppermute(x, "delay", goes), y)
+    return y
+
+
 def from_even(x):
     return jnp.where((lax.axis_index("delay") & 1) != 0, swap(x, "delay", 1), x)
 
@@ -381,7 +416,7 @@
     moments = incident.shape[0]
     groups = lax.axis_size("src")
     bands = lax.axis_size("delay")
-    assert moments - 1 <= slot_count and moments % 2 == 0
+    assert 1 < moments <= slot_count + 1
     assert groups & (groups - 1) == 0 and bands & (bands - 1) == 0
     me = lax.axis_index("src").reshape(1)
     band = lax.axis_index("delay").reshape(1)
@@ -406,21 +441,24 @@
     now = now + swap(now, "delay", 1)
     now, field = lax.optimization_barrier((now, field))
     (later,) = past_field("late", moments, past, blocks, before, field, slots_before)
-
-    newest = first_currents(inverse, incident, summands(now))
-    results = [newest]
-    rights = None
+    first = newest = first_currents(inverse, incident, summands(now))
+    earlier = None
     for moment in range(1, moments):
         shared = front_over_src(newest)
         if moment == 1:
             rights = [incident] + front_summands(later + swap(later, "delay", 1))
         else:
-            rights, newest = older_field(slot_count, moments - moment, newer, blocks, packed, newest, rights)
+            rights, earlier = older_field(
+                slot_count, moments - moment, newer, blocks, packed, newest, rights, earlier
+            )
             rights = [rights]
-            results.append(from_even(from_front(newest)))
-        newest, packed = next_currents(slot_count, newer, blocks, inverse, rights, shared)
-    results.append(from_even(from_front(newest)))
-    return jnp.stack(results)
+        made = next_currents(
+            slot_count, newer, blocks, inverse, rights, shared, earlier if moment > 1 and moment + 1 == moments else None
+        )
+        if len(made) > 1:
+            newest, packed = made
+    (others,) = made if len(made) == 1 else (newest[None],)
+    return jnp.concatenate([first[None], from_even(from_front_at_once(others))])
 
 
 def solution(mesh):

time: 71.2 us -> 69.2 us (0.972)
  starting transfers between devices: 38.2 us -> 32.5 us
  waiting for transfers between devices: 12.6 us -> 16.9 us
  other arithmetic: 1.5 us -> 0.72 us
    ppermute x6 -> x3, waiting for transfers between devices: 1.39 us -> 3.94 us  [from_front_at_once(): y = jnp.where(pair == c, lax.ppermute(x, 'delay', goes), y)]
    ppermute x11 -> x9, starting transfers between devices: 12.7 us -> 10.2 us  [swap(): return lax.ppermute(x, axis, [(i, i ^ bits) for i in range(n)])]
    ppermute x6 -> x3, starting transfers between devices: 2.14 us -> 0.11 us  [from_front_at_once(): y = jnp.where(pair == c, lax.ppermute(x, 'delay', goes), y)]
    ppermute x9, waiting for transfers between devices: 5.98 us -> 7.36 us  [front_over_src(): return [x] + [lax.ppermute(x, ('src', 'delay'), p) for p in pairs]]
    pallas_call x5, Pallas kernels: 7.69 us -> 6.35 us  [the longest x3 3.76 us: next_currents(): pl.pallas_call(functools.partial(step_kernel, places, len(rights), len(gi...]
    pallas_call x1, Pallas kernels: 2.47 us -> 3.68 us  [make_plan(): pl.pallas_call(functools.partial(plan_kernel, groups, group_blocks, steps...]
    ppermute x4, starting transfers between devices: 2.69 us -> 1.67 us  [body(): before = [lax.ppermute(p, 'delay', ring) for p in parts]]
    select_n x6 -> x2, other arithmetic: 0.81 us -> 0.04 us  [the longest x1 0.02 us: from_front_at_once(): y = jnp.where(pair == c, lax.ppermute(x, 'delay', goes), y)]
  transfers between devices with their start and end apart: 34 -> 29, of which waited for: 11 -> 9; matrix products, arithmetic and copies ran while one was open for 1% -> 0% of each run, Pallas kernels for 18% -> 15%
where the time goes in v3:
time: 69.2 us; the launch traced here: 68.7 us
  starting transfers between devices  32.5 us (47%)
  waiting for transfers between devices  16.9 us (24%)
  Pallas kernels  14.7 us (21%)
  local copies, waits for them, and re-layouts  2.91 us (4%)
  between operations  0.89 us (1%)
  other arithmetic  0.72 us (1%)
    ppermute x9, starting transfers between devices, front_over_src(): return [x] + [lax.ppermute(x, ('src', 'delay'), p) for p in pairs]  16.4 us
    ppermute x9, starting transfers between devices, swap(): return lax.ppermute(x, axis, [(i, i ^ bits) for i in range(n)])  10.2 us
    ppermute x9, waiting for transfers between devices, front_over_src(): return [x] + [lax.ppermute(x, ('src', 'delay'), p) for p in pairs]  7.36 us
    ppermute x3, waiting for transfers between devices, from_front_at_once(): y = jnp.where(pair == c, lax.ppermute(x, 'delay', goes), y)  3.94 us
    pallas_call x3, Pallas kernels, past_field(): pl.pallas_call(functools.partial(past_kernel, when), in_specs=[whole(SMEM...  3.78 us
    pallas_call x3, Pallas kernels, next_currents(): pl.pallas_call(functools.partial(step_kernel, places, len(rights), len(gi...  3.76 us
    ppermute x9, waiting for transfers between devices, swap(): return lax.ppermute(x, axis, [(i, i ^ bits) for i in range(n)])  3.72 us
    pallas_call x1, Pallas kernels, make_plan(): pl.pallas_call(functools.partial(plan_kernel, groups, group_blocks, steps...  3.68 us
  transfers between devices with their start and end apart: 29, of which 9 were waited for; matrix products, arithmetic and copies ran while one was open for 0% of the time, Pallas kernels for 15%

profile of v3, /device:TPU:0, one launch (start us, length us, event | category | flops | bytes accessed | tf_op | source)
XLA Modules:
  0.0 68.7 jit_solution(17779222828019518509)
XLA Ops:
  0.0 3.0 %collective-permute-start = (f32[4,4,16,128]{3,2,1,0:T(8,128)}, f32[4,4,16,128]{3,2,1,0:T(8,128)S(1)}, u32[]{:S(2)}, u32[]{:S(2)}) collective-permute-start(f32[4,4,16,128]{3,2,1,0:T(8,128)} %refs_1_.1), channel_id=1, source_target_pairs={{0,8},{8,0},{16,24},{24,16},{1,9},{9,1},{17,25},{25,17},{2,10},{10... | collective-permute-start | bytes 393224 | tf_op jit(solution)/shard_map/ppermute | solution.py:24
  3.0 2.6 %collective-permute-start.2 = (f32[4,4,16,128]{3,2,1,0:T(8,128)}, f32[4,4,16,128]{3,2,1,0:T(8,128)S(1)}, u32[]{:S(2)}, u32[]{:S(2)}) collective-permute-start(f32[4,4,16,128]{3,2,1,0:T(8,128)} %refs_1_.1), channel_id=1, source_target_pairs={{0,16},{8,24},{16,0},{24,8},{1,17},{9,25},{17,1},{25,9},{2,18},{10... | collective-permute-start | bytes 393224 | tf_op jit(solution)/shard_map/ppermute | solution.py:24
  5.6 1.8 %collective-permute-start.1 = (s32[4]{0:T(128)}, s32[4]{0:T(128)S(1)}, u32[]{:S(2)}, u32[]{:S(2)}) collective-permute-start(s32[4]{0:T(128)} %slots.1), channel_id=1, source_target_pairs={{0,1},{1,2},{2,3},{3,4},{4,5},{5,6},{6,7},{7,0},{8,9},{9,10},{10,1... | collective-permute-start | bytes 56 | tf_op jit(solution)/shard_map/ppermute | solution.py:431
  8.1 3.7 %make_plan.1 = (s32[1091]{0:T(1024)}, s32[772]{0:T(1024)}) custom-call(s32[1]{0:T(128)} %bitcast.me, s32[1]{0:T(128)} %bitcast.1.band, s32[3,48]{1,0:T(4,128)} %pattern.1, s32[1]{0:T(128)S(6)} %copy.8.live, s32[4]{0:T(128)} %slots.1), custom_call_target="tpu_custom_call" | custom-call | tf_op jit(solution)/shard_map/make_plan/pallas_call | solution.py:116
  11.8 1.9 %copy-done = f32[48,128,128]{2,1,0:T(8,128)S(1)} copy-done((f32[48,128,128]{2,1,0:T(8,128)S(1)}, f32[48,128,128]{2,1,0:T(8,128)}, u32[]{:S(2)}) %copy-start) | copy-done | bytes 3145752
  13.7 0.9 %copy-done.2 = f32[4,128,128]{2,1,0:T(8,128)S(1)} copy-done((f32[4,128,128]{2,1,0:T(8,128)S(1)}, f32[4,128,128]{2,1,0:T(8,128)}, u32[]{:S(2)}) %copy-start.2) | copy-done | bytes 262168
  14.6 0.7 %split_blocks.1 = (bf16[48,128,256]{2,1,0:T(8,128)(2,1)S(1)}, bf16[4,128,256]{2,1,0:T(8,128)(2,1)S(1)}) custom-call(f32[48,128,128]{2,1,0:T(8,128)S(1)} %copy-done, f32[4,128,128]{2,1,0:T(8,128)S(1)} %copy-done.2), custom_call_target="tpu_custom_call" | custom-call | flops 6291456 | bytes 6291456 | tf_op jit(solution)/shard_map/split_blocks/pallas_call | solution.py:154
  15.4 0.1 collective-permute-start.9
  15.5 0.1 copy-done.3
  15.5 1.5 %near_field.1.refs_1_ = f32[4,4,16,128]{3,2,1,0:T(8,128)S(1)} custom-call(s32[1091]{0:T(1024)S(1)} %copy-done.5, bf16[48,128,256]{2,1,0:T(8,128)(2,1)S(1)} %get-tuple-element.36.refs_0_.refs_1_.blocks, f32[4,4,16,128]{3,2,1,0:T(8,128)S(1)} %copy-done.3, f32[4,4,16,128]{3,2,1,0:T(8,128)S(1)} %collective-permute-done.refs_2_), custom_call_target="tpu_custom_call" | custom-call | flops 1 | bytes 1 | tf_op jit(solution)/shard_map/near_field/pallas_call | solution.py:230
  17.1 0.6 collective-permute-start.10
  17.7 1.0 %collective-permute-start.11 = (f32[4,4,16,128]{3,2,1,0:T(8,128)S(1)}, f32[4,4,16,128]{3,2,1,0:T(8,128)S(1)}, u32[]{:S(2)}, u32[]{:S(2)}) collective-permute-start(f32[4,4,16,128]{3,2,1,0:T(8,128)S(1)} %collective-permute-done.3.refs_3_), channel_id=1, source_target_pairs={{0,1},{1,2},{2,3},{3,4},{4,5},{5,6},{6,7},{7,0},{8,9},{9,10},{10,1... | collective-permute-start | bytes 393224 | tf_op jit(solution)/shard_map/ppermute | solution.py:439
  18.7 1.6 %far_field.1 = (f32[4,4,16,128]{3,2,1,0:T(8,128)S(1)}, f32[4,16,128]{2,1,0:T(8,128)S(1)}) custom-call(s32[1091]{0:T(1024)S(1)} %copy-done.5, bf16[48,128,256]{2,1,0:T(8,128)(2,1)S(1)} %get-tuple-element.36.refs_0_.refs_1_.blocks, f32[4,4,16,128]{3,2,1,0:T(8,128)S(1)} %near_field.1.refs_1_, f32[4,4,16,128]{3,2,1,0:T(8,128)S(1)} %collective-permute-done.2.refs_2_, ...), custom_call_target="tpu_custom_call" | custom-call | flops 1 | bytes 1 | tf_op jit(solution)/shard_map/far_field/pallas_call | solution.py:230
  20.3 0.8 %collective-permute-start.4 = (f32[4,16,128]{2,1,0:T(8,128)S(1)}, f32[4,16,128]{2,1,0:T(8,128)S(1)}, u32[]{:S(2)}, u32[]{:S(2)}) collective-permute-start(f32[4,16,128]{2,1,0:T(8,128)S(1)} %get-tuple-element.41), channel_id=1, source_target_pairs={{0,1},{1,0},{2,3},{3,2},{4,5},{5,4},{6,7},{7,6},{8,9},{9,8},{10,11... | collective-permute-start | bytes 98312 | tf_op jit(solution)/shard_map/ppermute | solution.py:24
  21.1 0.9 %collective-permute-done.4 = f32[4,16,128]{2,1,0:T(8,128)S(1)} collective-permute-done((f32[4,16,128]{2,1,0:T(8,128)S(1)}, f32[4,16,128]{2,1,0:T(8,128)S(1)}, u32[]{:S(2)}, u32[]{:S(2)}) %collective-permute-start.4) | collective-permute-done | bytes 32800 | tf_op jit(solution)/shard_map/ppermute | solution.py:24
  22.0 0.5 collective-permute-done.10.refs_5_
  22.5 1.4 %collective-permute-done.11.refs_6_ = f32[4,4,16,128]{3,2,1,0:T(8,128)S(1)} collective-permute-done((f32[4,4,16,128]{3,2,1,0:T(8,128)S(1)}, f32[4,4,16,128]{3,2,1,0:T(8,128)S(1)}, u32[]{:S(2)}, u32[]{:S(2)}) %collective-permute-start.11) | collective-permute-done | bytes 131104 | tf_op jit(solution)/shard_map/ppermute | solution.py:439
  23.9 0.7 late_field.1
  24.5 0.1 collective-permute-start.12
  24.6 1.6 %collective-permute-start.5 = (f32[4,16,128]{2,1,0:T(8,128)S(1)}, f32[4,16,128]{2,1,0:T(8,128)S(1)}, u32[]{:S(2)}, u32[]{:S(2)}) collective-permute-start(f32[4,16,128]{2,1,0:T(8,128)S(1)} %add.7.refs_0_), channel_id=1, source_target_pairs={{0,2},{1,3},{2,0},{3,1},{4,6},{5,7},{6,4},{7,5},{8,10},{9,11},{10,... | collective-permute-start | bytes 98312 | tf_op jit(solution)/shard_map/ppermute | solution.py:24
  26.2 1.2 %collective-permute-start.6 = (f32[4,16,128]{2,1,0:T(8,128)S(1)}, f32[4,16,128]{2,1,0:T(8,128)S(1)}, u32[]{:S(2)}, u32[]{:S(2)}) collective-permute-start(f32[4,16,128]{2,1,0:T(8,128)S(1)} %add.7.refs_0_), channel_id=1, source_target_pairs={{0,4},{1,5},{2,6},{3,7},{4,0},{5,1},{6,2},{7,3},{8,12},{9,13},{10,... | collective-permute-start | bytes 98312 | tf_op jit(solution)/shard_map/ppermute | solution.py:24
  27.3 0.9 %collective-permute-start.7 = (f32[4,16,128]{2,1,0:T(8,128)S(1)}, f32[4,16,128]{2,1,0:T(8,128)S(1)}, u32[]{:S(2)}, u32[]{:S(2)}) collective-permute-start(f32[4,16,128]{2,1,0:T(8,128)S(1)} %add.7.refs_0_), channel_id=1, source_target_pairs={{0,6},{1,7},{2,4},{3,5},{4,2},{5,3},{6,0},{7,1},{8,14},{9,15},{10,... | collective-permute-start | bytes 98312 | tf_op jit(solution)/shard_map/ppermute | solution.py:24
  28.3 0.1 collective-permute-start.13
  28.4 1.3 %collective-permute-start.14 = (f32[3,4,16,128]{3,2,1,0:T(8,128)S(1)}, f32[3,4,16,128]{3,2,1,0:T(8,128)S(1)}, u32[]{:S(2)}, u32[]{:S(2)}) collective-permute-start(f32[3,4,16,128]{3,2,1,0:T(8,128)S(1)} %add.8.refs_1_), channel_id=1, source_target_pairs={{0,1},{1,5},{2,3},{3,2},{4,0},{5,4},{6,7},{7,6},{8,9},{9,13},{10,1... | collective-permute-start | bytes 294920 | tf_op jit(solution)/shard_map/ppermute | solution.py:370
  29.7 0.9 %collective-permute-start.15 = (f32[3,4,16,128]{3,2,1,0:T(8,128)S(1)}, f32[3,4,16,128]{3,2,1,0:T(8,128)S(1)}, u32[]{:S(2)}, u32[]{:S(2)}) collective-permute-start(f32[3,4,16,128]{3,2,1,0:T(8,128)S(1)} %add.8.refs_1_), channel_id=1, source_target_pairs={{0,1},{1,3},{2,0},{3,2},{4,5},{5,4},{6,7},{7,6},{8,9},{9,11},{10,8... | collective-permute-start | bytes 294920 | tf_op jit(solution)/shard_map/ppermute | solution.py:370
  30.6 1.6 %collective-permute-done.7.refs_3_ = f32[4,16,128]{2,1,0:T(8,128)S(1)} collective-permute-done((f32[4,16,128]{2,1,0:T(8,128)S(1)}, f32[4,16,128]{2,1,0:T(8,128)S(1)}, u32[]{:S(2)}, u32[]{:S(2)}) %collective-permute-start.7) | collective-permute-done | bytes 32800 | tf_op jit(solution)/shard_map/ppermute | solution.py:24
  32.2 0.2 first_currents.1.refs_5_
  32.3 2.0 %collective-permute-start.16 = (f32[4,16,128]{2,1,0:T(8,128)S(1)}, f32[4,16,128]{2,1,0:T(8,128)S(1)}, u32[]{:S(2)}, u32[]{:S(2)}) collective-permute-start(f32[4,16,128]{2,1,0:T(8,128)S(1)} %first_currents.1.refs_5_), channel_id=1, source_target_pairs={{0,8},{1,2},{2,3},{3,4},{4,5},{5,6},{6,7},{7,1},{8,0},{9,10},{10,1... | collective-permute-start | bytes 98312 | tf_op jit(solution)/shard_map/ppermute | solution.py:427
  34.3 2.2 %collective-permute-start.17 = (f32[4,16,128]{2,1,0:T(8,128)S(1)}, f32[4,16,128]{2,1,0:T(8,128)S(1)}, u32[]{:S(2)}, u32[]{:S(2)}) collective-permute-start(f32[4,16,128]{2,1,0:T(8,128)S(1)} %first_currents.1.refs_5_), channel_id=1, source_target_pairs={{0,16},{1,2},{2,3},{3,4},{4,5},{5,6},{6,7},{7,1},{8,24},{9,10},{10... | collective-permute-start | bytes 98312 | tf_op jit(solution)/shard_map/ppermute | solution.py:427
  36.5 3.3 %collective-permute-start.18 = (f32[4,16,128]{2,1,0:T(8,128)S(1)}, f32[4,16,128]{2,1,0:T(8,128)S(1)}, u32[]{:S(2)}, u32[]{:S(2)}) collective-permute-start(f32[4,16,128]{2,1,0:T(8,128)S(1)} %first_currents.1.refs_5_), channel_id=1, source_target_pairs={{0,24},{1,2},{2,3},{3,4},{4,5},{5,6},{6,7},{7,1},{8,16},{9,10},{10... | collective-permute-start | bytes 98312 | tf_op jit(solution)/shard_map/ppermute | solution.py:427
  39.9 2.4 %collective-permute-done.18.refs_8_ = f32[4,16,128]{2,1,0:T(8,128)S(1)} collective-permute-done((f32[4,16,128]{2,1,0:T(8,128)S(1)}, f32[4,16,128]{2,1,0:T(8,128)S(1)}, u32[]{:S(2)}, u32[]{:S(2)}) %collective-permute-start.18) | collective-permute-done | bytes 32800 | tf_op jit(solution)/shard_map/ppermute | solution.py:427
  42.3 1.3 %next_currents.3 = (f32[4,16,128]{2,1,0:T(8,128)S(1)}, bf16[17,32,128]{2,1,0:T(8,128)(2,1)S(1)}) custom-call(s32[772]{0:T(1024)S(1)} %copy-done.4, bf16[48,128,256]{2,1,0:T(8,128)(2,1)S(1)} %get-tuple-element.36.refs_0_.refs_1_.blocks, bf16[4,128,256]{2,1,0:T(8,128)(2,1)S(1)} %get-tuple-element.34.inverse, f32[4,4,16,128]{3,2,1,0:T(8,128)S(1)} %copy-done.1, ...), custom_call_target="tpu_custom_call" | custom-call | flops 1 | bytes 1 | tf_op jit(solution)/shard_map/next_currents/pallas_call | solution.py:316
  43.5 3.9 %collective-permute-start.20 = (f32[4,16,128]{2,1,0:T(8,128)S(1)}, f32[4,16,128]{2,1,0:T(8,128)S(1)}, u32[]{:S(2)}, u32[]{:S(2)}) collective-permute-start(f32[4,16,128]{2,1,0:T(8,128)S(1)} %get-tuple-element.48.newest.refs_1_), channel_id=1, source_target_pairs={{0,16},{1,2},{2,3},{3,4},{4,5},{5,6},{6,7},{7,1},{8,24},{9,10},{10... | collective-permute-start | bytes 98312 | tf_op jit(solution)/shard_map/ppermute | solution.py:427
  47.5 0.5 collective-permute-start.21
  48.0 1.5 %older_field.2 = (f32[2,4,16,128]{3,2,1,0:T(8,128)S(1)}, f32[1,4,16,128]{3,2,1,0:T(8,128)S(1)}) custom-call(s32[772]{0:T(1024)S(1)} %copy-done.4, bf16[48,128,256]{2,1,0:T(8,128)(2,1)S(1)} %get-tuple-element.36.refs_0_.refs_1_.blocks, bf16[17,32,128]{2,1,0:T(8,128)(2,1)S(1)} %get-tuple-element.47.packed, f32[4,16,128]{2,1,0:T(8,128)S(1)} %get-tuple-element.48.newest.refs_1_, ...), custom_call_target="tpu_custom_call" | custom-call | flops 1 | bytes 1 | tf_op jit(solution)/shard_map/older_field/pallas_call | solution.py:345
  49.5 3.7 %collective-permute-done.21.refs_4_ = f32[4,16,128]{2,1,0:T(8,128)S(1)} collective-permute-done((f32[4,16,128]{2,1,0:T(8,128)S(1)}, f32[4,16,128]{2,1,0:T(8,128)S(1)}, u32[]{:S(2)}, u32[]{:S(2)}) %collective-permute-start.21) | collective-permute-done | bytes 32800 | tf_op jit(solution)/shard_map/ppermute | solution.py:427
  53.2 1.2 %next_currents.4 = (f32[4,16,128]{2,1,0:T(8,128)S(1)}, bf16[17,32,128]{2,1,0:T(8,128)(2,1)S(1)}) custom-call(s32[772]{0:T(1024)S(1)} %copy-done.4, bf16[48,128,256]{2,1,0:T(8,128)(2,1)S(1)} %get-tuple-element.36.refs_0_.refs_1_.blocks, bf16[4,128,256]{2,1,0:T(8,128)(2,1)S(1)} %get-tuple-element.34.inverse, f32[2,4,16,128]{3,2,1,0:T(8,128)S(1)} %get-tuple-element.49.refs_0_, ...), custom_call_target="tpu_custom_call" | custom-call | flops 1 | bytes 1 | tf_op jit(solution)/shard_map/next_currents/pallas_call | solution.py:316
  54.4 1.1 %collective-permute-start.23 = (f32[4,16,128]{2,1,0:T(8,128)S(1)}, f32[4,16,128]{2,1,0:T(8,128)S(1)}, u32[]{:S(2)}, u32[]{:S(2)}) collective-permute-start(f32[4,16,128]{2,1,0:T(8,128)S(1)} %get-tuple-element.51.newest.refs_2_), channel_id=1, source_target_pairs={{0,16},{1,2},{2,3},{3,4},{4,5},{5,6},{6,7},{7,1},{8,24},{9,10},{10... | collective-permute-start | bytes 98312 | tf_op jit(solution)/shard_map/ppermute | solution.py:427
  55.5 3.3 %collective-permute-start.24 = (f32[4,16,128]{2,1,0:T(8,128)S(1)}, f32[4,16,128]{2,1,0:T(8,128)S(1)}, u32[]{:S(2)}, u32[]{:S(2)}) collective-permute-start(f32[4,16,128]{2,1,0:T(8,128)S(1)} %get-tuple-element.51.newest.refs_2_), channel_id=1, source_target_pairs={{0,24},{1,2},{2,3},{3,4},{4,5},{5,6},{6,7},{7,1},{8,16},{9,10},{10... | collective-permute-start | bytes 98312 | tf_op jit(solution)/shard_map/ppermute | solution.py:427
  58.9 1.1 %older_field.3 = (f32[1,4,16,128]{3,2,1,0:T(8,128)S(1)}, f32[2,4,16,128]{3,2,1,0:T(8,128)S(1)}) custom-call(s32[772]{0:T(1024)S(1)} %copy-done.4, bf16[48,128,256]{2,1,0:T(8,128)(2,1)S(1)} %get-tuple-element.36.refs_0_.refs_1_.blocks, bf16[17,32,128]{2,1,0:T(8,128)(2,1)S(1)} %get-tuple-element.50.packed, f32[4,16,128]{2,1,0:T(8,128)S(1)} %get-tuple-element.51.newest.refs_2_, ...), custom_call_target="tpu_custom_call" | custom-call | flops 1 | bytes 1 | tf_op jit(solution)/shard_map/older_field/pallas_call | solution.py:345
  59.9 1.3 %collective-permute-done.24.refs_5_ = f32[4,16,128]{2,1,0:T(8,128)S(1)} collective-permute-done((f32[4,16,128]{2,1,0:T(8,128)S(1)}, f32[4,16,128]{2,1,0:T(8,128)S(1)}, u32[]{:S(2)}, u32[]{:S(2)}) %collective-permute-start.24) | collective-permute-done | bytes 32800 | tf_op jit(solution)/shard_map/ppermute | solution.py:427
  61.2 1.3 %next_currents.5 = f32[3,4,16,128]{3,2,1,0:T(8,128)S(1)} custom-call(s32[772]{0:T(1024)S(1)} %copy-done.4, bf16[48,128,256]{2,1,0:T(8,128)(2,1)S(1)} %get-tuple-element.36.refs_0_.refs_1_.blocks, bf16[4,128,256]{2,1,0:T(8,128)(2,1)S(1)} %get-tuple-element.34.inverse, f32[1,4,16,128]{3,2,1,0:T(8,128)S(1)} %get-tuple-element.53.refs_0_, ...), custom_call_target="tpu_custom_call" | custom-call | flops 1 | bytes 1 | tf_op jit(solution)/shard_map/next_currents/pallas_call | solution.py:316
  62.5 0.0 collective-permute-start.26
  62.5 0.1 collective-permute-start.27
  62.6 3.9 %collective-permute-done.25 = f32[3,4,16,128]{3,2,1,0:T(8,128)S(1)} collective-permute-done((f32[3,4,16,128]{3,2,1,0:T(8,128)S(1)}, f32[3,4,16,128]{3,2,1,0:T(8,128)S(1)}, u32[]{:S(2)}, u32[]{:S(2)}) %collective-permute-start.25) | collective-permute-done | bytes 98336 | tf_op jit(solution)/shard_map/ppermute | solution.py:406
  66.6 0.1 collective-permute-start.28
  66.7 1.3 %collective-permute-done.28 = f32[3,4,16,128]{3,2,1,0:T(8,128)S(1)} collective-permute-done((f32[3,4,16,128]{3,2,1,0:T(8,128)S(1)}, f32[3,4,16,128]{3,2,1,0:T(8,128)S(1)}, u32[]{:S(2)}, u32[]{:S(2)}) %collective-permute-start.28) | collective-permute-done | bytes 98336 | tf_op jit(solution)/shard_map/ppermute | solution.py:24
  68.0 0.7 pad_maximum_fusion
  (38 shorter events, 0.2 us)
Async XLA Ops:
  0.0 15.4 %collective-permute-start = (f32[4,4,16,128]{3,2,1,0:T(8,128)}, f32[4,4,16,128]{3,2,1,0:T(8,128)S(1)}, u32[]{:S(2)}, u32[]{:S(2)}) collective-permute-start(f32[4,4,16,128]{3,2,1,0:T(8,128)} %refs_1_.1), channel_id=1, source_target_pairs={{0,8},{8,0},{16,24},{24,16},{1,9},{9,1},{17,25},{25,17},{2,10},{10... | collective-permute-start | bytes 393224 | tf_op jit(solution)/shard_map/ppermute | solution.py:24
  3.0 14.1 %collective-permute-start.2 = (f32[4,4,16,128]{3,2,1,0:T(8,128)}, f32[4,4,16,128]{3,2,1,0:T(8,128)S(1)}, u32[]{:S(2)}, u32[]{:S(2)}) collective-permute-start(f32[4,4,16,128]{3,2,1,0:T(8,128)} %refs_1_.1), channel_id=1, source_target_pairs={{0,16},{8,24},{16,0},{24,8},{1,17},{9,25},{17,1},{25,9},{2,18},{10... | collective-permute-start | bytes 393224 | tf_op jit(solution)/shard_map/ppermute | solution.py:24
  5.6 11.5 %collective-permute-start.3 = (f32[4,4,16,128]{3,2,1,0:T(8,128)}, f32[4,4,16,128]{3,2,1,0:T(8,128)S(1)}, u32[]{:S(2)}, u32[]{:S(2)}) collective-permute-start(f32[4,4,16,128]{3,2,1,0:T(8,128)} %refs_1_.1), channel_id=1, source_target_pairs={{0,24},{8,16},{16,8},{24,0},{1,25},{9,17},{17,9},{25,1},{2,26},{10... | collective-permute-start | bytes 393224 | tf_op jit(solution)/shard_map/ppermute | solution.py:24
  5.6 16.4 %collective-permute-start.8 = (f32[4,4,16,128]{3,2,1,0:T(8,128)}, f32[4,4,16,128]{3,2,1,0:T(8,128)S(1)}, u32[]{:S(2)}, u32[]{:S(2)}) collective-permute-start(f32[4,4,16,128]{3,2,1,0:T(8,128)} %refs_1_.1), channel_id=1, source_target_pairs={{0,1},{1,2},{2,3},{3,4},{4,5},{5,6},{6,7},{7,0},{8,9},{9,10},{10,1... | collective-permute-start | bytes 393224 | tf_op jit(solution)/shard_map/ppermute | solution.py:439
  5.6 9.8 %collective-permute-start.1 = (s32[4]{0:T(128)}, s32[4]{0:T(128)S(1)}, u32[]{:S(2)}, u32[]{:S(2)}) collective-permute-start(s32[4]{0:T(128)} %slots.1), channel_id=1, source_target_pairs={{0,1},{1,2},{2,3},{3,4},{4,5},{5,6},{6,7},{7,0},{8,9},{9,10},{10,1... | collective-permute-start | bytes 56 | tf_op jit(solution)/shard_map/ppermute | solution.py:431
  11.8 1.9 %copy-start = (f32[48,128,128]{2,1,0:T(8,128)S(1)}, f32[48,128,128]{2,1,0:T(8,128)}, u32[]{:S(2)}) copy-start(f32[48,128,128]{2,1,0:T(8,128)} %blocks.1) | copy-start | bytes 9437188
  13.7 0.9 %copy-start.2 = (f32[4,128,128]{2,1,0:T(8,128)S(1)}, f32[4,128,128]{2,1,0:T(8,128)}, u32[]{:S(2)}) copy-start(f32[4,128,128]{2,1,0:T(8,128)} %inverse.1) | copy-start | bytes 786436
  14.6 0.9 %copy-start.3 = (f32[4,4,16,128]{3,2,1,0:T(8,128)S(1)}, f32[4,4,16,128]{3,2,1,0:T(8,128)}, u32[]{:S(2)}) copy-start(f32[4,4,16,128]{3,2,1,0:T(8,128)} %refs_1_.1) | copy-start | bytes 393220
  14.6 0.9 %copy-start.5 = (s32[1091]{0:T(1024)S(1)}, s32[1091]{0:T(1024)}, u32[]{:S(2)}) copy-start(s32[1091]{0:T(1024)} %get-tuple-element.35.plan) | copy-start | bytes 13096
  15.4 6.6 %collective-permute-start.9 = (f32[4,4,16,128]{3,2,1,0:T(8,128)S(1)}, f32[4,4,16,128]{3,2,1,0:T(8,128)S(1)}, u32[]{:S(2)}, u32[]{:S(2)}) collective-permute-start(f32[4,4,16,128]{3,2,1,0:T(8,128)S(1)} %collective-permute-done.refs_2_), channel_id=1, source_target_pairs={{0,1},{1,2},{2,3},{3,4},{4,5},{5,6},{6,7},{7,0},{8,9},{9,10},{10,1... | collective-permute-start | bytes 393224 | tf_op jit(solution)/shard_map/ppermute | solution.py:439
  17.1 15.1 %copy-start.1 = (f32[4,4,16,128]{3,2,1,0:T(8,128)S(1)}, f32[4,4,16,128]{3,2,1,0:T(8,128)}, u32[]{:S(2)}) copy-start(f32[4,4,16,128]{3,2,1,0:T(8,128)} %refs_0_.3) | copy-start | bytes 393220
  17.1 5.3 %collective-permute-start.10 = (f32[4,4,16,128]{3,2,1,0:T(8,128)S(1)}, f32[4,4,16,128]{3,2,1,0:T(8,128)S(1)}, u32[]{:S(2)}, u32[]{:S(2)}) collective-permute-start(f32[4,4,16,128]{3,2,1,0:T(8,128)S(1)} %collective-permute-done.2.refs_2_), channel_id=1, source_target_pairs={{0,1},{1,2},{2,3},{3,4},{4,5},{5,6},{6,7},{7,0},{8,9},{9,10},{10,1... | collective-permute-start | bytes 393224 | tf_op jit(solution)/shard_map/ppermute | solution.py:439
  17.7 6.1 %collective-permute-start.11 = (f32[4,4,16,128]{3,2,1,0:T(8,128)S(1)}, f32[4,4,16,128]{3,2,1,0:T(8,128)S(1)}, u32[]{:S(2)}, u32[]{:S(2)}) collective-permute-start(f32[4,4,16,128]{3,2,1,0:T(8,128)S(1)} %collective-permute-done.3.refs_3_), channel_id=1, source_target_pairs={{0,1},{1,2},{2,3},{3,4},{4,5},{5,6},{6,7},{7,0},{8,9},{9,10},{10,1... | collective-permute-start | bytes 393224 | tf_op jit(solution)/shard_map/ppermute | solution.py:439
  20.3 22.0 %copy-start.4 = (s32[772]{0:T(1024)S(1)}, s32[772]{0:T(1024)}, u32[]{:S(2)}) copy-start(s32[772]{0:T(1024)} %get-tuple-element.44.plan) | copy-start | bytes 9268
  20.3 1.7 %collective-permute-start.4 = (f32[4,16,128]{2,1,0:T(8,128)S(1)}, f32[4,16,128]{2,1,0:T(8,128)S(1)}, u32[]{:S(2)}, u32[]{:S(2)}) collective-permute-start(f32[4,16,128]{2,1,0:T(8,128)S(1)} %get-tuple-element.41), channel_id=1, source_target_pairs={{0,1},{1,0},{2,3},{3,2},{4,5},{5,4},{6,7},{7,6},{8,9},{9,8},{10,11... | collective-permute-start | bytes 98312 | tf_op jit(solution)/shard_map/ppermute | solution.py:24
  24.5 3.7 %collective-permute-start.12 = (f32[3,4,16,128]{3,2,1,0:T(8,128)S(1)}, f32[3,4,16,128]{3,2,1,0:T(8,128)S(1)}, u32[]{:S(2)}, u32[]{:S(2)}) collective-permute-start(f32[3,4,16,128]{3,2,1,0:T(8,128)S(1)} %late_field.1), channel_id=1, source_target_pairs={{0,1},{1,0},{2,3},{3,2},{4,5},{5,4},{6,7},{7,6},{8,9},{9,8},{10,11... | collective-permute-start | bytes 294920 | tf_op jit(solution)/shard_map/ppermute | solution.py:24
  24.6 5.0 %collective-permute-start.5 = (f32[4,16,128]{2,1,0:T(8,128)S(1)}, f32[4,16,128]{2,1,0:T(8,128)S(1)}, u32[]{:S(2)}, u32[]{:S(2)}) collective-permute-start(f32[4,16,128]{2,1,0:T(8,128)S(1)} %add.7.refs_0_), channel_id=1, source_target_pairs={{0,2},{1,3},{2,0},{3,1},{4,6},{5,7},{6,4},{7,5},{8,10},{9,11},{10,... | collective-permute-start | bytes 98312 | tf_op jit(solution)/shard_map/ppermute | solution.py:24
  26.2 4.4 %collective-permute-start.6 = (f32[4,16,128]{2,1,0:T(8,128)S(1)}, f32[4,16,128]{2,1,0:T(8,128)S(1)}, u32[]{:S(2)}, u32[]{:S(2)}) collective-permute-start(f32[4,16,128]{2,1,0:T(8,128)S(1)} %add.7.refs_0_), channel_id=1, source_target_pairs={{0,4},{1,5},{2,6},{3,7},{4,0},{5,1},{6,2},{7,3},{8,12},{9,13},{10,... | collective-permute-start | bytes 98312 | tf_op jit(solution)/shard_map/ppermute | solution.py:24
  27.3 4.8 %collective-permute-start.7 = (f32[4,16,128]{2,1,0:T(8,128)S(1)}, f32[4,16,128]{2,1,0:T(8,128)S(1)}, u32[]{:S(2)}, u32[]{:S(2)}) collective-permute-start(f32[4,16,128]{2,1,0:T(8,128)S(1)} %add.7.refs_0_), channel_id=1, source_target_pairs={{0,6},{1,7},{2,4},{3,5},{4,2},{5,3},{6,0},{7,1},{8,14},{9,15},{10,... | collective-permute-start | bytes 98312 | tf_op jit(solution)/shard_map/ppermute | solution.py:24
  28.3 14.0 %collective-permute-start.13 = (f32[3,4,16,128]{3,2,1,0:T(8,128)S(1)}, f32[3,4,16,128]{3,2,1,0:T(8,128)S(1)}, u32[]{:S(2)}, u32[]{:S(2)}) collective-permute-start(f32[3,4,16,128]{3,2,1,0:T(8,128)S(1)} %add.8.refs_1_), channel_id=1, source_target_pairs={{0,1},{1,7},{2,3},{3,2},{4,5},{5,4},{6,0},{7,6},{8,9},{9,15},{10,1... | collective-permute-start | bytes 294920 | tf_op jit(solution)/shard_map/ppermute | solution.py:370
  28.4 13.9 %collective-permute-start.14 = (f32[3,4,16,128]{3,2,1,0:T(8,128)S(1)}, f32[3,4,16,128]{3,2,1,0:T(8,128)S(1)}, u32[]{:S(2)}, u32[]{:S(2)}) collective-permute-start(f32[3,4,16,128]{3,2,1,0:T(8,128)S(1)} %add.8.refs_1_), channel_id=1, source_target_pairs={{0,1},{1,5},{2,3},{3,2},{4,0},{5,4},{6,7},{7,6},{8,9},{9,13},{10,1... | collective-permute-start | bytes 294920 | tf_op jit(solution)/shard_map/ppermute | solution.py:370
  29.7 12.6 %collective-permute-start.15 = (f32[3,4,16,128]{3,2,1,0:T(8,128)S(1)}, f32[3,4,16,128]{3,2,1,0:T(8,128)S(1)}, u32[]{:S(2)}, u32[]{:S(2)}) collective-permute-start(f32[3,4,16,128]{3,2,1,0:T(8,128)S(1)} %add.8.refs_1_), channel_id=1, source_target_pairs={{0,1},{1,3},{2,0},{3,2},{4,5},{5,4},{6,7},{7,6},{8,9},{9,11},{10,8... | collective-permute-start | bytes 294920 | tf_op jit(solution)/shard_map/ppermute | solution.py:370
  32.3 4.2 %collective-permute-start.16 = (f32[4,16,128]{2,1,0:T(8,128)S(1)}, f32[4,16,128]{2,1,0:T(8,128)S(1)}, u32[]{:S(2)}, u32[]{:S(2)}) collective-permute-start(f32[4,16,128]{2,1,0:T(8,128)S(1)} %first_currents.1.refs_5_), channel_id=1, source_target_pairs={{0,8},{1,2},{2,3},{3,4},{4,5},{5,6},{6,7},{7,1},{8,0},{9,10},{10,1... | collective-permute-start | bytes 98312 | tf_op jit(solution)/shard_map/ppermute | solution.py:427
  34.3 5.6 %collective-permute-start.17 = (f32[4,16,128]{2,1,0:T(8,128)S(1)}, f32[4,16,128]{2,1,0:T(8,128)S(1)}, u32[]{:S(2)}, u32[]{:S(2)}) collective-permute-start(f32[4,16,128]{2,1,0:T(8,128)S(1)} %first_currents.1.refs_5_), channel_id=1, source_target_pairs={{0,16},{1,2},{2,3},{3,4},{4,5},{5,6},{6,7},{7,1},{8,24},{9,10},{10... | collective-permute-start | bytes 98312 | tf_op jit(solution)/shard_map/ppermute | solution.py:427
  36.5 5.7 %collective-permute-start.18 = (f32[4,16,128]{2,1,0:T(8,128)S(1)}, f32[4,16,128]{2,1,0:T(8,128)S(1)}, u32[]{:S(2)}, u32[]{:S(2)}) collective-permute-start(f32[4,16,128]{2,1,0:T(8,128)S(1)} %first_currents.1.refs_5_), channel_id=1, source_target_pairs={{0,24},{1,2},{2,3},{3,4},{4,5},{5,6},{6,7},{7,1},{8,16},{9,10},{10... | collective-permute-start | bytes 98312 | tf_op jit(solution)/shard_map/ppermute | solution.py:427
  43.5 6.0 %collective-permute-start.19 = (f32[4,16,128]{2,1,0:T(8,128)S(1)}, f32[4,16,128]{2,1,0:T(8,128)S(1)}, u32[]{:S(2)}, u32[]{:S(2)}) collective-permute-start(f32[4,16,128]{2,1,0:T(8,128)S(1)} %get-tuple-element.48.newest.refs_1_), channel_id=1, source_target_pairs={{0,8},{1,2},{2,3},{3,4},{4,5},{5,6},{6,7},{7,1},{8,0},{9,10},{10,1... | collective-permute-start | bytes 98312 | tf_op jit(solution)/shard_map/ppermute | solution.py:427
  43.5 6.0 %collective-permute-start.20 = (f32[4,16,128]{2,1,0:T(8,128)S(1)}, f32[4,16,128]{2,1,0:T(8,128)S(1)}, u32[]{:S(2)}, u32[]{:S(2)}) collective-permute-start(f32[4,16,128]{2,1,0:T(8,128)S(1)} %get-tuple-element.48.newest.refs_1_), channel_id=1, source_target_pairs={{0,16},{1,2},{2,3},{3,4},{4,5},{5,6},{6,7},{7,1},{8,24},{9,10},{10... | collective-permute-start | bytes 98312 | tf_op jit(solution)/shard_map/ppermute | solution.py:427
  47.5 5.7 %collective-permute-start.21 = (f32[4,16,128]{2,1,0:T(8,128)S(1)}, f32[4,16,128]{2,1,0:T(8,128)S(1)}, u32[]{:S(2)}, u32[]{:S(2)}) collective-permute-start(f32[4,16,128]{2,1,0:T(8,128)S(1)} %get-tuple-element.48.newest.refs_1_), channel_id=1, source_target_pairs={{0,24},{1,2},{2,3},{3,4},{4,5},{5,6},{6,7},{7,1},{8,16},{9,10},{10... | collective-permute-start | bytes 98312 | tf_op jit(solution)/shard_map/ppermute | solution.py:427
  54.4 5.5 %collective-permute-start.22 = (f32[4,16,128]{2,1,0:T(8,128)S(1)}, f32[4,16,128]{2,1,0:T(8,128)S(1)}, u32[]{:S(2)}, u32[]{:S(2)}) collective-permute-start(f32[4,16,128]{2,1,0:T(8,128)S(1)} %get-tuple-element.51.newest.refs_2_), channel_id=1, source_target_pairs={{0,8},{1,2},{2,3},{3,4},{4,5},{5,6},{6,7},{7,1},{8,0},{9,10},{10,1... | collective-permute-start | bytes 98312 | tf_op jit(solution)/shard_map/ppermute | solution.py:427
  54.4 5.5 %collective-permute-start.23 = (f32[4,16,128]{2,1,0:T(8,128)S(1)}, f32[4,16,128]{2,1,0:T(8,128)S(1)}, u32[]{:S(2)}, u32[]{:S(2)}) collective-permute-start(f32[4,16,128]{2,1,0:T(8,128)S(1)} %get-tuple-element.51.newest.refs_2_), channel_id=1, source_target_pairs={{0,16},{1,2},{2,3},{3,4},{4,5},{5,6},{6,7},{7,1},{8,24},{9,10},{10... | collective-permute-start | bytes 98312 | tf_op jit(solution)/shard_map/ppermute | solution.py:427
  55.5 5.7 %collective-permute-start.24 = (f32[4,16,128]{2,1,0:T(8,128)S(1)}, f32[4,16,128]{2,1,0:T(8,128)S(1)}, u32[]{:S(2)}, u32[]{:S(2)}) collective-permute-start(f32[4,16,128]{2,1,0:T(8,128)S(1)} %get-tuple-element.51.newest.refs_2_), channel_id=1, source_target_pairs={{0,24},{1,2},{2,3},{3,4},{4,5},{5,6},{6,7},{7,1},{8,16},{9,10},{10... | collective-permute-start | bytes 98312 | tf_op jit(solution)/shard_map/ppermute | solution.py:427
  62.5 4.1 %collective-permute-start.25 = (f32[3,4,16,128]{3,2,1,0:T(8,128)S(1)}, f32[3,4,16,128]{3,2,1,0:T(8,128)S(1)}, u32[]{:S(2)}, u32[]{:S(2)}) collective-permute-start(f32[3,4,16,128]{3,2,1,0:T(8,128)S(1)} %next_currents.5), channel_id=1, source_target_pairs={{0,2},{2,3},{3,0},{1,5},{5,1},{4,6},{6,7},{7,4},{8,10},{10,11},{11... | collective-permute-start | bytes 294920 | tf_op jit(solution)/shard_map/ppermute | solution.py:406
  62.5 4.1 %collective-permute-start.26 = (f32[3,4,16,128]{3,2,1,0:T(8,128)S(1)}, f32[3,4,16,128]{3,2,1,0:T(8,128)S(1)}, u32[]{:S(2)}, u32[]{:S(2)}) collective-permute-start(f32[3,4,16,128]{3,2,1,0:T(8,128)S(1)} %next_currents.5), channel_id=1, source_target_pairs={{0,4},{4,5},{5,0},{1,7},{7,1},{2,3},{3,6},{6,2},{8,12},{12,13},{13... | collective-permute-start | bytes 294920 | tf_op jit(solution)/shard_map/ppermute | solution.py:406
  62.5 4.0 %collective-permute-start.27 = (f32[3,4,16,128]{3,2,1,0:T(8,128)S(1)}, f32[3,4,16,128]{3,2,1,0:T(8,128)S(1)}, u32[]{:S(2)}, u32[]{:S(2)}) collective-permute-start(f32[3,4,16,128]{3,2,1,0:T(8,128)S(1)} %next_currents.5), channel_id=1, source_target_pairs={{0,6},{6,7},{7,1},{1,0},{2,3},{3,2},{4,5},{5,4},{8,14},{14,15},{15... | collective-permute-start | bytes 294920 | tf_op jit(solution)/shard_map/ppermute | solution.py:406
  66.6 1.4 %collective-permute-start.28 = (f32[3,4,16,128]{3,2,1,0:T(8,128)S(1)}, f32[3,4,16,128]{3,2,1,0:T(8,128)S(1)}, u32[]{:S(2)}, u32[]{:S(2)}) collective-permute-start(f32[3,4,16,128]{3,2,1,0:T(8,128)S(1)} %select_select_fusion), channel_id=1, source_target_pairs={{0,1},{1,0},{2,3},{3,2},{4,5},{5,4},{6,7},{7,6},{8,9},{9,8},{10,11... | collective-permute-start | bytes 294920 | tf_op jit(solution)/shard_map/ppermute | solution.py:24

commit v4 on v3

--- a/solution.py
+++ b/solution.py
@@ -44,83 +44,102 @@
     return (pairs + UNROLL - 1) // UNROLL * UNROLL + UNROLL
 
 
-def plan_kernel(groups, group_blocks, steps, me, band, pattern, live, slots, past, newer, held, count):
+def plan_kernel(groups, group_blocks, steps, me, band, pattern, live, slots, near, far, late, later, newest, older, held, count):
     places = slots.shape[0]
     size = room(pattern.shape[1])
     cells = places * group_blocks
     for d in range(places):
         held[d] = sum(jnp.where(slots[j] == d, j, 0) for j in range(places))
         count[d] = 0
-    wide_entry, late_entry, late_start = 2 + steps, 1 + steps, 3 + 2 * size * (2 + steps)
+
+    def put(ref, to, e, row, cell):
+        ref[to] = e
+        ref[to + 1] = row
+        for t in range(len(cell)):
+            ref[to + 2 + t] = cell[t]
+
+    def put_newer(d, n, e, row, cell):
+        @pl.when(d == 0)
+        def _():
+            put(newest, 1 + n * 3, e, row, [cell])
+
+        @pl.when(d != 0)
+        def _():
+            put(older, places - 1 + ((d - 1) * size + n) * 3, e, row, [cell])
 
     def place(e, taken):
-        near, few = taken
+        n_near, n_far, n_late, n_later = taken
         row, column, d = pattern[0, e], pattern[1, e], pattern[2, e]
         group = (column // group_blocks) ^ me[0]
         block = column % group_blocks
         is_far = (group >= 2).astype(jnp.int32)
-        to = 3 + (is_far * size + jnp.where(is_far == 1, e - near, near)) * wide_entry
-        past[to] = e
-        past[to + 1] = row
-        for t in range(steps):
-            at = ((group - 2 * is_far) * places + held[jnp.maximum(d - t, 0)]) * group_blocks + block
-            nothing = jnp.where(is_far == 1, (groups - 2) * cells, 2 * cells)
-            past[to + 2 + t] = jnp.where(d >= t, at, nothing)
-        to = late_start + few * late_entry
-        past[to] = e
-        past[to + 1] = row
-        for t in range(1, steps):
-            at = (group * places + d - t + places) * group_blocks + block
-            past[to + 1 + t] = jnp.where(d < t, at, groups * cells)
+        nothing = jnp.where(is_far == 1, (groups - 2) * cells, 2 * cells)
+        cell = [
+            jnp.where(
+                d >= t, ((group - 2 * is_far) * places + held[jnp.maximum(d - t, 0)]) * group_blocks + block, nothing
+            )
+            for t in range(steps)
+        ]
+
+        @pl.when(is_far == 0)
+        def _():
+            put(near, 1 + n_near * (2 + steps), e, row, cell)
+
+        @pl.when(is_far == 1)
+        def _():
+            put(far, 1 + n_far * (2 + steps), e, row, cell)
+
+        before = [
+            jnp.where(d < t, ((group - 2 * is_far) * places + d - t + places) * group_blocks + block, nothing)
+            for t in range(1, steps)
+        ]
+
+        @pl.when(is_far == 0)
+        def _():
+            put(late, 1 + n_late * (1 + steps), e, row, before)
+
+        @pl.when(is_far == 1)
+        def _():
+            put(later, 1 + n_later * (1 + steps), e, row, before)
+
         n = count[d]
         count[d] = n + 1
-        to = places + (d * size + n) * 3
-        newer[to] = e
-        newer[to + 1] = row
-        newer[to + 2] = group * group_blocks + block
-        return near + 1 - is_far, few + (d < steps - 1).astype(jnp.int32)
-
-    near, few = lax.fori_loop(0, live[0], place, (jnp.int32(0), jnp.int32(0)))
-    far = live[0] - near
-    past[0] = near
-    past[1] = far
-    past[2] = jnp.where(band[0] == 0, 0, few)
+        put_newer(d, n, e, row, group * group_blocks + block)
+        reads = (d < steps - 1).astype(jnp.int32)
+        return n_near + 1 - is_far, n_far + is_far, n_late + reads * (1 - is_far), n_later + reads * is_far
+
+    zero = jnp.int32(0)
+    n_near, n_far, n_late, n_later = lax.fori_loop(0, live[0], place, (zero, zero, zero, zero))
+    near[0] = n_near
+    far[0] = n_far
+    late[0] = jnp.where(band[0] == 0, 0, n_late)
+    later[0] = jnp.where(band[0] == 0, 0, n_later)
 
     def fill(i, c):
-        for k, n, nothing in ((0, near, 2 * cells), (1, far, (groups - 2) * cells)):
-            to = 3 + (k * size + n + i) * wide_entry
-            past[to] = 0
-            past[to + 1] = 0
-            for t in range(steps):
-                past[to + 2 + t] = nothing
-        to = late_start + (few + i) * late_entry
-        past[to] = 0
-        past[to + 1] = 0
-        for t in range(1, steps):
-            past[to + 1 + t] = groups * cells
-        for d in range(places):
-            to = places + (d * size + count[d] + i) * 3
-            newer[to] = 0
-            newer[to + 1] = 0
-            newer[to + 2] = groups * group_blocks
+        put(near, 1 + (n_near + i) * (2 + steps), 0, 0, [2 * cells] * steps)
+        put(far, 1 + (n_far + i) * (2 + steps), 0, 0, [(groups - 2) * cells] * steps)
+        put(late, 1 + (n_late + i) * (1 + steps), 0, 0, [2 * cells] * (steps - 1))
+        put(later, 1 + (n_later + i) * (1 + steps), 0, 0, [(groups - 2) * cells] * (steps - 1))
+        put(newest, 1 + (count[0] + i) * 3, 0, 0, [groups * group_blocks])
+        for d in range(1, places):
+            put(older, places - 1 + ((d - 1) * size + count[d] + i) * 3, 0, 0, [groups * group_blocks])
         return c
 
     lax.fori_loop(0, UNROLL, fill, 0)
-    for d in range(places):
-        newer[d] = jnp.where(band[0] == 0, count[d], 0)
+    newest[0] = jnp.where(band[0] == 0, count[0], 0)
+    for d in range(1, places):
+        older[d - 1] = jnp.where(band[0] == 0, count[d], 0)
 
 
 def make_plan(groups, group_blocks, steps, me, band, pattern, live, slots):
     places = slots.shape[0]
     size = room(pattern.shape[1])
+    lengths = [1 + size * (2 + steps)] * 2 + [1 + size * (1 + steps)] * 2 + [1 + size * 3, (places - 1) * (1 + size * 3)]
     return pl.pallas_call(
         functools.partial(plan_kernel, groups, group_blocks, steps),
         in_specs=[whole(SMEM)] * 5,
-        out_specs=[whole(SMEM)] * 2,
-        out_shape=[
-            jax.ShapeDtypeStruct((3 + size * (2 * (2 + steps) + 1 + steps),), jnp.int32),
-            jax.ShapeDtypeStruct((places + places * size * 3,), jnp.int32),
-        ],
+        out_specs=[whole(SMEM)] * len(lengths),
+        out_shape=[jax.ShapeDtypeStruct((n,), jnp.int32) for n in lengths],
         scratch_shapes=[SMEM((places,), jnp.int32), SMEM((places,), jnp.int32)],
         name="make_plan",
     )(me, band, pattern, live, slots)
@@ -195,25 +214,21 @@
         out[...] = base[...]
     else:
         slots, blocks, base, *parts, out, packed = refs
-        out[...] = base[1:]
+        out[...] = base[1:] if when == "late" else base[...]
     places, group_blocks, columns, width = parts[0].shape
     cells = places * group_blocks
     for k in range(len(parts)):
-        if when == "late":
+        if when in ("late", "later"):
             for j in range(places):
                 pack(packed, (k * places + slots[j]) * group_blocks, parts[k][j])
         else:
             pack(packed, k * cells, parts[k][...].reshape(cells, columns, width))
     packed[len(parts) * cells] = jnp.zeros((2 * columns, width), BF16)
-    size = room(blocks.shape[0])
-    which = ("near", "far", "late").index(when)
-    entry = 2 + out.shape[0]
-    start = 3 + which * size * (entry + which // 2)
 
     def add(row, y):
         out[:, row] += y
 
-    batches(plan, start, entry, plan[which], packed, blocks, add)
+    batches(plan, 1, 2 + out.shape[0], plan[0], packed, blocks, add)
     if when == "far":
         now[...] = out[0]
 
@@ -222,10 +237,10 @@
     places, group_blocks, columns, width = parts[0].shape
     shape = (group_blocks, columns, width)
     packed = VMEM((len(parts) * places * group_blocks + 1, 2 * columns, width), BF16)
-    out = [jax.ShapeDtypeStruct((steps - (when == "late"),) + shape, F32)]
+    out = [jax.ShapeDtypeStruct((steps - (when in ("late", "later")),) + shape, F32)]
     if when == "far":
         out.append(jax.ShapeDtypeStruct(shape, F32))
-    scalars = [plan] + [slots] * (when == "late")
+    scalars = [plan] + [slots] * (when in ("late", "later"))
     given = [blocks] + [base] * (when != "near")
     return pl.pallas_call(
         functools.partial(past_kernel, when),
@@ -273,18 +288,13 @@
     )(inverse, incident, *terms)
 
 
-def recent(kind, plan, places, packed, blocks, add):
-    start = places + kind * room(blocks.shape[0]) * 3
-    batches(plan, start, 3, plan[kind], packed, blocks, lambda row, y: add(row, y[0]))
-
-
 def right_side(rights, t):
     if len(rights) == 1:
         return rights[0][t]
     return rights[0][t + 1] - summed(rights[1:], t)
 
 
-def step_kernel(places, count, done, plan, blocks, inverse, *refs):
+def step_kernel(count, done, plan, blocks, inverse, *refs):
     rights, refs = refs[:count], refs[count:]
     earlier, parts, (out, packed, right) = refs[:done], refs[done:-3], refs[-3:]
     group_blocks, columns, width = right.shape
@@ -296,7 +306,7 @@
     def add(row, y):
         right[row] -= y
 
-    recent(0, plan, places, packed, blocks, add)
+    batches(plan, 1, 3, plan[0], packed, blocks, lambda row, y: add(row, y[0]))
     if done:
         last = out.shape[0] - 1
         out[:last] = earlier[0][...]
@@ -304,7 +314,7 @@
     solve(inverse, right, out)
 
 
-def next_currents(places, plan, blocks, inverse, rights, parts, earlier=None):
+def next_currents(plan, blocks, inverse, rights, parts, earlier=None):
     shape = parts[0].shape
     packed = (len(parts) * shape[0] + 1, 2 * shape[1], shape[2])
     scratch = [VMEM(shape, F32)]
@@ -314,7 +324,7 @@
         given, out = [earlier], [jax.ShapeDtypeStruct((earlier.shape[0] + 1,) + shape, F32)]
         scratch.insert(0, VMEM(packed, BF16))
     return pl.pallas_call(
-        functools.partial(step_kernel, places, len(rights), len(given)),
+        functools.partial(step_kernel, len(rights), len(given)),
         in_specs=[whole(SMEM)] + [whole(VMEM)] * (2 + len(rights) + len(given) + len(parts)),
         out_specs=[whole(VMEM)] * len(out),
         out_shape=out,
@@ -336,7 +346,8 @@
         def add(row, y):
             out[t, row] -= y
 
-        recent(t + 1, plan, places, packed, blocks, add)
+        start = places - 1 + t * room(blocks.shape[0]) * 3
+        batches(plan, start, 3, plan[t], packed, blocks, lambda row, y: add(row, y[0]))
 
 
 def older_field(places, steps, plan, blocks, packed, newest, rights, earlier):
@@ -356,7 +367,7 @@
 def summands(x):
     bands = lax.axis_size("delay")
     if bands <= 8:
-        return [x] + [swap(x, "delay", k) for k in range(2, bands, 2)]
+        return [x] + [swap(x, "delay", k) for k in range(bands - 2, 0, -2)]
     return [doubled(x)]
 
 
@@ -430,17 +441,19 @@
     ring = [(i, (i + 1) % bands) for i in range(bands)]
     slots_before = lax.ppermute(slot_map, "delay", ring)
     blocks, inverse = split_blocks(interaction, near_inverse)
-    past, newer = make_plan(groups, history.shape[1], moments, me, band, pattern, live, slot_map)
-    parts[1], slots_before, past, newer, blocks, inverse = lax.optimization_barrier(
-        (parts[1], slots_before, past, newer, blocks, inverse)
+    plan = make_plan(groups, history.shape[1], moments, me, band, pattern, live, slot_map)
+    parts[1], slots_before, plan, blocks, inverse = lax.optimization_barrier(
+        (parts[1], slots_before, plan, blocks, inverse)
     )
-    (field,) = past_field("near", moments, past, blocks, parts[:2])
+    near_list, far_list, late_list, later_list, newest_list, older_list = plan
+    (field,) = past_field("near", moments, near_list, blocks, parts[:2])
     field, parts[2:] = lax.optimization_barrier((field, parts[2:]))
     before = [lax.ppermute(p, "delay", ring) for p in parts]
-    field, now = past_field("far", moments, past, blocks, parts[2:], field)
+    field, now = past_field("far", moments, far_list, blocks, parts[2:], field)
     now = now + swap(now, "delay", 1)
     now, field = lax.optimization_barrier((now, field))
-    (later,) = past_field("late", moments, past, blocks, before, field, slots_before)
+    (later,) = past_field("late", moments, late_list, blocks, before[:2], field, slots_before)
+    (later,) = past_field("later", moments, later_list, blocks, before[2:], later, slots_before)
     first = newest = first_currents(inverse, incident, summands(now))
     earlier = None
     for moment in range(1, moments):
@@ -449,11 +462,11 @@
             rights = [incident] + front_summands(later + swap(later, "delay", 1))
         else:
             rights, earlier = older_field(
-                slot_count, moments - moment, newer, blocks, packed, newest, rights, earlier
+                slot_count, moments - moment, older_list, blocks, packed, newest, rights, earlier
             )
             rights = [rights]
         made = next_currents(
-            slot_count, newer, blocks, inverse, rights, shared, earlier if moment > 1 and moment + 1 == moments else None
+            newest_list, blocks, inverse, rights, shared, earlier if moment > 1 and moment + 1 == moments else None
         )
         if len(made) > 1:
             newest, packed = made

time: 69.2 us -> 68.5 us (0.990)
  Pallas kernels: 14.7 us -> 14 us
    ppermute x9, starting transfers between devices: 10.2 us -> 12.4 us  [swap(): return lax.ppermute(x, axis, [(i, i ^ bits) for i in range(n)])]
    ppermute x3, starting transfers between devices: 2.3 us -> 0.13 us  [front_summands(): terms.append(lax.ppermute(x, 'delay', list(goes.items())))]
    ppermute x4, waiting for transfers between devices: 1.89 us -> 0.94 us  [body(): before = [lax.ppermute(p, 'delay', ring) for p in parts]]
    pallas_call x3 -> x4, Pallas kernels: 3.78 us -> 3.3 us  [past_field(): pl.pallas_call(functools.partial(past_kernel, when), in_specs=[whole(SMEM...]
    unnamed x12 -> x20, local copies, waits for them, and re-layouts: 2.91 us -> 2.87 us
  transfers between devices with their start and end apart: 29 -> 29, of which waited for: 9 -> 9; matrix products, arithmetic and copies ran while one was open for 0% -> 0% of each run, Pallas kernels for 15% -> 14%
where the time goes in v4:
time: 68.5 us; the launch traced here: 68 us
  starting transfers between devices  33.1 us (48%)
  waiting for transfers between devices  16.4 us (24%)
  Pallas kernels  14 us (20%)
  local copies, waits for them, and re-layouts  2.87 us (4%)
  between operations  0.92 us (1%)
  other arithmetic  0.72 us (1%)
    ppermute x9, starting transfers between devices, front_over_src(): return [x] + [lax.ppermute(x, ('src', 'delay'), p) for p in pairs]  16.3 us
    ppermute x9, starting transfers between devices, swap(): return lax.ppermute(x, axis, [(i, i ^ bits) for i in range(n)])  12.4 us
    ppermute x9, waiting for transfers between devices, front_over_src(): return [x] + [lax.ppermute(x, ('src', 'delay'), p) for p in pairs]  7.4 us
    ppermute x9, waiting for transfers between devices, swap(): return lax.ppermute(x, axis, [(i, i ^ bits) for i in range(n)])  4.11 us
    ppermute x3, waiting for transfers between devices, from_front_at_once(): y = jnp.where(pair == c, lax.ppermute(x, 'delay', goes), y)  3.94 us
    pallas_call x3, Pallas kernels, next_currents(): pl.pallas_call(functools.partial(step_kernel, len(rights), len(given)), i...  3.63 us
    pallas_call x1, Pallas kernels, make_plan(): pl.pallas_call(functools.partial(plan_kernel, groups, group_blocks, steps...  3.59 us
    pallas_call x4, Pallas kernels, past_field(): pl.pallas_call(functools.partial(past_kernel, when), in_specs=[whole(SMEM...  3.3 us
  transfers between devices with their start and end apart: 29, of which 9 were waited for; matrix products, arithmetic and copies ran while one was open for 0% of the time, Pallas kernels for 14%

profile of v4, /device:TPU:0, one launch (start us, length us, event | category | flops | bytes accessed | tf_op | source)
XLA Modules:
  0.0 68.0 jit_solution(1276103338395843362)
XLA Ops:
  0.0 3.0 %collective-permute-start = (f32[4,4,16,128]{3,2,1,0:T(8,128)}, f32[4,4,16,128]{3,2,1,0:T(8,128)S(1)}, u32[]{:S(2)}, u32[]{:S(2)}) collective-permute-start(f32[4,4,16,128]{3,2,1,0:T(8,128)} %refs_1_.1), channel_id=1, source_target_pairs={{0,8},{8,0},{16,24},{24,16},{1,9},{9,1},{17,25},{25,17},{2,10},{10... | collective-permute-start | bytes 393224 | tf_op jit(solution)/shard_map/ppermute | solution.py:24
  3.0 2.6 %collective-permute-start.2 = (f32[4,4,16,128]{3,2,1,0:T(8,128)}, f32[4,4,16,128]{3,2,1,0:T(8,128)S(1)}, u32[]{:S(2)}, u32[]{:S(2)}) collective-permute-start(f32[4,4,16,128]{3,2,1,0:T(8,128)} %refs_1_.1), channel_id=1, source_target_pairs={{0,16},{8,24},{16,0},{24,8},{1,17},{9,25},{17,1},{25,9},{2,18},{10... | collective-permute-start | bytes 393224 | tf_op jit(solution)/shard_map/ppermute | solution.py:24
  5.6 1.8 %collective-permute-start.1 = (s32[4]{0:T(128)}, s32[4]{0:T(128)S(1)}, u32[]{:S(2)}, u32[]{:S(2)}) collective-permute-start(s32[4]{0:T(128)} %slots.1), channel_id=1, source_target_pairs={{0,1},{1,2},{2,3},{3,4},{4,5},{5,6},{6,7},{7,0},{8,9},{9,10},{10,1... | collective-permute-start | bytes 56 | tf_op jit(solution)/shard_map/ppermute | solution.py:442
  8.1 3.6 %make_plan.1 = (s32[385]{0:T(512)}, s32[385]{0:T(512)}, s32[321]{0:T(512)}, s32[321]{0:T(512)}, s32[193]{0:T(256)}, /*index=5*/s32[579]{0:T(1024)}) custom-call(s32[1]{0:T(128)} %bitcast.me, s32[1]{0:T(128)} %bitcast.1.band, s32[3,48]{1,0:T(4,128)} %pattern.1, s32[1]{0:T(128)S(6)} %copy.8.live, s32[4]{0:T(128)} %slots.1), custom_call_target="tpu_custom_call" | custom-call | tf_op jit(solution)/shard_map/make_plan/pallas_call | solution.py:138
  11.7 1.9 %copy-done = f32[48,128,128]{2,1,0:T(8,128)S(1)} copy-done((f32[48,128,128]{2,1,0:T(8,128)S(1)}, f32[48,128,128]{2,1,0:T(8,128)}, u32[]{:S(2)}) %copy-start) | copy-done | bytes 3145752
  13.6 0.9 %copy-done.2 = f32[4,128,128]{2,1,0:T(8,128)S(1)} copy-done((f32[4,128,128]{2,1,0:T(8,128)S(1)}, f32[4,128,128]{2,1,0:T(8,128)}, u32[]{:S(2)}) %copy-start.2) | copy-done | bytes 262168
  14.5 0.7 %split_blocks.1 = (bf16[48,128,256]{2,1,0:T(8,128)(2,1)S(1)}, bf16[4,128,256]{2,1,0:T(8,128)(2,1)S(1)}) custom-call(f32[48,128,128]{2,1,0:T(8,128)S(1)} %copy-done, f32[4,128,128]{2,1,0:T(8,128)S(1)} %copy-done.2), custom_call_target="tpu_custom_call" | custom-call | flops 6291456 | bytes 6291456 | tf_op jit(solution)/shard_map/split_blocks/pallas_call | solution.py:173
  15.3 0.9 %collective-permute-start.9 = (f32[4,4,16,128]{3,2,1,0:T(8,128)S(1)}, f32[4,4,16,128]{3,2,1,0:T(8,128)S(1)}, u32[]{:S(2)}, u32[]{:S(2)}) collective-permute-start(f32[4,4,16,128]{3,2,1,0:T(8,128)S(1)} %collective-permute-done.refs_2_), channel_id=1, source_target_pairs={{0,1},{1,2},{2,3},{3,4},{4,5},{5,6},{6,7},{7,0},{8,9},{9,10},{10,1... | collective-permute-start | bytes 393224 | tf_op jit(solution)/shard_map/ppermute | solution.py:451
  16.2 1.1 %near_field.1.refs_1_ = f32[4,4,16,128]{3,2,1,0:T(8,128)S(1)} custom-call(s32[385]{0:T(512)S(1)} %copy-done.9, bf16[48,128,256]{2,1,0:T(8,128)(2,1)S(1)} %get-tuple-element.48.refs_0_.refs_1_.blocks, f32[4,4,16,128]{3,2,1,0:T(8,128)S(1)} %copy-done.3, f32[4,4,16,128]{3,2,1,0:T(8,128)S(1)} %collective-permute-done.refs_2_), custom_call_target="tpu_custom_call" | custom-call | flops 1 | bytes 1 | tf_op jit(solution)/shard_map/near_field/pallas_call | solution.py:245
  17.3 1.0 %collective-permute-start.10 = (f32[4,4,16,128]{3,2,1,0:T(8,128)S(1)}, f32[4,4,16,128]{3,2,1,0:T(8,128)S(1)}, u32[]{:S(2)}, u32[]{:S(2)}) collective-permute-start(f32[4,4,16,128]{3,2,1,0:T(8,128)S(1)} %collective-permute-done.2.refs_2_), channel_id=1, source_target_pairs={{0,1},{1,2},{2,3},{3,4},{4,5},{5,6},{6,7},{7,0},{8,9},{9,10},{10,1... | collective-permute-start | bytes 393224 | tf_op jit(solution)/shard_map/ppermute | solution.py:451
  18.4 0.3 collective-permute-start.11
  18.7 1.1 %far_field.1 = (f32[4,4,16,128]{3,2,1,0:T(8,128)S(1)}, f32[4,16,128]{2,1,0:T(8,128)S(1)}) custom-call(s32[385]{0:T(512)S(1)} %copy-done.8, bf16[48,128,256]{2,1,0:T(8,128)(2,1)S(1)} %get-tuple-element.48.refs_0_.refs_1_.blocks, f32[4,4,16,128]{3,2,1,0:T(8,128)S(1)} %near_field.1.refs_1_, f32[4,4,16,128]{3,2,1,0:T(8,128)S(1)} %collective-permute-done.2.refs_2_, ...), custom_call_target="tpu_custom_call" | custom-call | flops 1 | bytes 1 | tf_op jit(solution)/shard_map/far_field/pallas_call | solution.py:245
  19.8 1.8 %collective-permute-start.4 = (f32[4,16,128]{2,1,0:T(8,128)S(1)}, f32[4,16,128]{2,1,0:T(8,128)S(1)}, u32[]{:S(2)}, u32[]{:S(2)}) collective-permute-start(f32[4,16,128]{2,1,0:T(8,128)S(1)} %get-tuple-element.54), channel_id=1, source_target_pairs={{0,1},{1,0},{2,3},{3,2},{4,5},{5,4},{6,7},{7,6},{8,9},{9,8},{10,11... | collective-permute-start | bytes 98312 | tf_op jit(solution)/shard_map/ppermute | solution.py:24
  21.6 0.9 %collective-permute-done.4 = f32[4,16,128]{2,1,0:T(8,128)S(1)} collective-permute-done((f32[4,16,128]{2,1,0:T(8,128)S(1)}, f32[4,16,128]{2,1,0:T(8,128)S(1)}, u32[]{:S(2)}, u32[]{:S(2)}) %collective-permute-start.4) | collective-permute-done | bytes 32800 | tf_op jit(solution)/shard_map/ppermute | solution.py:24
  22.5 0.6 late_field.1.refs_2_
  23.1 0.9 %collective-permute-done.11.refs_4_ = f32[4,4,16,128]{3,2,1,0:T(8,128)S(1)} collective-permute-done((f32[4,4,16,128]{3,2,1,0:T(8,128)S(1)}, f32[4,4,16,128]{3,2,1,0:T(8,128)S(1)}, u32[]{:S(2)}, u32[]{:S(2)}) %collective-permute-start.11) | collective-permute-done | bytes 131104 | tf_op jit(solution)/shard_map/ppermute | solution.py:451
  24.1 0.6 later_field.1
  24.7 1.4 %collective-permute-start.12 = (f32[3,4,16,128]{3,2,1,0:T(8,128)S(1)}, f32[3,4,16,128]{3,2,1,0:T(8,128)S(1)}, u32[]{:S(2)}, u32[]{:S(2)}) collective-permute-start(f32[3,4,16,128]{3,2,1,0:T(8,128)S(1)} %later_field.1), channel_id=1, source_target_pairs={{0,1},{1,0},{2,3},{3,2},{4,5},{5,4},{6,7},{7,6},{8,9},{9,8},{10,11... | collective-permute-start | bytes 294920 | tf_op jit(solution)/shard_map/ppermute | solution.py:24
  26.1 0.2 collective-permute-start.5
  26.3 1.5 %collective-permute-start.6 = (f32[4,16,128]{2,1,0:T(8,128)S(1)}, f32[4,16,128]{2,1,0:T(8,128)S(1)}, u32[]{:S(2)}, u32[]{:S(2)}) collective-permute-start(f32[4,16,128]{2,1,0:T(8,128)S(1)} %add.7.refs_0_), channel_id=1, source_target_pairs={{0,4},{1,5},{2,6},{3,7},{4,0},{5,1},{6,2},{7,3},{8,12},{9,13},{10,... | collective-permute-start | bytes 98312 | tf_op jit(solution)/shard_map/ppermute | solution.py:24
  27.8 1.8 %collective-permute-start.7 = (f32[4,16,128]{2,1,0:T(8,128)S(1)}, f32[4,16,128]{2,1,0:T(8,128)S(1)}, u32[]{:S(2)}, u32[]{:S(2)}) collective-permute-start(f32[4,16,128]{2,1,0:T(8,128)S(1)} %add.7.refs_0_), channel_id=1, source_target_pairs={{0,2},{1,3},{2,0},{3,1},{4,6},{5,7},{6,4},{7,5},{8,10},{9,11},{10,... | collective-permute-start | bytes 98312 | tf_op jit(solution)/shard_map/ppermute | solution.py:24
  29.6 0.1 collective-permute-start.13
  29.7 0.1 collective-permute-start.14
  29.7 1.5 %collective-permute-done.5.refs_1_ = f32[4,16,128]{2,1,0:T(8,128)S(1)} collective-permute-done((f32[4,16,128]{2,1,0:T(8,128)S(1)}, f32[4,16,128]{2,1,0:T(8,128)S(1)}, u32[]{:S(2)}, u32[]{:S(2)}) %collective-permute-start.5) | collective-permute-done | bytes 32800 | tf_op jit(solution)/shard_map/ppermute | solution.py:24
  31.2 0.5 collective-permute-done.7.refs_3_
  31.7 0.2 first_currents.1.refs_5_
  31.9 0.6 collective-permute-start.16
  32.5 3.5 %collective-permute-start.17 = (f32[4,16,128]{2,1,0:T(8,128)S(1)}, f32[4,16,128]{2,1,0:T(8,128)S(1)}, u32[]{:S(2)}, u32[]{:S(2)}) collective-permute-start(f32[4,16,128]{2,1,0:T(8,128)S(1)} %first_currents.1.refs_5_), channel_id=1, source_target_pairs={{0,16},{1,2},{2,3},{3,4},{4,5},{5,6},{6,7},{7,1},{8,24},{9,10},{10... | collective-permute-start | bytes 98312 | tf_op jit(solution)/shard_map/ppermute | solution.py:438
  36.0 3.3 %collective-permute-start.18 = (f32[4,16,128]{2,1,0:T(8,128)S(1)}, f32[4,16,128]{2,1,0:T(8,128)S(1)}, u32[]{:S(2)}, u32[]{:S(2)}) collective-permute-start(f32[4,16,128]{2,1,0:T(8,128)S(1)} %first_currents.1.refs_5_), channel_id=1, source_target_pairs={{0,24},{1,2},{2,3},{3,4},{4,5},{5,6},{6,7},{7,1},{8,16},{9,10},{10... | collective-permute-start | bytes 98312 | tf_op jit(solution)/shard_map/ppermute | solution.py:438
  39.3 2.4 %collective-permute-done.18.refs_8_ = f32[4,16,128]{2,1,0:T(8,128)S(1)} collective-permute-done((f32[4,16,128]{2,1,0:T(8,128)S(1)}, f32[4,16,128]{2,1,0:T(8,128)S(1)}, u32[]{:S(2)}, u32[]{:S(2)}) %collective-permute-start.18) | collective-permute-done | bytes 32800 | tf_op jit(solution)/shard_map/ppermute | solution.py:438
  41.7 1.2 %next_currents.3 = (f32[4,16,128]{2,1,0:T(8,128)S(1)}, bf16[17,32,128]{2,1,0:T(8,128)(2,1)S(1)}) custom-call(s32[193]{0:T(256)S(1)} %copy-done.5, bf16[48,128,256]{2,1,0:T(8,128)(2,1)S(1)} %get-tuple-element.48.refs_0_.refs_1_.blocks, bf16[4,128,256]{2,1,0:T(8,128)(2,1)S(1)} %get-tuple-element.46.inverse, f32[4,4,16,128]{3,2,1,0:T(8,128)S(1)} %copy-done.1, ...), custom_call_target="tpu_custom_call" | custom-call | flops 1 | bytes 1 | tf_op jit(solution)/shard_map/next_currents/pallas_call | solution.py:326
  42.9 3.9 %collective-permute-start.20 = (f32[4,16,128]{2,1,0:T(8,128)S(1)}, f32[4,16,128]{2,1,0:T(8,128)S(1)}, u32[]{:S(2)}, u32[]{:S(2)}) collective-permute-start(f32[4,16,128]{2,1,0:T(8,128)S(1)} %get-tuple-element.64.newest.refs_1_), channel_id=1, source_target_pairs={{0,16},{1,2},{2,3},{3,4},{4,5},{5,6},{6,7},{7,1},{8,24},{9,10},{10... | collective-permute-start | bytes 98312 | tf_op jit(solution)/shard_map/ppermute | solution.py:438
  46.9 0.5 collective-permute-start.21
  47.4 1.5 %older_field.2 = (f32[2,4,16,128]{3,2,1,0:T(8,128)S(1)}, f32[1,4,16,128]{3,2,1,0:T(8,128)S(1)}) custom-call(s32[579]{0:T(1024)S(1)} %copy-done.4, bf16[48,128,256]{2,1,0:T(8,128)(2,1)S(1)} %get-tuple-element.48.refs_0_.refs_1_.blocks, bf16[17,32,128]{2,1,0:T(8,128)(2,1)S(1)} %get-tuple-element.63.packed, f32[4,16,128]{2,1,0:T(8,128)S(1)} %get-tuple-element.64.newest.refs_1_, ...), custom_call_target="tpu_custom_call" | custom-call | flops 1 | bytes 1 | tf_op jit(solution)/shard_map/older_field/pallas_call | solution.py:356
  48.9 3.7 %collective-permute-done.21.refs_4_ = f32[4,16,128]{2,1,0:T(8,128)S(1)} collective-permute-done((f32[4,16,128]{2,1,0:T(8,128)S(1)}, f32[4,16,128]{2,1,0:T(8,128)S(1)}, u32[]{:S(2)}, u32[]{:S(2)}) %collective-permute-start.21) | collective-permute-done | bytes 32800 | tf_op jit(solution)/shard_map/ppermute | solution.py:438
  52.6 1.2 %next_currents.4 = (f32[4,16,128]{2,1,0:T(8,128)S(1)}, bf16[17,32,128]{2,1,0:T(8,128)(2,1)S(1)}) custom-call(s32[193]{0:T(256)S(1)} %copy-done.5, bf16[48,128,256]{2,1,0:T(8,128)(2,1)S(1)} %get-tuple-element.48.refs_0_.refs_1_.blocks, bf16[4,128,256]{2,1,0:T(8,128)(2,1)S(1)} %get-tuple-element.46.inverse, f32[2,4,16,128]{3,2,1,0:T(8,128)S(1)} %get-tuple-element.65.refs_0_, ...), custom_call_target="tpu_custom_call" | custom-call | flops 1 | bytes 1 | tf_op jit(solution)/shard_map/next_currents/pallas_call | solution.py:326
  53.8 1.1 %collective-permute-start.23 = (f32[4,16,128]{2,1,0:T(8,128)S(1)}, f32[4,16,128]{2,1,0:T(8,128)S(1)}, u32[]{:S(2)}, u32[]{:S(2)}) collective-permute-start(f32[4,16,128]{2,1,0:T(8,128)S(1)} %get-tuple-element.67.newest.refs_2_), channel_id=1, source_target_pairs={{0,16},{1,2},{2,3},{3,4},{4,5},{5,6},{6,7},{7,1},{8,24},{9,10},{10... | collective-permute-start | bytes 98312 | tf_op jit(solution)/shard_map/ppermute | solution.py:438
  54.9 3.3 %collective-permute-start.24 = (f32[4,16,128]{2,1,0:T(8,128)S(1)}, f32[4,16,128]{2,1,0:T(8,128)S(1)}, u32[]{:S(2)}, u32[]{:S(2)}) collective-permute-start(f32[4,16,128]{2,1,0:T(8,128)S(1)} %get-tuple-element.67.newest.refs_2_), channel_id=1, source_target_pairs={{0,24},{1,2},{2,3},{3,4},{4,5},{5,6},{6,7},{7,1},{8,16},{9,10},{10... | collective-permute-start | bytes 98312 | tf_op jit(solution)/shard_map/ppermute | solution.py:438
  58.2 1.0 %older_field.3 = (f32[1,4,16,128]{3,2,1,0:T(8,128)S(1)}, f32[2,4,16,128]{3,2,1,0:T(8,128)S(1)}) custom-call(s32[579]{0:T(1024)S(1)} %copy-done.4, bf16[48,128,256]{2,1,0:T(8,128)(2,1)S(1)} %get-tuple-element.48.refs_0_.refs_1_.blocks, bf16[17,32,128]{2,1,0:T(8,128)(2,1)S(1)} %get-tuple-element.66.packed, f32[4,16,128]{2,1,0:T(8,128)S(1)} %get-tuple-element.67.newest.refs_2_, ...), custom_call_target="tpu_custom_call" | custom-call | flops 1 | bytes 1 | tf_op jit(solution)/shard_map/older_field/pallas_call | solution.py:356
  59.3 1.3 %collective-permute-done.24.refs_5_ = f32[4,16,128]{2,1,0:T(8,128)S(1)} collective-permute-done((f32[4,16,128]{2,1,0:T(8,128)S(1)}, f32[4,16,128]{2,1,0:T(8,128)S(1)}, u32[]{:S(2)}, u32[]{:S(2)}) %collective-permute-start.24) | collective-permute-done | bytes 32800 | tf_op jit(solution)/shard_map/ppermute | solution.py:438
  60.6 1.2 %next_currents.5 = f32[3,4,16,128]{3,2,1,0:T(8,128)S(1)} custom-call(s32[193]{0:T(256)S(1)} %copy-done.5, bf16[48,128,256]{2,1,0:T(8,128)(2,1)S(1)} %get-tuple-element.48.refs_0_.refs_1_.blocks, bf16[4,128,256]{2,1,0:T(8,128)(2,1)S(1)} %get-tuple-element.46.inverse, f32[1,4,16,128]{3,2,1,0:T(8,128)S(1)} %get-tuple-element.69.refs_0_, ...), custom_call_target="tpu_custom_call" | custom-call | flops 1 | bytes 1 | tf_op jit(solution)/shard_map/next_currents/pallas_call | solution.py:326
  61.8 0.0 collective-permute-start.26
  61.8 0.1 collective-permute-start.27
  61.9 3.9 %collective-permute-done.25 = f32[3,4,16,128]{3,2,1,0:T(8,128)S(1)} collective-permute-done((f32[3,4,16,128]{3,2,1,0:T(8,128)S(1)}, f32[3,4,16,128]{3,2,1,0:T(8,128)S(1)}, u32[]{:S(2)}, u32[]{:S(2)}) %collective-permute-start.25) | collective-permute-done | bytes 98336 | tf_op jit(solution)/shard_map/ppermute | solution.py:417
  65.9 0.0 collective-permute-done.26
  65.9 0.1 collective-permute-start.28
  66.0 1.3 %collective-permute-done.28 = f32[3,4,16,128]{3,2,1,0:T(8,128)S(1)} collective-permute-done((f32[3,4,16,128]{3,2,1,0:T(8,128)S(1)}, f32[3,4,16,128]{3,2,1,0:T(8,128)S(1)}, u32[]{:S(2)}, u32[]{:S(2)}) %collective-permute-start.28) | collective-permute-done | bytes 98336 | tf_op jit(solution)/shard_map/ppermute | solution.py:24
  67.3 0.7 pad_maximum_fusion
  (47 shorter events, 0.2 us)
Async XLA Ops:
  0.0 15.3 %collective-permute-start = (f32[4,4,16,128]{3,2,1,0:T(8,128)}, f32[4,4,16,128]{3,2,1,0:T(8,128)S(1)}, u32[]{:S(2)}, u32[]{:S(2)}) collective-permute-start(f32[4,4,16,128]{3,2,1,0:T(8,128)} %refs_1_.1), channel_id=1, source_target_pairs={{0,8},{8,0},{16,24},{24,16},{1,9},{9,1},{17,25},{25,17},{2,10},{10... | collective-permute-start | bytes 393224 | tf_op jit(solution)/shard_map/ppermute | solution.py:24
  3.0 14.3 %collective-permute-start.2 = (f32[4,4,16,128]{3,2,1,0:T(8,128)}, f32[4,4,16,128]{3,2,1,0:T(8,128)S(1)}, u32[]{:S(2)}, u32[]{:S(2)}) collective-permute-start(f32[4,4,16,128]{3,2,1,0:T(8,128)} %refs_1_.1), channel_id=1, source_target_pairs={{0,16},{8,24},{16,0},{24,8},{1,17},{9,25},{17,1},{25,9},{2,18},{10... | collective-permute-start | bytes 393224 | tf_op jit(solution)/shard_map/ppermute | solution.py:24
  5.6 11.7 %collective-permute-start.3 = (f32[4,4,16,128]{3,2,1,0:T(8,128)}, f32[4,4,16,128]{3,2,1,0:T(8,128)S(1)}, u32[]{:S(2)}, u32[]{:S(2)}) collective-permute-start(f32[4,4,16,128]{3,2,1,0:T(8,128)} %refs_1_.1), channel_id=1, source_target_pairs={{0,24},{8,16},{16,8},{24,0},{1,25},{9,17},{17,9},{25,1},{2,26},{10... | collective-permute-start | bytes 393224 | tf_op jit(solution)/shard_map/ppermute | solution.py:24
  5.6 16.9 %collective-permute-start.8 = (f32[4,4,16,128]{3,2,1,0:T(8,128)}, f32[4,4,16,128]{3,2,1,0:T(8,128)S(1)}, u32[]{:S(2)}, u32[]{:S(2)}) collective-permute-start(f32[4,4,16,128]{3,2,1,0:T(8,128)} %refs_1_.1), channel_id=1, source_target_pairs={{0,1},{1,2},{2,3},{3,4},{4,5},{5,6},{6,7},{7,0},{8,9},{9,10},{10,1... | collective-permute-start | bytes 393224 | tf_op jit(solution)/shard_map/ppermute | solution.py:451
  5.6 9.7 %collective-permute-start.1 = (s32[4]{0:T(128)}, s32[4]{0:T(128)S(1)}, u32[]{:S(2)}, u32[]{:S(2)}) collective-permute-start(s32[4]{0:T(128)} %slots.1), channel_id=1, source_target_pairs={{0,1},{1,2},{2,3},{3,4},{4,5},{5,6},{6,7},{7,0},{8,9},{9,10},{10,1... | collective-permute-start | bytes 56 | tf_op jit(solution)/shard_map/ppermute | solution.py:442
  11.7 1.9 %copy-start = (f32[48,128,128]{2,1,0:T(8,128)S(1)}, f32[48,128,128]{2,1,0:T(8,128)}, u32[]{:S(2)}) copy-start(f32[48,128,128]{2,1,0:T(8,128)} %blocks.1) | copy-start | bytes 9437188
  13.6 0.9 %copy-start.2 = (f32[4,128,128]{2,1,0:T(8,128)S(1)}, f32[4,128,128]{2,1,0:T(8,128)}, u32[]{:S(2)}) copy-start(f32[4,128,128]{2,1,0:T(8,128)} %inverse.1) | copy-start | bytes 786436
  14.5 1.7 %copy-start.3 = (f32[4,4,16,128]{3,2,1,0:T(8,128)S(1)}, f32[4,4,16,128]{3,2,1,0:T(8,128)}, u32[]{:S(2)}) copy-start(f32[4,4,16,128]{3,2,1,0:T(8,128)} %refs_1_.1) | copy-start | bytes 393220
  14.5 1.7 %copy-start.9 = (s32[385]{0:T(512)S(1)}, s32[385]{0:T(512)}, u32[]{:S(2)}) copy-start(s32[385]{0:T(512)} %get-tuple-element.49.plan) | copy-start | bytes 4624
  14.5 4.2 %copy-start.8 = (s32[385]{0:T(512)S(1)}, s32[385]{0:T(512)}, u32[]{:S(2)}) copy-start(s32[385]{0:T(512)} %get-tuple-element.47.plan) | copy-start | bytes 4624
  15.3 7.2 %copy-start.7 = (s32[321]{0:T(512)S(1)}, s32[321]{0:T(512)}, u32[]{:S(2)}) copy-start(s32[321]{0:T(512)} %get-tuple-element.61.plan) | copy-start | bytes 3856
  15.3 7.2 %collective-permute-start.9 = (f32[4,4,16,128]{3,2,1,0:T(8,128)S(1)}, f32[4,4,16,128]{3,2,1,0:T(8,128)S(1)}, u32[]{:S(2)}, u32[]{:S(2)}) collective-permute-start(f32[4,4,16,128]{3,2,1,0:T(8,128)S(1)} %collective-permute-done.refs_2_), channel_id=1, source_target_pairs={{0,1},{1,2},{2,3},{3,4},{4,5},{5,6},{6,7},{7,0},{8,9},{9,10},{10,1... | collective-permute-start | bytes 393224 | tf_op jit(solution)/shard_map/ppermute | solution.py:451
  17.3 6.8 %copy-start.6 = (s32[321]{0:T(512)S(1)}, s32[321]{0:T(512)}, u32[]{:S(2)}) copy-start(s32[321]{0:T(512)} %get-tuple-element.59.plan) | copy-start | bytes 3856
  17.3 5.8 %collective-permute-start.10 = (f32[4,4,16,128]{3,2,1,0:T(8,128)S(1)}, f32[4,4,16,128]{3,2,1,0:T(8,128)S(1)}, u32[]{:S(2)}, u32[]{:S(2)}) collective-permute-start(f32[4,4,16,128]{3,2,1,0:T(8,128)S(1)} %collective-permute-done.2.refs_2_), channel_id=1, source_target_pairs={{0,1},{1,2},{2,3},{3,4},{4,5},{5,6},{6,7},{7,0},{8,9},{9,10},{10,1... | collective-permute-start | bytes 393224 | tf_op jit(solution)/shard_map/ppermute | solution.py:451
  18.4 5.7 %collective-permute-start.11 = (f32[4,4,16,128]{3,2,1,0:T(8,128)S(1)}, f32[4,4,16,128]{3,2,1,0:T(8,128)S(1)}, u32[]{:S(2)}, u32[]{:S(2)}) collective-permute-start(f32[4,4,16,128]{3,2,1,0:T(8,128)S(1)} %collective-permute-done.3.refs_3_), channel_id=1, source_target_pairs={{0,1},{1,2},{2,3},{3,4},{4,5},{5,6},{6,7},{7,0},{8,9},{9,10},{10,1... | collective-permute-start | bytes 393224 | tf_op jit(solution)/shard_map/ppermute | solution.py:451
  19.8 2.7 %collective-permute-start.4 = (f32[4,16,128]{2,1,0:T(8,128)S(1)}, f32[4,16,128]{2,1,0:T(8,128)S(1)}, u32[]{:S(2)}, u32[]{:S(2)}) collective-permute-start(f32[4,16,128]{2,1,0:T(8,128)S(1)} %get-tuple-element.54), channel_id=1, source_target_pairs={{0,1},{1,0},{2,3},{3,2},{4,5},{5,4},{6,7},{7,6},{8,9},{9,8},{10,11... | collective-permute-start | bytes 98312 | tf_op jit(solution)/shard_map/ppermute | solution.py:24
  22.5 9.2 %copy-start.1 = (f32[4,4,16,128]{3,2,1,0:T(8,128)S(1)}, f32[4,4,16,128]{3,2,1,0:T(8,128)}, u32[]{:S(2)}) copy-start(f32[4,4,16,128]{3,2,1,0:T(8,128)} %refs_0_.3) | copy-start | bytes 393220
  22.5 19.2 %copy-start.5 = (s32[193]{0:T(256)S(1)}, s32[193]{0:T(256)}, u32[]{:S(2)}) copy-start(s32[193]{0:T(256)} %get-tuple-element.57.plan) | copy-start | bytes 2320
  24.7 22.7 %copy-start.4 = (s32[579]{0:T(1024)S(1)}, s32[579]{0:T(1024)}, u32[]{:S(2)}) copy-start(s32[579]{0:T(1024)} %get-tuple-element.58.plan) | copy-start | bytes 6952
  24.7 4.9 %collective-permute-start.12 = (f32[3,4,16,128]{3,2,1,0:T(8,128)S(1)}, f32[3,4,16,128]{3,2,1,0:T(8,128)S(1)}, u32[]{:S(2)}, u32[]{:S(2)}) collective-permute-start(f32[3,4,16,128]{3,2,1,0:T(8,128)S(1)} %later_field.1), channel_id=1, source_target_pairs={{0,1},{1,0},{2,3},{3,2},{4,5},{5,4},{6,7},{7,6},{8,9},{9,8},{10,11... | collective-permute-start | bytes 294920 | tf_op jit(solution)/shard_map/ppermute | solution.py:24
  26.1 5.1 %collective-permute-start.5 = (f32[4,16,128]{2,1,0:T(8,128)S(1)}, f32[4,16,128]{2,1,0:T(8,128)S(1)}, u32[]{:S(2)}, u32[]{:S(2)}) collective-permute-start(f32[4,16,128]{2,1,0:T(8,128)S(1)} %add.7.refs_0_), channel_id=1, source_target_pairs={{0,6},{1,7},{2,4},{3,5},{4,2},{5,3},{6,0},{7,1},{8,14},{9,15},{10,... | collective-permute-start | bytes 98312 | tf_op jit(solution)/shard_map/ppermute | solution.py:24
  26.3 5.0 %collective-permute-start.6 = (f32[4,16,128]{2,1,0:T(8,128)S(1)}, f32[4,16,128]{2,1,0:T(8,128)S(1)}, u32[]{:S(2)}, u32[]{:S(2)}) collective-permute-start(f32[4,16,128]{2,1,0:T(8,128)S(1)} %add.7.refs_0_), channel_id=1, source_target_pairs={{0,4},{1,5},{2,6},{3,7},{4,0},{5,1},{6,2},{7,3},{8,12},{9,13},{10,... | collective-permute-start | bytes 98312 | tf_op jit(solution)/shard_map/ppermute | solution.py:24
  27.8 3.9 %collective-permute-start.7 = (f32[4,16,128]{2,1,0:T(8,128)S(1)}, f32[4,16,128]{2,1,0:T(8,128)S(1)}, u32[]{:S(2)}, u32[]{:S(2)}) collective-permute-start(f32[4,16,128]{2,1,0:T(8,128)S(1)} %add.7.refs_0_), channel_id=1, source_target_pairs={{0,2},{1,3},{2,0},{3,1},{4,6},{5,7},{6,4},{7,5},{8,10},{9,11},{10,... | collective-permute-start | bytes 98312 | tf_op jit(solution)/shard_map/ppermute | solution.py:24
  29.6 12.1 %collective-permute-start.13 = (f32[3,4,16,128]{3,2,1,0:T(8,128)S(1)}, f32[3,4,16,128]{3,2,1,0:T(8,128)S(1)}, u32[]{:S(2)}, u32[]{:S(2)}) collective-permute-start(f32[3,4,16,128]{3,2,1,0:T(8,128)S(1)} %add.8.refs_1_), channel_id=1, source_target_pairs={{0,1},{1,7},{2,3},{3,2},{4,5},{5,4},{6,0},{7,6},{8,9},{9,15},{10,1... | collective-permute-start | bytes 294920 | tf_op jit(solution)/shard_map/ppermute | solution.py:381
  29.7 12.0 %collective-permute-start.14 = (f32[3,4,16,128]{3,2,1,0:T(8,128)S(1)}, f32[3,4,16,128]{3,2,1,0:T(8,128)S(1)}, u32[]{:S(2)}, u32[]{:S(2)}) collective-permute-start(f32[3,4,16,128]{3,2,1,0:T(8,128)S(1)} %add.8.refs_1_), channel_id=1, source_target_pairs={{0,1},{1,5},{2,3},{3,2},{4,0},{5,4},{6,7},{7,6},{8,9},{9,13},{10,1... | collective-permute-start | bytes 294920 | tf_op jit(solution)/shard_map/ppermute | solution.py:381
  31.2 10.5 %collective-permute-start.15 = (f32[3,4,16,128]{3,2,1,0:T(8,128)S(1)}, f32[3,4,16,128]{3,2,1,0:T(8,128)S(1)}, u32[]{:S(2)}, u32[]{:S(2)}) collective-permute-start(f32[3,4,16,128]{3,2,1,0:T(8,128)S(1)} %add.8.refs_1_), channel_id=1, source_target_pairs={{0,1},{1,3},{2,0},{3,2},{4,5},{5,4},{6,7},{7,6},{8,9},{9,11},{10,8... | collective-permute-start | bytes 294920 | tf_op jit(solution)/shard_map/ppermute | solution.py:381
  31.9 4.1 %collective-permute-start.16 = (f32[4,16,128]{2,1,0:T(8,128)S(1)}, f32[4,16,128]{2,1,0:T(8,128)S(1)}, u32[]{:S(2)}, u32[]{:S(2)}) collective-permute-start(f32[4,16,128]{2,1,0:T(8,128)S(1)} %first_currents.1.refs_5_), channel_id=1, source_target_pairs={{0,8},{1,2},{2,3},{3,4},{4,5},{5,6},{6,7},{7,1},{8,0},{9,10},{10,1... | collective-permute-start | bytes 98312 | tf_op jit(solution)/shard_map/ppermute | solution.py:438
  32.5 6.8 %collective-permute-start.17 = (f32[4,16,128]{2,1,0:T(8,128)S(1)}, f32[4,16,128]{2,1,0:T(8,128)S(1)}, u32[]{:S(2)}, u32[]{:S(2)}) collective-permute-start(f32[4,16,128]{2,1,0:T(8,128)S(1)} %first_currents.1.refs_5_), channel_id=1, source_target_pairs={{0,16},{1,2},{2,3},{3,4},{4,5},{5,6},{6,7},{7,1},{8,24},{9,10},{10... | collective-permute-start | bytes 98312 | tf_op jit(solution)/shard_map/ppermute | solution.py:438
  36.0 5.7 %collective-permute-start.18 = (f32[4,16,128]{2,1,0:T(8,128)S(1)}, f32[4,16,128]{2,1,0:T(8,128)S(1)}, u32[]{:S(2)}, u32[]{:S(2)}) collective-permute-start(f32[4,16,128]{2,1,0:T(8,128)S(1)} %first_currents.1.refs_5_), channel_id=1, source_target_pairs={{0,24},{1,2},{2,3},{3,4},{4,5},{5,6},{6,7},{7,1},{8,16},{9,10},{10... | collective-permute-start | bytes 98312 | tf_op jit(solution)/shard_map/ppermute | solution.py:438
  42.9 5.9 %collective-permute-start.19 = (f32[4,16,128]{2,1,0:T(8,128)S(1)}, f32[4,16,128]{2,1,0:T(8,128)S(1)}, u32[]{:S(2)}, u32[]{:S(2)}) collective-permute-start(f32[4,16,128]{2,1,0:T(8,128)S(1)} %get-tuple-element.64.newest.refs_1_), channel_id=1, source_target_pairs={{0,8},{1,2},{2,3},{3,4},{4,5},{5,6},{6,7},{7,1},{8,0},{9,10},{10,1... | collective-permute-start | bytes 98312 | tf_op jit(solution)/shard_map/ppermute | solution.py:438
  42.9 6.0 %collective-permute-start.20 = (f32[4,16,128]{2,1,0:T(8,128)S(1)}, f32[4,16,128]{2,1,0:T(8,128)S(1)}, u32[]{:S(2)}, u32[]{:S(2)}) collective-permute-start(f32[4,16,128]{2,1,0:T(8,128)S(1)} %get-tuple-element.64.newest.refs_1_), channel_id=1, source_target_pairs={{0,16},{1,2},{2,3},{3,4},{4,5},{5,6},{6,7},{7,1},{8,24},{9,10},{10... | collective-permute-start | bytes 98312 | tf_op jit(solution)/shard_map/ppermute | solution.py:438
  46.9 5.7 %collective-permute-start.21 = (f32[4,16,128]{2,1,0:T(8,128)S(1)}, f32[4,16,128]{2,1,0:T(8,128)S(1)}, u32[]{:S(2)}, u32[]{:S(2)}) collective-permute-start(f32[4,16,128]{2,1,0:T(8,128)S(1)} %get-tuple-element.64.newest.refs_1_), channel_id=1, source_target_pairs={{0,24},{1,2},{2,3},{3,4},{4,5},{5,6},{6,7},{7,1},{8,16},{9,10},{10... | collective-permute-start | bytes 98312 | tf_op jit(solution)/shard_map/ppermute | solution.py:438
  53.8 5.5 %collective-permute-start.22 = (f32[4,16,128]{2,1,0:T(8,128)S(1)}, f32[4,16,128]{2,1,0:T(8,128)S(1)}, u32[]{:S(2)}, u32[]{:S(2)}) collective-permute-start(f32[4,16,128]{2,1,0:T(8,128)S(1)} %get-tuple-element.67.newest.refs_2_), channel_id=1, source_target_pairs={{0,8},{1,2},{2,3},{3,4},{4,5},{5,6},{6,7},{7,1},{8,0},{9,10},{10,1... | collective-permute-start | bytes 98312 | tf_op jit(solution)/shard_map/ppermute | solution.py:438
  53.8 5.5 %collective-permute-start.23 = (f32[4,16,128]{2,1,0:T(8,128)S(1)}, f32[4,16,128]{2,1,0:T(8,128)S(1)}, u32[]{:S(2)}, u32[]{:S(2)}) collective-permute-start(f32[4,16,128]{2,1,0:T(8,128)S(1)} %get-tuple-element.67.newest.refs_2_), channel_id=1, source_target_pairs={{0,16},{1,2},{2,3},{3,4},{4,5},{5,6},{6,7},{7,1},{8,24},{9,10},{10... | collective-permute-start | bytes 98312 | tf_op jit(solution)/shard_map/ppermute | solution.py:438
  54.9 5.7 %collective-permute-start.24 = (f32[4,16,128]{2,1,0:T(8,128)S(1)}, f32[4,16,128]{2,1,0:T(8,128)S(1)}, u32[]{:S(2)}, u32[]{:S(2)}) collective-permute-start(f32[4,16,128]{2,1,0:T(8,128)S(1)} %get-tuple-element.67.newest.refs_2_), channel_id=1, source_target_pairs={{0,24},{1,2},{2,3},{3,4},{4,5},{5,6},{6,7},{7,1},{8,16},{9,10},{10... | collective-permute-start | bytes 98312 | tf_op jit(solution)/shard_map/ppermute | solution.py:438
  61.8 4.1 %collective-permute-start.25 = (f32[3,4,16,128]{3,2,1,0:T(8,128)S(1)}, f32[3,4,16,128]{3,2,1,0:T(8,128)S(1)}, u32[]{:S(2)}, u32[]{:S(2)}) collective-permute-start(f32[3,4,16,128]{3,2,1,0:T(8,128)S(1)} %next_currents.5), channel_id=1, source_target_pairs={{0,2},{2,3},{3,0},{1,5},{5,1},{4,6},{6,7},{7,4},{8,10},{10,11},{11... | collective-permute-start | bytes 294920 | tf_op jit(solution)/shard_map/ppermute | solution.py:417
  61.8 4.1 %collective-permute-start.26 = (f32[3,4,16,128]{3,2,1,0:T(8,128)S(1)}, f32[3,4,16,128]{3,2,1,0:T(8,128)S(1)}, u32[]{:S(2)}, u32[]{:S(2)}) collective-permute-start(f32[3,4,16,128]{3,2,1,0:T(8,128)S(1)} %next_currents.5), channel_id=1, source_target_pairs={{0,4},{4,5},{5,0},{1,7},{7,1},{2,3},{3,6},{6,2},{8,12},{12,13},{13... | collective-permute-start | bytes 294920 | tf_op jit(solution)/shard_map/ppermute | solution.py:417
  61.8 4.0 %collective-permute-start.27 = (f32[3,4,16,128]{3,2,1,0:T(8,128)S(1)}, f32[3,4,16,128]{3,2,1,0:T(8,128)S(1)}, u32[]{:S(2)}, u32[]{:S(2)}) collective-permute-start(f32[3,4,16,128]{3,2,1,0:T(8,128)S(1)} %next_currents.5), channel_id=1, source_target_pairs={{0,6},{6,7},{7,1},{1,0},{2,3},{3,2},{4,5},{5,4},{8,14},{14,15},{15... | collective-permute-start | bytes 294920 | tf_op jit(solution)/shard_map/ppermute | solution.py:417
  65.9 1.4 %collective-permute-start.28 = (f32[3,4,16,128]{3,2,1,0:T(8,128)S(1)}, f32[3,4,16,128]{3,2,1,0:T(8,128)S(1)}, u32[]{:S(2)}, u32[]{:S(2)}) collective-permute-start(f32[3,4,16,128]{3,2,1,0:T(8,128)S(1)} %select_select_fusion), channel_id=1, source_target_pairs={{0,1},{1,0},{2,3},{3,2},{4,5},{5,4},{6,7},{7,6},{8,9},{9,8},{10,11... | collective-permute-start | bytes 294920 | tf_op jit(solution)/shard_map/ppermute | solution.py:24
